TPU v7x, 32 devices: a whole 2x2x4 slice. The times are simulated.
32 devices in a mesh: groups: 2 (over y), segment: 4 (over x, core), space: 4 (over z).
Axes of the slice: x: 2, y: 2, z: 4, core: 2. Of those that a mesh axis runs over, the one named last changes fastest.
Arguments:
- inputs: bfloat16 [4, 32, 8, 256], P('groups', 'space'), parts along dimension 0, may hold values from -6 to 6
- cotangent: bfloat16 [4, 32, 256], P('groups', 'space'), parts along dimension 0, may hold values from -6 to 6
- lift_weight: bfloat16 [8, 64], replicated, may hold values from -2 to 2
- lift_bias: float32 [64], replicated, may hold values from -3 to 3
- point_weight: bfloat16 [4, 64, 64], P('segment'), may hold values from -0.75 to 0.75
- layer_bias: float32 [4, 64], P('segment'), may hold values from -2 to 2
- spectral_weight: bfloat16 [4, 16, 32, 2, 64, 64], P('segment', 'space'), may hold values from -0.5 to 0.5
- proj_weight: bfloat16 [64, 128], replicated, may hold values from -0.75 to 0.75
- proj_bias: float32 [128], replicated, may hold values from -3 to 3
- out_weight: bfloat16 [128], replicated, may hold values from -0.5 to 0.5
Outputs:
- spectral_grad: float32 [8, 16, 32, 2, 64, 64], P(('groups', 'segment'), 'space'), parts along dimension 0
- point_grad: float32 [8, 64, 64], P(('groups', 'segment')), parts along dimension 0
There are 2 independent parts, one for each index of `groups`. A program takes and returns all parts, laid end to end along the dimension named above; an argument that names none is the same for every part. Nothing has to cross between parts.
All inputs are finite; a program needn't handle non-finite values.
Results may differ from a plain program's by a relative error of at most 0.033.
Values may be sent and summed in bfloat16 or wider, within the bound.
No kernel may reach another device: no remote copies, remote signals or barrier semaphores. Data moves between devices by JAX's collectives and lax.ppermute only.
A program may use at most 64 MiB of HBM per device.

v0:
```python
from functools import partial
import math

import jax
import jax.numpy as jnp
from jax import lax
from jax.sharding import PartitionSpec as P

highest = lax.Precision.HIGHEST


def as_sent(array):
    return jax.tree.map(lambda a: a.astype(jnp.bfloat16) if a.dtype == jnp.float32 else a, array)


def passed_along(block, axis, distance):
    devices = range(lax.axis_size(axis))
    route = [(i - distance, i) for i in devices if i - distance in devices]
    return lax.ppermute(block, axis, route)


def y_tables(col_count, mode_count):
    ycells = jnp.arange(col_count, dtype=jnp.int32)[:, None]
    ymodes = jnp.arange(mode_count, dtype=jnp.int32)[None, :]
    angles = (ycells * ymodes % col_count).astype(jnp.float32) * (2.0 * math.pi / col_count)
    factor = 1.0 / math.sqrt(col_count)
    forward = jnp.stack([jnp.cos(angles), -jnp.sin(angles)], axis=1) * factor
    doubled = jnp.where(ymodes == 0, 1.0, 2.0).astype(jnp.float32)
    inverse = jnp.stack([doubled * jnp.cos(angles), -doubled * jnp.sin(angles)], axis=0) * factor
    return (forward.astype(jnp.bfloat16), jnp.transpose(inverse, (0, 2, 1)).astype(jnp.bfloat16))


def x_tables(row_total, mode_count):
    kx_count = 2 * mode_count
    indices = jnp.arange(kx_count, dtype=jnp.int32)
    freq_values = jnp.where(indices < mode_count, indices, indices - kx_count)
    xcells = jnp.arange(row_total, dtype=jnp.int32)
    angles = (freq_values[:, None] * xcells[None, :] % row_total).astype(jnp.float32) * (
        2.0 * math.pi / row_total
    )
    factor = 1.0 / math.sqrt(row_total)
    cosine_part = jnp.cos(angles) * factor
    sine_part = jnp.sin(angles) * factor
    forward = jnp.stack(
        [jnp.stack([cosine_part, sine_part], -1), jnp.stack([-sine_part, cosine_part], -1)], axis=1
    )
    cosine_flip = cosine_part.T
    sine_flip = sine_part.T
    inverse = jnp.stack(
        [jnp.stack([cosine_flip, -sine_flip], -1), jnp.stack([sine_flip, cosine_flip], -1)], axis=1
    )
    return (forward, inverse)


def mode_mult(coeffs, kernel):
    real_in, imag_in = (coeffs[:, :, 0], coeffs[:, :, 1])
    real_kernel, imag_kernel = (kernel[:, :, 0], kernel[:, :, 1])
    product = partial(jnp.einsum, "mjc,mjco->mjo", precision=highest)
    real_out = product(real_in, real_kernel) - product(imag_in, imag_kernel)
    imag_out = product(real_in, imag_kernel) + product(imag_in, real_kernel)
    return jnp.stack([real_out, imag_out], axis=2)


def mode_back(coeffs, mode_grads, kernel):
    real_in, imag_in = (coeffs[:, :, 0], coeffs[:, :, 1])
    real_grad, imag_grad = (mode_grads[:, :, 0], mode_grads[:, :, 1])
    real_kernel, imag_kernel = (kernel[:, :, 0], kernel[:, :, 1])
    outer_sum = partial(jnp.einsum, "mjc,mjo->mjco", precision=highest)
    inner_sum = partial(jnp.einsum, "mjo,mjco->mjc", precision=highest)
    kernel_real = outer_sum(real_in, real_grad) + outer_sum(imag_in, imag_grad)
    kernel_imag = outer_sum(real_in, imag_grad) - outer_sum(imag_in, real_grad)
    coeff_real = inner_sum(real_grad, real_kernel) + inner_sum(imag_grad, imag_kernel)
    coeff_imag = inner_sum(imag_grad, real_kernel) - inner_sum(real_grad, imag_kernel)
    return (
        jnp.stack([kernel_real, kernel_imag], axis=2),
        jnp.stack([coeff_real, coeff_imag], axis=2),
    )


def gelu_grad(pre_act, upstream):
    _, pullback = jax.vjp(jax.nn.gelu, pre_act)
    return pullback(upstream)[0]


def store_slot(buffer, value, slot_clip, is_valid):
    previous = lax.dynamic_index_in_dim(buffer, slot_clip, 0, keepdims=False)
    return lax.dynamic_update_index_in_dim(
        buffer, jnp.where(is_valid, value, previous), slot_clip, 0
    )


def on_device(
    inputs,
    cotangent,
    lift_weight,
    lift_bias,
    point_weight,
    layer_bias,
    spectral_weight,
    proj_weight,
    proj_bias,
    out_weight,
):
    batch_count, row_count, _, col_count = inputs.shape
    segment_count = lax.axis_size("segment")
    segment_index = lax.axis_index("segment")
    space_count = lax.axis_size("space")
    owned_modes = spectral_weight.shape[1]
    kx_count = spectral_weight.shape[2]
    channels = point_weight.shape[1]
    mode_count = kx_count // 2
    y_forward, y_inverse = y_tables(col_count, mode_count)
    x_forward, x_inverse = x_tables(row_count * space_count, mode_count)
    x_forward_adj = jnp.transpose(x_forward, (2, 3, 0, 1))
    x_inverse_adj = jnp.transpose(x_inverse, (2, 3, 0, 1))
    y_forward_wide = y_forward.astype(jnp.float32)
    y_inverse_wide = y_inverse.astype(jnp.float32)
    kernel = spectral_weight[0].astype(jnp.float32)
    point_matrix = point_weight[0]
    bias_vector = layer_bias[0]
    tick_count = batch_count + segment_count - 1

    def to_owners(y_coeffs, x_table):
        exchanged = lax.all_to_all(
            y_coeffs.astype(jnp.bfloat16), "space", split_axis=1, concat_axis=0, tiled=True
        ).astype(y_coeffs.dtype)
        return jnp.einsum("jqxp,xmpc->mjqc", x_table, exchanged, precision=highest)

    def from_owners(owned, x_table):
        spread = jnp.einsum("xpjq,mjqc->xmpc", x_table, owned, precision=highest)
        return lax.all_to_all(
            as_sent(spread), "space", split_axis=0, concat_axis=1, tiled=True
        ).astype(spread.dtype)

    def lifted(pick_slot):
        sample = lax.dynamic_index_in_dim(inputs, pick_slot, 0, keepdims=False)
        mixed = jnp.einsum("xty,tc->xcy", sample, lift_weight, preferred_element_type=jnp.float32)
        return (mixed + lift_bias[None, :, None]).astype(jnp.bfloat16)

    def forward_tick(state_now, tick_now):
        incoming, pre_store, act_store, mode_store = state_now
        pick_slot = jnp.clip(tick_now, 0, batch_count - 1)
        layer_in = lax.cond(segment_index == 0, lambda: lifted(pick_slot), lambda: incoming)
        y_coeffs = jnp.einsum(
            "xcy,ypm->xmpc", layer_in, y_forward, preferred_element_type=jnp.float32
        )
        coeffs = to_owners(y_coeffs, x_forward)
        back_rows = from_owners(mode_mult(coeffs, kernel), x_inverse)
        branch = jnp.einsum("xmpc,pmy->xcy", back_rows, y_inverse_wide, precision=highest)
        pointwise = jnp.einsum(
            "xcy,co->xoy", layer_in, point_matrix, preferred_element_type=jnp.float32
        )
        pre_act = pointwise + branch + bias_vector[None, :, None]
        slot_index = tick_now - segment_index
        is_valid = (slot_index >= 0) & (slot_index < batch_count)
        slot_clip = jnp.clip(slot_index, 0, batch_count - 1)
        pre_store = store_slot(pre_store, pre_act, slot_clip, is_valid)
        act_store = store_slot(act_store, layer_in, slot_clip, is_valid)
        mode_store = store_slot(mode_store, coeffs, slot_clip, is_valid)
        layer_out = jax.nn.gelu(pre_act).astype(jnp.bfloat16)
        sent = passed_along(layer_out, "segment", 1)
        return ((sent, pre_store, act_store, mode_store), None)

    start_state = (
        jnp.zeros((row_count, channels, col_count), jnp.bfloat16),
        jnp.zeros((batch_count, row_count, channels, col_count), jnp.float32),
        jnp.zeros((batch_count, row_count, channels, col_count), jnp.bfloat16),
        jnp.zeros((batch_count, owned_modes, kx_count, 2, channels), jnp.float32),
    )
    final_state, _ = lax.scan(forward_tick, start_state, jnp.arange(tick_count, dtype=jnp.int32))
    _, pre_store, act_store, mode_store = final_state

    def top_grad(slot_clip, pre_act):
        top_act = jax.nn.gelu(pre_act).astype(jnp.bfloat16)
        hidden = jnp.einsum("xcy,ck->xky", top_act, proj_weight, preferred_element_type=jnp.float32)
        hidden = hidden + proj_bias[None, :, None]
        target = lax.dynamic_index_in_dim(cotangent, slot_clip, 0, keepdims=False)
        upstream = (
            out_weight.astype(jnp.float32)[None, :, None] * target.astype(jnp.float32)[:, None, :]
        )
        hidden_grad = gelu_grad(hidden, upstream).astype(jnp.bfloat16)
        return jnp.einsum(
            "xky,ck->xcy", hidden_grad, proj_weight, preferred_element_type=jnp.float32
        ).astype(jnp.bfloat16)

    def backward_tick(state_now, tick_now):
        incoming, point_sum, kernel_sum = state_now
        slot_index = tick_now - (segment_count - 1 - segment_index)
        is_valid = (slot_index >= 0) & (slot_index < batch_count)
        slot_clip = jnp.clip(slot_index, 0, batch_count - 1)
        pre_act = lax.dynamic_index_in_dim(pre_store, slot_clip, 0, keepdims=False)
        layer_in = lax.dynamic_index_in_dim(act_store, slot_clip, 0, keepdims=False)
        coeffs = lax.dynamic_index_in_dim(mode_store, slot_clip, 0, keepdims=False)
        grad_out = lax.cond(
            segment_index == segment_count - 1,
            lambda: top_grad(slot_clip, pre_act),
            lambda: incoming,
        )
        pre_grad = gelu_grad(pre_act, grad_out.astype(jnp.float32)).astype(jnp.bfloat16)
        point_term = jnp.einsum(
            "xcy,xoy->co", layer_in, pre_grad, preferred_element_type=jnp.float32
        )
        y_grads = jnp.einsum(
            "xoy,pmy->xmpo", pre_grad, y_inverse, preferred_element_type=jnp.float32
        )
        mode_grads = to_owners(y_grads, x_inverse_adj)
        kernel_step, coeff_step = mode_back(coeffs, mode_grads, kernel)
        back_rows = from_owners(coeff_step, x_forward_adj)
        back_branch = jnp.einsum("xmpc,ypm->xcy", back_rows, y_forward_wide, precision=highest)
        pointwise_back = jnp.einsum(
            "co,xoy->xcy", point_matrix, pre_grad, preferred_element_type=jnp.float32
        )
        grad_in = (pointwise_back + back_branch).astype(jnp.bfloat16)
        point_sum = point_sum + jnp.where(is_valid, point_term, 0.0)
        kernel_sum = kernel_sum + jnp.where(is_valid, kernel_step, 0.0)
        sent = passed_along(grad_in, "segment", -1)
        return ((sent, point_sum, kernel_sum), None)

    back_start = (
        jnp.zeros((row_count, channels, col_count), jnp.bfloat16),
        jnp.zeros((channels, channels), jnp.float32),
        jnp.zeros((owned_modes, kx_count, 2, channels, channels), jnp.float32),
    )
    back_state, _ = lax.scan(backward_tick, back_start, jnp.arange(tick_count, dtype=jnp.int32))
    _, point_sum, kernel_sum = back_state
    point_total = lax.psum(point_sum, "space")
    factor = 1.0 / math.sqrt(batch_count * row_count * space_count * col_count)
    return (kernel_sum[None], (point_total * factor)[None])


def solution(mesh):
    in_specs = (
        P("groups", "space", None, None),
        P("groups", "space", None),
        P(),
        P(),
        P("segment", None, None),
        P("segment", None),
        P("segment", "space", None, None, None, None),
        P(),
        P(),
        P(),
    )
    out_specs = (
        P(("groups", "segment"), "space", None, None, None, None),
        P(("groups", "segment"), None, None),
    )
    return jax.shard_map(
        on_device, mesh=mesh, in_specs=in_specs, out_specs=out_specs, check_vma=False
    )
```

profile of v0, /device:TPU:3, one launch (start us, length us, event | category | flops | bytes accessed | tf_op | source)
XLA Modules:
  0.0 617.1 jit_solution(17774434167392830245)
XLA Ops:
  10.8 236.3 %while.40 = (s32[]{:T(128)}, bf16[8,64,256]{2,1,0:T(8,128)(2,1)S(1)}, f32[2,8,64,256]{3,2,1,0:T(8,128)S(1)}, bf16[2,8,64,256]{3,2,1,0:T(8,128)(2,1)S(1)}, f32[2,...) while((s32[]{:T(128)}, ...), condition=%wide.region_3.4_spmd, body=%wide.region_0.3_spmd.sunk | while | flops 129974280 | bytes 43396328 | solution.py:170
  95.3 8.6 %collective-permute-done = bf16[8,64,256]{2,1,0:T(8,128)(2,1)S(1)} collective-permute-done((bf16[8,64,256]{2,1,0:T(8,128)(2,1)S(1)}, bf16[8,64,256]{2,1,0:T(8,128)(2,1)S(1)}, u32[]{:S(2)}, u32[]{:S(2)}) %collective-permute-start) | collective-permute-done | bytes 262176 | tf_op jit(solution)/shard_map/while/body/eval_jaxpr/ppermute | solution.py:19
  143.0 8.6 %collective-permute-done = bf16[8,64,256]{2,1,0:T(8,128)(2,1)S(1)} collective-permute-done((bf16[8,64,256]{2,1,0:T(8,128)(2,1)S(1)}, bf16[8,64,256]{2,1,0:T(8,128)(2,1)S(1)}, u32[]{:S(2)}, u32[]{:S(2)}) %collective-permute-start) | collective-permute-done | bytes 262176 | tf_op jit(solution)/shard_map/while/body/eval_jaxpr/ppermute | solution.py:19
  190.8 8.6 %collective-permute-done = bf16[8,64,256]{2,1,0:T(8,128)(2,1)S(1)} collective-permute-done((bf16[8,64,256]{2,1,0:T(8,128)(2,1)S(1)}, bf16[8,64,256]{2,1,0:T(8,128)(2,1)S(1)}, u32[]{:S(2)}, u32[]{:S(2)}) %collective-permute-start) | collective-permute-done | bytes 262176 | tf_op jit(solution)/shard_map/while/body/eval_jaxpr/ppermute | solution.py:19
  238.5 8.6 %collective-permute-done = bf16[8,64,256]{2,1,0:T(8,128)(2,1)S(1)} collective-permute-done((bf16[8,64,256]{2,1,0:T(8,128)(2,1)S(1)}, bf16[8,64,256]{2,1,0:T(8,128)(2,1)S(1)}, u32[]{:S(2)}, u32[]{:S(2)}) %collective-permute-start) | collective-permute-done | bytes 262176 | tf_op jit(solution)/shard_map/while/body/eval_jaxpr/ppermute | solution.py:19
  247.1 353.4 %while.41 = (s32[]{:T(128)}, bf16[8,64,256]{2,1,0:T(8,128)(2,1)S(1)}, f32[64,64]{1,0:T(8,128)}, f32[4,32,2,64,64]{4,3,2,1,0:T(8,128)}, pred[]{:T(512)}, /*index=...) while((s32[]{:T(128)}, ...), condition=%wide.region_7.8_spmd.clone, body=%wide.region_4.7_spmd.clone.sunk | while | flops 227227776 | bytes 42694932 | solution.py:224
  262.9 8.3 %fusion.282 = f32[4,32,1,64]{3,2,1,0:T(1,128)S(1)} fusion(f32[4,32,64,1]{2,3,1,0:T(1,128)S(1)} %bitcast.491, f32[4,32,2,64,64]{4,3,2,1,0:T(8,128)} %get-tuple-element.1103), kind=kOutput, calls=%fused_computation.118.clone.1 | convolution fusion | flops 6291456 | bytes 4259840 | tf_op jit(solution)/shard_map/while/body/eval_jaxpr/mjo,mjco->mjc/dot_general | solution.py:72
  271.2 8.3 %fusion.281 = f32[4,32,1,64]{3,2,1,0:T(1,128)S(1)} fusion(f32[4,32,64,1]{2,3,1,0:T(1,128)S(1)} %bitcast.492, f32[4,32,2,64,64]{4,3,2,1,0:T(8,128)} %get-tuple-element.1103), kind=kOutput, calls=%fused_computation.112.clone.1 | convolution fusion | flops 6291456 | bytes 4259840 | tf_op jit(solution)/shard_map/while/body/eval_jaxpr/mjo,mjco->mjc/dot_general | solution.py:73
  279.6 8.3 %fusion.283 = f32[4,32,1,64]{3,2,1,0:T(1,128)S(1)} fusion(f32[4,32,64,1]{2,3,1,0:T(1,128)S(1)} %bitcast.487, f32[4,32,2,64,64]{4,3,2,1,0:T(8,128)} %get-tuple-element.1103), kind=kOutput, calls=%fused_computation.114.clone.1 | convolution fusion | flops 6291456 | bytes 4259840 | tf_op jit(solution)/shard_map/while/body/eval_jaxpr/mjo,mjco->mjc/dot_general | solution.py:72
  287.9 8.3 %fusion.280 = f32[4,32,1,64]{3,2,1,0:T(1,128)S(1)} fusion(f32[4,32,64,1]{2,3,1,0:T(1,128)S(1)} %bitcast.488, f32[4,32,2,64,64]{4,3,2,1,0:T(8,128)} %get-tuple-element.1103), kind=kOutput, calls=%fused_computation.116.clone.1 | convolution fusion | flops 6291456 | bytes 4259840 | tf_op jit(solution)/shard_map/while/body/eval_jaxpr/mjo,mjco->mjc/dot_general | solution.py:73
  311.5 7.2 %fusion.287 = f32[4,32,2,64,64]{4,3,2,1,0:T(8,128)} fusion(f32[4,32,1,64,64]{4,3,2,1,0:T(8,128)} %get-tuple-element.977, f32[4,32,1,64,64]{4,3,2,1,0:T(8,128)} %get-tuple-element.978, f32[4,32,2,64,64]{4,3,2,1,0:T(8,128)} %get-tuple-element.1068, pred[]{:T(512)S(6)} %compare.49, pred[]{:T(512)S(6)} %and.179), kind=kLoop, calls=%fused_computation.111.clone.1 | loop fusion | flops 4194304 | bytes 12582914 | tf_op jit(solution)/shard_map/while/body/eval_jaxpr/add | solution.py:215
  334.9 8.3 %fusion.282 = f32[4,32,1,64]{3,2,1,0:T(1,128)S(1)} fusion(f32[4,32,64,1]{2,3,1,0:T(1,128)S(1)} %bitcast.491, f32[4,32,2,64,64]{4,3,2,1,0:T(8,128)} %get-tuple-element.1103), kind=kOutput, calls=%fused_computation.118.clone.1 | convolution fusion | flops 6291456 | bytes 4259840 | tf_op jit(solution)/shard_map/while/body/eval_jaxpr/mjo,mjco->mjc/dot_general | solution.py:72
  343.2 8.3 %fusion.281 = f32[4,32,1,64]{3,2,1,0:T(1,128)S(1)} fusion(f32[4,32,64,1]{2,3,1,0:T(1,128)S(1)} %bitcast.492, f32[4,32,2,64,64]{4,3,2,1,0:T(8,128)} %get-tuple-element.1103), kind=kOutput, calls=%fused_computation.112.clone.1 | convolution fusion | flops 6291456 | bytes 4259840 | tf_op jit(solution)/shard_map/while/body/eval_jaxpr/mjo,mjco->mjc/dot_general | solution.py:73
  351.5 8.3 %fusion.283 = f32[4,32,1,64]{3,2,1,0:T(1,128)S(1)} fusion(f32[4,32,64,1]{2,3,1,0:T(1,128)S(1)} %bitcast.487, f32[4,32,2,64,64]{4,3,2,1,0:T(8,128)} %get-tuple-element.1103), kind=kOutput, calls=%fused_computation.114.clone.1 | convolution fusion | flops 6291456 | bytes 4259840 | tf_op jit(solution)/shard_map/while/body/eval_jaxpr/mjo,mjco->mjc/dot_general | solution.py:72
  359.8 8.3 %fusion.280 = f32[4,32,1,64]{3,2,1,0:T(1,128)S(1)} fusion(f32[4,32,64,1]{2,3,1,0:T(1,128)S(1)} %bitcast.488, f32[4,32,2,64,64]{4,3,2,1,0:T(8,128)} %get-tuple-element.1103), kind=kOutput, calls=%fused_computation.116.clone.1 | convolution fusion | flops 6291456 | bytes 4259840 | tf_op jit(solution)/shard_map/while/body/eval_jaxpr/mjo,mjco->mjc/dot_general | solution.py:73
  379.3 9.4 %fusion.287 = f32[4,32,2,64,64]{4,3,2,1,0:T(8,128)} fusion(f32[4,32,1,64,64]{4,3,2,1,0:T(8,128)} %get-tuple-element.977, f32[4,32,1,64,64]{4,3,2,1,0:T(8,128)} %get-tuple-element.978, f32[4,32,2,64,64]{4,3,2,1,0:T(8,128)} %get-tuple-element.1068, pred[]{:T(512)S(6)} %compare.49, pred[]{:T(512)S(6)} %and.179), kind=kLoop, calls=%fused_computation.111.clone.1 | loop fusion | flops 4194304 | bytes 12582914 | tf_op jit(solution)/shard_map/while/body/eval_jaxpr/add | solution.py:215
  405.5 8.3 %fusion.282 = f32[4,32,1,64]{3,2,1,0:T(1,128)S(1)} fusion(f32[4,32,64,1]{2,3,1,0:T(1,128)S(1)} %bitcast.491, f32[4,32,2,64,64]{4,3,2,1,0:T(8,128)} %get-tuple-element.1103), kind=kOutput, calls=%fused_computation.118.clone.1 | convolution fusion | flops 6291456 | bytes 4259840 | tf_op jit(solution)/shard_map/while/body/eval_jaxpr/mjo,mjco->mjc/dot_general | solution.py:72
  413.8 8.3 %fusion.281 = f32[4,32,1,64]{3,2,1,0:T(1,128)S(1)} fusion(f32[4,32,64,1]{2,3,1,0:T(1,128)S(1)} %bitcast.492, f32[4,32,2,64,64]{4,3,2,1,0:T(8,128)} %get-tuple-element.1103), kind=kOutput, calls=%fused_computation.112.clone.1 | convolution fusion | flops 6291456 | bytes 4259840 | tf_op jit(solution)/shard_map/while/body/eval_jaxpr/mjo,mjco->mjc/dot_general | solution.py:73
  422.1 8.3 %fusion.283 = f32[4,32,1,64]{3,2,1,0:T(1,128)S(1)} fusion(f32[4,32,64,1]{2,3,1,0:T(1,128)S(1)} %bitcast.487, f32[4,32,2,64,64]{4,3,2,1,0:T(8,128)} %get-tuple-element.1103), kind=kOutput, calls=%fused_computation.114.clone.1 | convolution fusion | flops 6291456 | bytes 4259840 | tf_op jit(solution)/shard_map/while/body/eval_jaxpr/mjo,mjco->mjc/dot_general | solution.py:72
  430.4 8.3 %fusion.280 = f32[4,32,1,64]{3,2,1,0:T(1,128)S(1)} fusion(f32[4,32,64,1]{2,3,1,0:T(1,128)S(1)} %bitcast.488, f32[4,32,2,64,64]{4,3,2,1,0:T(8,128)} %get-tuple-element.1103), kind=kOutput, calls=%fused_computation.116.clone.1 | convolution fusion | flops 6291456 | bytes 4259840 | tf_op jit(solution)/shard_map/while/body/eval_jaxpr/mjo,mjco->mjc/dot_general | solution.py:73
  449.9 9.4 %fusion.287 = f32[4,32,2,64,64]{4,3,2,1,0:T(8,128)} fusion(f32[4,32,1,64,64]{4,3,2,1,0:T(8,128)} %get-tuple-element.977, f32[4,32,1,64,64]{4,3,2,1,0:T(8,128)} %get-tuple-element.978, f32[4,32,2,64,64]{4,3,2,1,0:T(8,128)} %get-tuple-element.1068, pred[]{:T(512)S(6)} %compare.49, pred[]{:T(512)S(6)} %and.179), kind=kLoop, calls=%fused_computation.111.clone.1 | loop fusion | flops 4194304 | bytes 12582914 | tf_op jit(solution)/shard_map/while/body/eval_jaxpr/add | solution.py:215
  476.1 8.3 %fusion.282 = f32[4,32,1,64]{3,2,1,0:T(1,128)S(1)} fusion(f32[4,32,64,1]{2,3,1,0:T(1,128)S(1)} %bitcast.491, f32[4,32,2,64,64]{4,3,2,1,0:T(8,128)} %get-tuple-element.1103), kind=kOutput, calls=%fused_computation.118.clone.1 | convolution fusion | flops 6291456 | bytes 4259840 | tf_op jit(solution)/shard_map/while/body/eval_jaxpr/mjo,mjco->mjc/dot_general | solution.py:72
  484.4 8.3 %fusion.281 = f32[4,32,1,64]{3,2,1,0:T(1,128)S(1)} fusion(f32[4,32,64,1]{2,3,1,0:T(1,128)S(1)} %bitcast.492, f32[4,32,2,64,64]{4,3,2,1,0:T(8,128)} %get-tuple-element.1103), kind=kOutput, calls=%fused_computation.112.clone.1 | convolution fusion | flops 6291456 | bytes 4259840 | tf_op jit(solution)/shard_map/while/body/eval_jaxpr/mjo,mjco->mjc/dot_general | solution.py:73
  492.7 8.3 %fusion.283 = f32[4,32,1,64]{3,2,1,0:T(1,128)S(1)} fusion(f32[4,32,64,1]{2,3,1,0:T(1,128)S(1)} %bitcast.487, f32[4,32,2,64,64]{4,3,2,1,0:T(8,128)} %get-tuple-element.1103), kind=kOutput, calls=%fused_computation.114.clone.1 | convolution fusion | flops 6291456 | bytes 4259840 | tf_op jit(solution)/shard_map/while/body/eval_jaxpr/mjo,mjco->mjc/dot_general | solution.py:72
  501.1 8.3 %fusion.280 = f32[4,32,1,64]{3,2,1,0:T(1,128)S(1)} fusion(f32[4,32,64,1]{2,3,1,0:T(1,128)S(1)} %bitcast.488, f32[4,32,2,64,64]{4,3,2,1,0:T(8,128)} %get-tuple-element.1103), kind=kOutput, calls=%fused_computation.116.clone.1 | convolution fusion | flops 6291456 | bytes 4259840 | tf_op jit(solution)/shard_map/while/body/eval_jaxpr/mjo,mjco->mjc/dot_general | solution.py:73
  520.5 9.4 %fusion.287 = f32[4,32,2,64,64]{4,3,2,1,0:T(8,128)} fusion(f32[4,32,1,64,64]{4,3,2,1,0:T(8,128)} %get-tuple-element.977, f32[4,32,1,64,64]{4,3,2,1,0:T(8,128)} %get-tuple-element.978, f32[4,32,2,64,64]{4,3,2,1,0:T(8,128)} %get-tuple-element.1068, pred[]{:T(512)S(6)} %compare.49, pred[]{:T(512)S(6)} %and.179), kind=kLoop, calls=%fused_computation.111.clone.1 | loop fusion | flops 4194304 | bytes 12582914 | tf_op jit(solution)/shard_map/while/body/eval_jaxpr/add | solution.py:215
  546.7 8.3 %fusion.282 = f32[4,32,1,64]{3,2,1,0:T(1,128)S(1)} fusion(f32[4,32,64,1]{2,3,1,0:T(1,128)S(1)} %bitcast.491, f32[4,32,2,64,64]{4,3,2,1,0:T(8,128)} %get-tuple-element.1103), kind=kOutput, calls=%fused_computation.118.clone.1 | convolution fusion | flops 6291456 | bytes 4259840 | tf_op jit(solution)/shard_map/while/body/eval_jaxpr/mjo,mjco->mjc/dot_general | solution.py:72
  555.0 8.3 %fusion.281 = f32[4,32,1,64]{3,2,1,0:T(1,128)S(1)} fusion(f32[4,32,64,1]{2,3,1,0:T(1,128)S(1)} %bitcast.492, f32[4,32,2,64,64]{4,3,2,1,0:T(8,128)} %get-tuple-element.1103), kind=kOutput, calls=%fused_computation.112.clone.1 | convolution fusion | flops 6291456 | bytes 4259840 | tf_op jit(solution)/shard_map/while/body/eval_jaxpr/mjo,mjco->mjc/dot_general | solution.py:73
  563.3 8.3 %fusion.283 = f32[4,32,1,64]{3,2,1,0:T(1,128)S(1)} fusion(f32[4,32,64,1]{2,3,1,0:T(1,128)S(1)} %bitcast.487, f32[4,32,2,64,64]{4,3,2,1,0:T(8,128)} %get-tuple-element.1103), kind=kOutput, calls=%fused_computation.114.clone.1 | convolution fusion | flops 6291456 | bytes 4259840 | tf_op jit(solution)/shard_map/while/body/eval_jaxpr/mjo,mjco->mjc/dot_general | solution.py:72
  571.7 8.3 %fusion.280 = f32[4,32,1,64]{3,2,1,0:T(1,128)S(1)} fusion(f32[4,32,64,1]{2,3,1,0:T(1,128)S(1)} %bitcast.488, f32[4,32,2,64,64]{4,3,2,1,0:T(8,128)} %get-tuple-element.1103), kind=kOutput, calls=%fused_computation.116.clone.1 | convolution fusion | flops 6291456 | bytes 4259840 | tf_op jit(solution)/shard_map/while/body/eval_jaxpr/mjo,mjco->mjc/dot_general | solution.py:73
  591.1 9.4 %fusion.287 = f32[4,32,2,64,64]{4,3,2,1,0:T(8,128)} fusion(f32[4,32,1,64,64]{4,3,2,1,0:T(8,128)} %get-tuple-element.977, f32[4,32,1,64,64]{4,3,2,1,0:T(8,128)} %get-tuple-element.978, f32[4,32,2,64,64]{4,3,2,1,0:T(8,128)} %get-tuple-element.1068, pred[]{:T(512)S(6)} %compare.49, pred[]{:T(512)S(6)} %and.179), kind=kLoop, calls=%fused_computation.111.clone.1 | loop fusion | flops 4194304 | bytes 12582914 | tf_op jit(solution)/shard_map/while/body/eval_jaxpr/add | solution.py:215
  600.5 16.0 %psum.7 = f32[64,64]{1,0:T(8,128)S(1)} all-reduce(f32[64,64]{1,0:T(8,128)} %get-tuple-element.457), channel_id=1, replica_groups=mesh['groups'=2,'segment'=4,'space'=4] {'space'}, use_global_device_ids=true, to_apply=%region_8.9 | all-reduce | flops 4096 | bytes 32768 | tf_op jit(solution)/shard_map/psum | solution.py:226
  (363 shorter events, 363.3 us)
Async XLA Ops:
  10.8 236.3 %copy-start.2 = (bf16[1,64,64]{2,1,0:T(8,128)(2,1)S(1)}, bf16[1,64,64]{2,1,0:T(8,128)(2,1)}, u32[]{:S(2)}) copy-start(bf16[1,64,64]{2,1,0:T(8,128)(2,1)} %param.22) | copy-start | bytes 24580
  12.5 9.1 %all-to-all-start = ((bf16[4,2,2048]{2,1,0:T(2,128)(2,1)}), bf16[4,2,2048]{2,1,0:T(2,128)(2,1)S(1)}, u32[]{:S(2)}, u32[]{:S(2)}) async-start(bf16[4,2,2048]{2,1,0:T(2,128)(2,1)} %reshape.533), calls=%async_computation | async-start | bytes 65536 | tf_op jit(solution)/shard_map/while/body/eval_jaxpr/all_to_all | solution.py:124
  41.3 7.7 %all-to-all-start.1 = ((bf16[4,2,2048]{2,1,0:T(2,128)(2,1)}), bf16[4,2,2048]{2,1,0:T(2,128)(2,1)S(1)}, u32[]{:S(2)}, u32[]{:S(2)}) async-start(bf16[4,2,2048]{2,1,0:T(2,128)(2,1)} %reshape.535), calls=%async_computation.1 | async-start | bytes 65536 | tf_op jit(solution)/shard_map/while/body/eval_jaxpr/all_to_all | solution.py:131
  50.0 6.2 %collective-permute-start = (bf16[8,64,256]{2,1,0:T(8,128)(2,1)S(1)}, bf16[8,64,256]{2,1,0:T(8,128)(2,1)S(1)}, u32[]{:S(2)}, u32[]{:S(2)}) collective-permute-start(bf16[8,64,256]{2,1,0:T(8,128)(2,1)S(1)} %get-tuple-element.946), channel_id=1, source_target_pairs={{0,4},{4,8},{8,12},{1,5},{5,9},{9,13},{2,6},{6,10},{10,14},{3,7},{... | collective-permute-start | bytes 786440 | tf_op jit(solution)/shard_map/while/body/eval_jaxpr/ppermute | solution.py:19
  57.8 7.7 %all-to-all-start = ((bf16[4,2,2048]{2,1,0:T(2,128)(2,1)}), bf16[4,2,2048]{2,1,0:T(2,128)(2,1)S(1)}, u32[]{:S(2)}, u32[]{:S(2)}) async-start(bf16[4,2,2048]{2,1,0:T(2,128)(2,1)} %reshape.533), calls=%async_computation | async-start | bytes 65536 | tf_op jit(solution)/shard_map/while/body/eval_jaxpr/all_to_all | solution.py:124
  85.2 7.7 %all-to-all-start.1 = ((bf16[4,2,2048]{2,1,0:T(2,128)(2,1)}), bf16[4,2,2048]{2,1,0:T(2,128)(2,1)S(1)}, u32[]{:S(2)}, u32[]{:S(2)}) async-start(bf16[4,2,2048]{2,1,0:T(2,128)(2,1)} %reshape.535), calls=%async_computation.1 | async-start | bytes 65536 | tf_op jit(solution)/shard_map/while/body/eval_jaxpr/all_to_all | solution.py:131
  93.9 10.0 %collective-permute-start = (bf16[8,64,256]{2,1,0:T(8,128)(2,1)S(1)}, bf16[8,64,256]{2,1,0:T(8,128)(2,1)S(1)}, u32[]{:S(2)}, u32[]{:S(2)}) collective-permute-start(bf16[8,64,256]{2,1,0:T(8,128)(2,1)S(1)} %get-tuple-element.946), channel_id=1, source_target_pairs={{0,4},{4,8},{8,12},{1,5},{5,9},{9,13},{2,6},{6,10},{10,14},{3,7},{... | collective-permute-start | bytes 786440 | tf_op jit(solution)/shard_map/while/body/eval_jaxpr/ppermute | solution.py:19
  105.5 7.7 %all-to-all-start = ((bf16[4,2,2048]{2,1,0:T(2,128)(2,1)}), bf16[4,2,2048]{2,1,0:T(2,128)(2,1)S(1)}, u32[]{:S(2)}, u32[]{:S(2)}) async-start(bf16[4,2,2048]{2,1,0:T(2,128)(2,1)} %reshape.533), calls=%async_computation | async-start | bytes 65536 | tf_op jit(solution)/shard_map/while/body/eval_jaxpr/all_to_all | solution.py:124
  113.7 10.8 %copy-start = (f32[4,32,2,64,64]{4,3,2,1,0:T(8,128)S(1)}, f32[4,32,2,64,64]{4,3,2,1,0:T(8,128)}, u32[]{:S(2)}) copy-start(f32[4,32,2,64,64]{4,3,2,1,0:T(8,128)} %get-tuple-element.1034) | copy-start | bytes 12582916 | tf_op jit(solution)/shard_map/while
  133.0 7.7 %all-to-all-start.1 = ((bf16[4,2,2048]{2,1,0:T(2,128)(2,1)}), bf16[4,2,2048]{2,1,0:T(2,128)(2,1)S(1)}, u32[]{:S(2)}, u32[]{:S(2)}) async-start(bf16[4,2,2048]{2,1,0:T(2,128)(2,1)} %reshape.535), calls=%async_computation.1 | async-start | bytes 65536 | tf_op jit(solution)/shard_map/while/body/eval_jaxpr/all_to_all | solution.py:131
  141.6 10.0 %collective-permute-start = (bf16[8,64,256]{2,1,0:T(8,128)(2,1)S(1)}, bf16[8,64,256]{2,1,0:T(8,128)(2,1)S(1)}, u32[]{:S(2)}, u32[]{:S(2)}) collective-permute-start(bf16[8,64,256]{2,1,0:T(8,128)(2,1)S(1)} %get-tuple-element.946), channel_id=1, source_target_pairs={{0,4},{4,8},{8,12},{1,5},{5,9},{9,13},{2,6},{6,10},{10,14},{3,7},{... | collective-permute-start | bytes 786440 | tf_op jit(solution)/shard_map/while/body/eval_jaxpr/ppermute | solution.py:19
  153.2 7.7 %all-to-all-start = ((bf16[4,2,2048]{2,1,0:T(2,128)(2,1)}), bf16[4,2,2048]{2,1,0:T(2,128)(2,1)S(1)}, u32[]{:S(2)}, u32[]{:S(2)}) async-start(bf16[4,2,2048]{2,1,0:T(2,128)(2,1)} %reshape.533), calls=%async_computation | async-start | bytes 65536 | tf_op jit(solution)/shard_map/while/body/eval_jaxpr/all_to_all | solution.py:124
  180.7 7.7 %all-to-all-start.1 = ((bf16[4,2,2048]{2,1,0:T(2,128)(2,1)}), bf16[4,2,2048]{2,1,0:T(2,128)(2,1)S(1)}, u32[]{:S(2)}, u32[]{:S(2)}) async-start(bf16[4,2,2048]{2,1,0:T(2,128)(2,1)} %reshape.535), calls=%async_computation.1 | async-start | bytes 65536 | tf_op jit(solution)/shard_map/while/body/eval_jaxpr/all_to_all | solution.py:131
  189.4 10.0 %collective-permute-start = (bf16[8,64,256]{2,1,0:T(8,128)(2,1)S(1)}, bf16[8,64,256]{2,1,0:T(8,128)(2,1)S(1)}, u32[]{:S(2)}, u32[]{:S(2)}) collective-permute-start(bf16[8,64,256]{2,1,0:T(8,128)(2,1)S(1)} %get-tuple-element.946), channel_id=1, source_target_pairs={{0,4},{4,8},{8,12},{1,5},{5,9},{9,13},{2,6},{6,10},{10,14},{3,7},{... | collective-permute-start | bytes 786440 | tf_op jit(solution)/shard_map/while/body/eval_jaxpr/ppermute | solution.py:19
  201.0 7.7 %all-to-all-start = ((bf16[4,2,2048]{2,1,0:T(2,128)(2,1)}), bf16[4,2,2048]{2,1,0:T(2,128)(2,1)S(1)}, u32[]{:S(2)}, u32[]{:S(2)}) async-start(bf16[4,2,2048]{2,1,0:T(2,128)(2,1)} %reshape.533), calls=%async_computation | async-start | bytes 65536 | tf_op jit(solution)/shard_map/while/body/eval_jaxpr/all_to_all | solution.py:124
  228.4 7.7 %all-to-all-start.1 = ((bf16[4,2,2048]{2,1,0:T(2,128)(2,1)}), bf16[4,2,2048]{2,1,0:T(2,128)(2,1)S(1)}, u32[]{:S(2)}, u32[]{:S(2)}) async-start(bf16[4,2,2048]{2,1,0:T(2,128)(2,1)} %reshape.535), calls=%async_computation.1 | async-start | bytes 65536 | tf_op jit(solution)/shard_map/while/body/eval_jaxpr/all_to_all | solution.py:131
  237.1 10.0 %collective-permute-start = (bf16[8,64,256]{2,1,0:T(8,128)(2,1)S(1)}, bf16[8,64,256]{2,1,0:T(8,128)(2,1)S(1)}, u32[]{:S(2)}, u32[]{:S(2)}) collective-permute-start(bf16[8,64,256]{2,1,0:T(8,128)(2,1)S(1)} %get-tuple-element.946), channel_id=1, source_target_pairs={{0,4},{4,8},{8,12},{1,5},{5,9},{9,13},{2,6},{6,10},{10,14},{3,7},{... | collective-permute-start | bytes 786440 | tf_op jit(solution)/shard_map/while/body/eval_jaxpr/ppermute | solution.py:19
  254.8 7.7 %all-to-all-start.2 = ((bf16[4,2,2048]{2,1,0:T(2,128)(2,1)}), bf16[4,2,2048]{2,1,0:T(2,128)(2,1)S(1)}, u32[]{:S(2)}, u32[]{:S(2)}) async-start(bf16[4,2,2048]{2,1,0:T(2,128)(2,1)} %reshape.537), calls=%async_computation.2 | async-start | bytes 65536 | tf_op jit(solution)/shard_map/while/body/eval_jaxpr/all_to_all | solution.py:124
  297.3 7.9 %all-to-all-start.3 = ((bf16[4,2,2048]{2,1,0:T(2,128)(2,1)}), bf16[4,2,2048]{2,1,0:T(2,128)(2,1)S(1)}, u32[]{:S(2)}, u32[]{:S(2)}) async-start(bf16[4,2,2048]{2,1,0:T(2,128)(2,1)} %reshape.539), calls=%async_computation.3 | async-start | bytes 65536 | tf_op jit(solution)/shard_map/while/body/eval_jaxpr/all_to_all | solution.py:131
  306.0 12.8 %collective-permute-start.1 = (bf16[8,64,256]{2,1,0:T(8,128)(2,1)S(1)}, bf16[8,64,256]{2,1,0:T(8,128)(2,1)S(1)}, u32[]{:S(2)}, u32[]{:S(2)}) collective-permute-start(bf16[8,64,256]{2,1,0:T(8,128)(2,1)S(1)} %fusion.285), channel_id=1, source_target_pairs={{4,0},{8,4},{12,8},{5,1},{9,5},{13,9},{6,2},{10,6},{14,10},{7,3},{... | collective-permute-start | bytes 786440 | tf_op jit(solution)/shard_map/while/body/eval_jaxpr/ppermute | solution.py:19
  326.2 8.2 %all-to-all-start.2 = ((bf16[4,2,2048]{2,1,0:T(2,128)(2,1)}), bf16[4,2,2048]{2,1,0:T(2,128)(2,1)S(1)}, u32[]{:S(2)}, u32[]{:S(2)}) async-start(bf16[4,2,2048]{2,1,0:T(2,128)(2,1)} %reshape.537), calls=%async_computation.2 | async-start | bytes 65536 | tf_op jit(solution)/shard_map/while/body/eval_jaxpr/all_to_all | solution.py:124
  369.3 7.9 %all-to-all-start.3 = ((bf16[4,2,2048]{2,1,0:T(2,128)(2,1)}), bf16[4,2,2048]{2,1,0:T(2,128)(2,1)S(1)}, u32[]{:S(2)}, u32[]{:S(2)}) async-start(bf16[4,2,2048]{2,1,0:T(2,128)(2,1)} %reshape.539), calls=%async_computation.3 | async-start | bytes 65536 | tf_op jit(solution)/shard_map/while/body/eval_jaxpr/all_to_all | solution.py:131
  378.0 10.7 %collective-permute-start.1 = (bf16[8,64,256]{2,1,0:T(8,128)(2,1)S(1)}, bf16[8,64,256]{2,1,0:T(8,128)(2,1)S(1)}, u32[]{:S(2)}, u32[]{:S(2)}) collective-permute-start(bf16[8,64,256]{2,1,0:T(8,128)(2,1)S(1)} %fusion.285), channel_id=1, source_target_pairs={{4,0},{8,4},{12,8},{5,1},{9,5},{13,9},{6,2},{10,6},{14,10},{7,3},{... | collective-permute-start | bytes 786440 | tf_op jit(solution)/shard_map/while/body/eval_jaxpr/ppermute | solution.py:19
  396.1 9.0 %all-to-all-start.2 = ((bf16[4,2,2048]{2,1,0:T(2,128)(2,1)}), bf16[4,2,2048]{2,1,0:T(2,128)(2,1)S(1)}, u32[]{:S(2)}, u32[]{:S(2)}) async-start(bf16[4,2,2048]{2,1,0:T(2,128)(2,1)} %reshape.537), calls=%async_computation.2 | async-start | bytes 65536 | tf_op jit(solution)/shard_map/while/body/eval_jaxpr/all_to_all | solution.py:124
  439.9 7.9 %all-to-all-start.3 = ((bf16[4,2,2048]{2,1,0:T(2,128)(2,1)}), bf16[4,2,2048]{2,1,0:T(2,128)(2,1)S(1)}, u32[]{:S(2)}, u32[]{:S(2)}) async-start(bf16[4,2,2048]{2,1,0:T(2,128)(2,1)} %reshape.539), calls=%async_computation.3 | async-start | bytes 65536 | tf_op jit(solution)/shard_map/while/body/eval_jaxpr/all_to_all | solution.py:131
  448.6 10.7 %collective-permute-start.1 = (bf16[8,64,256]{2,1,0:T(8,128)(2,1)S(1)}, bf16[8,64,256]{2,1,0:T(8,128)(2,1)S(1)}, u32[]{:S(2)}, u32[]{:S(2)}) collective-permute-start(bf16[8,64,256]{2,1,0:T(8,128)(2,1)S(1)} %fusion.285), channel_id=1, source_target_pairs={{4,0},{8,4},{12,8},{5,1},{9,5},{13,9},{6,2},{10,6},{14,10},{7,3},{... | collective-permute-start | bytes 786440 | tf_op jit(solution)/shard_map/while/body/eval_jaxpr/ppermute | solution.py:19
  466.7 9.0 %all-to-all-start.2 = ((bf16[4,2,2048]{2,1,0:T(2,128)(2,1)}), bf16[4,2,2048]{2,1,0:T(2,128)(2,1)S(1)}, u32[]{:S(2)}, u32[]{:S(2)}) async-start(bf16[4,2,2048]{2,1,0:T(2,128)(2,1)} %reshape.537), calls=%async_computation.2 | async-start | bytes 65536 | tf_op jit(solution)/shard_map/while/body/eval_jaxpr/all_to_all | solution.py:124
  510.5 7.9 %all-to-all-start.3 = ((bf16[4,2,2048]{2,1,0:T(2,128)(2,1)}), bf16[4,2,2048]{2,1,0:T(2,128)(2,1)S(1)}, u32[]{:S(2)}, u32[]{:S(2)}) async-start(bf16[4,2,2048]{2,1,0:T(2,128)(2,1)} %reshape.539), calls=%async_computation.3 | async-start | bytes 65536 | tf_op jit(solution)/shard_map/while/body/eval_jaxpr/all_to_all | solution.py:131
  519.2 10.7 %collective-permute-start.1 = (bf16[8,64,256]{2,1,0:T(8,128)(2,1)S(1)}, bf16[8,64,256]{2,1,0:T(8,128)(2,1)S(1)}, u32[]{:S(2)}, u32[]{:S(2)}) collective-permute-start(bf16[8,64,256]{2,1,0:T(8,128)(2,1)S(1)} %fusion.285), channel_id=1, source_target_pairs={{4,0},{8,4},{12,8},{5,1},{9,5},{13,9},{6,2},{10,6},{14,10},{7,3},{... | collective-permute-start | bytes 786440 | tf_op jit(solution)/shard_map/while/body/eval_jaxpr/ppermute | solution.py:19
  537.3 9.0 %all-to-all-start.2 = ((bf16[4,2,2048]{2,1,0:T(2,128)(2,1)}), bf16[4,2,2048]{2,1,0:T(2,128)(2,1)S(1)}, u32[]{:S(2)}, u32[]{:S(2)}) async-start(bf16[4,2,2048]{2,1,0:T(2,128)(2,1)} %reshape.537), calls=%async_computation.2 | async-start | bytes 65536 | tf_op jit(solution)/shard_map/while/body/eval_jaxpr/all_to_all | solution.py:124
  581.1 7.9 %all-to-all-start.3 = ((bf16[4,2,2048]{2,1,0:T(2,128)(2,1)}), bf16[4,2,2048]{2,1,0:T(2,128)(2,1)S(1)}, u32[]{:S(2)}, u32[]{:S(2)}) async-start(bf16[4,2,2048]{2,1,0:T(2,128)(2,1)} %reshape.539), calls=%async_computation.3 | async-start | bytes 65536 | tf_op jit(solution)/shard_map/while/body/eval_jaxpr/all_to_all | solution.py:131
  589.8 10.7 %collective-permute-start.1 = (bf16[8,64,256]{2,1,0:T(8,128)(2,1)S(1)}, bf16[8,64,256]{2,1,0:T(8,128)(2,1)S(1)}, u32[]{:S(2)}, u32[]{:S(2)}) collective-permute-start(bf16[8,64,256]{2,1,0:T(8,128)(2,1)S(1)} %fusion.285), channel_id=1, source_target_pairs={{4,0},{8,4},{12,8},{5,1},{9,5},{13,9},{6,2},{10,6},{14,10},{7,3},{... | collective-permute-start | bytes 786440 | tf_op jit(solution)/shard_map/while/body/eval_jaxpr/ppermute | solution.py:19
  (13 other events, 94.5 us)
where the time goes:
time: 621 us; the launch traced here: 617 us
  matrix products  293 us (47%)
  waiting for transfers between devices  95 us (15%)
  starting transfers between devices  87.9 us (14%)
  other arithmetic  86.2 us (14%)
  local copies, waits for them, and re-layouts  30.1 us (5%)
  blocking collectives  16 us (3%)
  loops' own time  8.3 us (1%)
    dot_general x10, matrix products, mode_mult(): real_out = product(real_in, real_kernel) - product(imag_in, imag_kernel)  45.7 us
    dot_general x10, matrix products, mode_mult(): imag_out = product(real_in, imag_kernel) + product(imag_in, real_kernel)  44.9 us
    add x5, other arithmetic, backward_tick(): kernel_sum = kernel_sum + jnp.where(is_valid, kernel_step, 0.0)  44.7 us
    dot_general x5, matrix products, mode_back(): inner_sum(real_grad, real_kernel) + inner_sum(imag_grad, imag_kernel)  41.6 us
    dot_general x5, matrix products, mode_back(): inner_sum(real_grad, imag_kernel)  41.6 us
    dot_general x5, matrix products, mode_back(): inner_sum(imag_grad, imag_kernel)  41.6 us
    dot_general x5, matrix products, mode_back(): inner_sum(imag_grad, real_kernel) - inner_sum(real_grad, imag_kernel)  41.6 us
    ppermute x10, waiting for transfers between devices, passed_along(): return lax.ppermute(block, axis, route)  39.3 us
  transfers between devices with their start and end apart: 30, of which 20 were waited for; matrix products, arithmetic and copies ran while one was open for 12% of the time, Pallas kernels for 0%

commit v1 on v0

--- a/solution.py
+++ b/solution.py
@@ -3,7 +3,10 @@
 
 import jax
 import jax.numpy as jnp
+import numpy as np
 from jax import lax
+from jax.experimental import pallas as pl
+from jax.experimental.pallas import tpu as pltpu
 from jax.sharding import PartitionSpec as P
 
 highest = lax.Precision.HIGHEST
@@ -228,6 +231,540 @@
     return (kernel_sum[None], (point_total * factor)[None])
 
 
+f32, bf16 = (jnp.float32, jnp.bfloat16)
+NT = (((1,), (1,)), ((), ()))
+VMEM_LIMIT = 48 << 20
+
+
+def np_y_tables(col_count, mode_count):
+    ycells = np.arange(col_count)[:, None]
+    ymodes = np.arange(mode_count)[None, :]
+    angles = (ycells * ymodes % col_count) * (2.0 * math.pi / col_count)
+    factor = 1.0 / math.sqrt(col_count)
+    doubled = np.where(ymodes == 0, 1.0, 2.0)
+    forward = np.stack([np.cos(angles), -np.sin(angles)], axis=0) * factor
+    inverse = np.stack([doubled * np.cos(angles), -doubled * np.sin(angles)], axis=0) * factor
+    return (forward.transpose(2, 0, 1), inverse.transpose(2, 0, 1))
+
+
+def np_x_tables(row_total, mode_count):
+    kx_count = 2 * mode_count
+    indices = np.arange(kx_count)
+    freq = np.where(indices < mode_count, indices, indices - kx_count)
+    angles = (freq[:, None] * np.arange(row_total)[None, :] % row_total) * (2.0 * math.pi / row_total)
+    factor = 1.0 / math.sqrt(row_total)
+    c, s = (np.cos(angles) * factor, np.sin(angles) * factor)
+    forward = np.stack([np.stack([c, s], -1), np.stack([-s, c], -1)], axis=1)
+    inverse = np.stack([np.stack([c.T, -s.T], -1), np.stack([s.T, c.T], -1)], axis=1)
+    return (forward, inverse)
+
+
+def hdot(a, b):
+    return jnp.dot(a, b, precision=highest, preferred_element_type=f32)
+
+
+def split_rows(a):
+    hi = a.astype(bf16)
+    lo = (a - hi.astype(f32)).astype(bf16)
+    return jnp.concatenate([hi, lo], axis=0)
+
+
+def gelu_both(v, with_value=True):
+    k0 = math.sqrt(2.0 / math.pi)
+    k1 = k0 * 0.044715
+    v2 = v * v
+    t = jnp.tanh(v * (k0 + k1 * v2))
+    half = 0.5 * v
+    slope = (0.5 + 0.5 * t) + half * (1.0 - t * t) * (k0 + (3.0 * k1) * v2)
+    return (half + half * t if with_value else None, slope)
+
+
+def low_half(shape):
+    return lax.broadcasted_iota(jnp.int32, shape, 1) < shape[1] // 2
+
+
+def swap_halves(a):
+    return pltpu.roll(a, a.shape[1] // 2, 1)
+
+
+def own_rows(y_ref, row, x_count):
+    return jnp.concatenate(
+        [y_ref[pl.ds(row + p, x_count, stride=16), :] for p in range(2)], axis=0
+    )
+
+
+def forward_modes(y_ref, w_ref, lx_ref, xi_ref, t_ref, m_ref, out_ref):
+    pairs, lanes = (w_ref.shape[0], w_ref.shape[2])
+    x_count = y_ref.shape[0] // 16
+    half = t_ref.shape[0] // 2
+    ys = own_rows(y_ref, 8, x_count)
+    sw = swap_halves(ys)
+    low = low_half(ys.shape)
+    zero = jnp.zeros_like(ys)
+    rhs0 = jnp.concatenate([jnp.where(low, ys, zero), jnp.where(low, zero, sw)], axis=0)
+    rhs1 = jnp.concatenate([jnp.where(low, sw, zero), jnp.where(low, zero, ys)], axis=0)
+    t_ref[:half] = hdot(lx_ref[...], rhs0)
+    t_ref[half:] = hdot(lx_ref[...], rhs1)
+    for j in range(pairs):
+        rows = split_rows(t_ref[pl.ds(j, 8, stride=pairs), :])
+        prod = jnp.dot(rows, w_ref[j], preferred_element_type=f32)
+        m_ref[pl.ds(j, 8, stride=pairs), :] = prod[:8] + prod[8:]
+    m0, m1 = (m_ref[:half], m_ref[half:])
+    lowm = low_half(m0.shape)
+    first = (lax.broadcasted_iota(jnp.int32, m0.shape, 0) // pairs) % 2 == 0
+    s0 = jnp.where(first, m0, swap_halves(m0))
+    s1 = jnp.where(first, swap_halves(m1), m1)
+    out_ref[...] = hdot(xi_ref[...], jnp.where(lowm, s0, s1)).astype(bf16)
+
+
+def backward_modes(y_ref, w_ref, xa_ref, xf_ref, t_ref, m_ref, out_ref):
+    pairs = w_ref.shape[0]
+    x_count = y_ref.shape[0] // 16
+    half = t_ref.shape[0] // 2
+    g = hdot(xa_ref[...], own_rows(y_ref, 8, x_count))
+    sw = swap_halves(g)
+    low = low_half(g.shape)
+    first = (lax.broadcasted_iota(jnp.int32, g.shape, 0) // pairs) % 2 == 0
+    keep = low == first
+    zero = jnp.zeros_like(g)
+    t_ref[:half] = jnp.where(keep, jnp.where(first, g, sw), zero)
+    t_ref[half:] = jnp.where(keep, jnp.where(first, sw, g), zero)
+    for j in range(pairs):
+        rows = split_rows(t_ref[pl.ds(j, 8, stride=pairs), :])
+        prod = lax.dot_general(rows, w_ref[j], NT, preferred_element_type=f32)
+        m_ref[pl.ds(j, 8, stride=pairs), :] = prod[:8] + prod[8:]
+    quarter = half // 2
+    pr0, pi0, pr1, pi1 = (m_ref[i * quarter : (i + 1) * quarter] for i in range(4))
+    lowq = low_half(pr0.shape)
+    real = jnp.where(lowq, pr0 + swap_halves(pi0), swap_halves(pr1) + pi1)
+    imag = jnp.where(lowq, pi0 - swap_halves(pr0), swap_halves(pi1) - pr1)
+    out_ref[...] = hdot(xf_ref[...], jnp.concatenate([real, imag], axis=0)).astype(bf16)
+
+
+def widen(recv_ref, r_ref):
+    chunks, rows, _ = recv_ref.shape
+    for k in range(chunks):
+        r_ref[k * rows : (k + 1) * rows] = recv_ref[k].astype(f32)
+
+
+def row_product(weight, field, r_ref, table, x, x_count):
+    rows = r_ref[pl.ds(x, table.shape[0], stride=x_count), :]
+    lhs = jnp.concatenate([weight, rows.T.astype(bf16)], axis=1)
+    return jnp.dot(lhs, jnp.concatenate([field, table], axis=0), preferred_element_type=f32)
+
+
+def lift_kernel(in_ref, lw_ref, lb_ref, tab_ref, act_ref, y_ref, *, space, per_chunk, depth):
+    chunks = in_ref.shape[0]
+    for k in range(chunks):
+        base = (k % space) * (chunks // space) * per_chunk + (k // space) * per_chunk
+        for i in range(per_chunk):
+            cells = in_ref[k, i * depth : (i + 1) * depth, :]
+            act = jnp.dot(lw_ref[...], cells, preferred_element_type=f32) + lb_ref[...]
+            act = act.astype(bf16)
+            act_ref[base + i] = act
+            y_ref[(base + i) * 16 : (base + i + 1) * 16] = lax.dot_general(
+                tab_ref[...], act, NT, preferred_element_type=f32
+            )
+
+
+def first_modes_kernel(y_ref, w_ref, lx_ref, xi_ref, out_ref, t_ref, m_ref):
+    forward_modes(y_ref, w_ref, lx_ref, xi_ref, t_ref, m_ref, out_ref)
+
+
+def forward_kernel(
+    recv_ref, act_ref, pw_ref, pb_ref, inv_ref, tab_ref, w_ref, lx_ref, xi_ref,
+    next_ref, slope_ref, y_ref, out_ref, r_ref, t_ref, m_ref,
+):
+    step = pl.program_id(0)
+    block = act_ref.shape[0]
+    x_count = y_ref.shape[0] // 16
+
+    @pl.when(step == 0)
+    def _():
+        widen(recv_ref, r_ref)
+
+    def one(i, carry):
+        x = step * block + i
+        pre = row_product(pw_ref[...], act_ref[i], r_ref, inv_ref[...], x, x_count) + pb_ref[...]
+        value, slope = gelu_both(pre)
+        value = value.astype(bf16)
+        next_ref[i] = value
+        slope_ref[i] = slope.astype(bf16)
+        y_ref[pl.ds(pl.multiple_of(x * 16, 16), 16), :] = lax.dot_general(
+            tab_ref[...], value, NT, preferred_element_type=f32
+        )
+        return carry
+
+    lax.fori_loop(0, block, one, 0, unroll=2)
+
+    @pl.when(step == pl.num_programs(0) - 1)
+    def _():
+        forward_modes(y_ref, w_ref, lx_ref, xi_ref, t_ref, m_ref, out_ref)
+
+
+def adjoint_rows(x, i, grad, act, tab_ref, pre_ref, y_ref, point_ref):
+    pre_grad = grad.astype(bf16)
+    pre_ref[i] = pre_grad
+    both = lax.dot_general(
+        jnp.concatenate([tab_ref[...], act], axis=0), pre_grad, NT, preferred_element_type=f32
+    )
+    y_ref[pl.ds(pl.multiple_of(x * 16, 16), 16), :] = both[:16]
+    point_ref[...] += both[16:]
+
+
+def top_kernel(
+    recv_ref, act_ref, in_ref, pw_ref, pb_ref, inv_ref, up_ref, hb_ref, down_ref, ow_ref, tab_ref,
+    w_ref, xa_ref, xf_ref,
+    pre_ref, y_ref, point_ref, out_ref, r_ref, t_ref, m_ref, *, space, per_chunk, first_row, batch,
+):
+    step = pl.program_id(0)
+    block = act_ref.shape[0]
+    x_count = y_ref.shape[0] // 16
+    parts = in_ref.shape[0] // space
+
+    @pl.when(step == 0)
+    def _():
+        widen(recv_ref, r_ref)
+        point_ref[...] = jnp.zeros_like(point_ref)
+
+    def one(i, carry):
+        x = step * block + i
+        act = act_ref[i]
+        pre = row_product(pw_ref[...], act, r_ref, inv_ref[...], x, x_count) + pb_ref[...]
+        value, slope = gelu_both(pre)
+        value = value.astype(bf16)
+        pair = x // per_chunk
+        chunk = (pair % parts) * space + pair // parts
+        within = x % per_chunk
+        cots = in_ref[chunk, first_row : first_row + per_chunk * batch, :].astype(f32)
+        grads = []
+        size = value.shape[0] // batch
+        for b in range(batch):
+            hidden = jnp.dot(up_ref[...], value[b * size : (b + 1) * size], preferred_element_type=f32)
+            _, hidden_slope = gelu_both(hidden + hb_ref[...], False)
+            cot = cots[b : b + 1]
+            for other in range(1, per_chunk):
+                row = other * batch + b
+                cot = jnp.where(within == other, cots[row : row + 1], cot)
+            hidden_grad = (hidden_slope * (ow_ref[...] * cot)).astype(bf16)
+            grads.append(jnp.dot(down_ref[...], hidden_grad, preferred_element_type=f32))
+        grad = jnp.concatenate(grads, axis=0).astype(bf16).astype(f32)
+        adjoint_rows(x, i, grad * slope, act, tab_ref, pre_ref, y_ref, point_ref)
+        return carry
+
+    lax.fori_loop(0, block, one, 0)
+
+    @pl.when(step == pl.num_programs(0) - 1)
+    def _():
+        backward_modes(y_ref, w_ref, xa_ref, xf_ref, t_ref, m_ref, out_ref)
+
+
+def backward_kernel(
+    recv_ref, grad_ref, slope_ref, act_ref, pw_ref, fwd_ref, tab_ref, w_ref, xa_ref, xf_ref,
+    pre_ref, y_ref, point_ref, out_ref, r_ref, t_ref, m_ref, *, send,
+):
+    step = pl.program_id(0)
+    block = act_ref.shape[0]
+    x_count = y_ref.shape[0] // 16
+
+    @pl.when(step == 0)
+    def _():
+        widen(recv_ref, r_ref)
+        point_ref[...] = jnp.zeros_like(point_ref)
+
+    def one(i, carry):
+        x = step * block + i
+        grad = row_product(pw_ref[...], grad_ref[i], r_ref, fwd_ref[...], x, x_count)
+        grad = grad.astype(bf16).astype(f32) * slope_ref[i].astype(f32)
+        adjoint_rows(x, i, grad, act_ref[i], tab_ref, pre_ref, y_ref, point_ref)
+        return carry
+
+    lax.fori_loop(0, block, one, 0, unroll=2)
+
+    @pl.when(step == pl.num_programs(0) - 1)
+    def _():
+        if send:
+            backward_modes(y_ref, w_ref, xa_ref, xf_ref, t_ref, m_ref, out_ref)
+        else:
+            out_ref[...] = jnp.zeros_like(out_ref)
+
+
+def grads_kernel(seg_ref, *refs, layers, scale):
+    ya_refs, yg_refs, pg_refs = (refs[:layers], refs[layers : 2 * layers], refs[2 * layers : 3 * layers])
+    xz_ref, xa_ref, out_ref, point_ref, ya, yg, a_ref, b_ref = refs[3 * layers :]
+    mode = pl.program_id(0)
+    x_count = ya.shape[0] // 16
+
+    @pl.when(mode == 0)
+    def _():
+        for layer in range(layers):
+            @pl.when(seg_ref[0] == layer)
+            def _():
+                ya[...] = ya_refs[layer][...]
+                yg[...] = yg_refs[layer][...]
+                pg = pg_refs[layer][...]
+                c = point_ref.shape[0]
+                point_ref[...] = (pg[:c, :c] + pg[c:, c:]) * scale
+
+    z = hdot(xz_ref[...], own_rows(ya, 2 * mode, x_count))
+    g = hdot(xa_ref[...], own_rows(yg, 2 * mode, x_count))
+    rows = z.shape[0]
+    kx = rows // 2
+    zs, gs = (swap_halves(z), swap_halves(g))
+    c = z.shape[1] // 2
+    a_ref[:rows] = z
+    a_ref[rows:] = zs
+    low = low_half((kx, z.shape[1]))
+    b_ref[:kx] = jnp.where(low, g[:kx], gs[kx:])
+    b_ref[kx:rows] = jnp.where(low, g[kx:], -gs[:kx])
+    b_ref[rows : rows + kx] = jnp.where(low, gs[:kx], g[kx:])
+    b_ref[rows + kx :] = jnp.where(low, gs[kx:], -g[:kx])
+    for j in range(kx):
+        a = a_ref[pl.ds(j, 4, stride=kx), :][:, :c]
+        b = b_ref[pl.ds(j, 4, stride=kx), :]
+        ah, bh = (a.astype(bf16), b.astype(bf16))
+        al, bl = ((a - ah.astype(f32)).astype(bf16), (b - bh.astype(f32)).astype(bf16))
+        left = jnp.concatenate([ah.astype(f32), al.astype(f32), ah.astype(f32)], axis=0)
+        right = jnp.concatenate([bh.astype(f32), bh.astype(f32), bl.astype(f32)], axis=0).astype(bf16)
+        left = left.T.astype(bf16)
+        out_ref[0, j, 0] = jnp.dot(left, right[:, :c], preferred_element_type=f32)
+        out_ref[0, j, 1] = jnp.dot(left, right[:, c:], preferred_element_type=f32)
+
+
+def replicated(
+    inputs, cotangent, lift_weight, lift_bias, point_weight, layer_bias, spectral_weight,
+    proj_weight, proj_bias, out_weight,
+):
+    batch, row_count, depth, cols = inputs.shape
+    segments, space = (lax.axis_size("segment"), lax.axis_size("space"))
+    seg, place = (lax.axis_index("segment"), lax.axis_index("space"))
+    both = ("segment", "space")
+    chunks = segments * space
+    owned, kx = spectral_weight.shape[1:3]
+    c = point_weight.shape[1]
+    bc = batch * c
+    x_count = row_count * space
+    mode_count = owned * space
+    per_chunk = row_count // segments
+    pairs = kx // 2
+
+    stack = spectral_weight[0].reshape(owned, 2, pairs, 2 * c, c)
+    packed = [
+        jnp.concatenate([w[0], w[1]], axis=-1)
+        for w in (
+            lax.dynamic_index_in_dim(stack, (seg + d) % segments, 0, keepdims=False)
+            for d in range(segments)
+        )
+    ]
+    moved = []
+    for parity in range(2):
+        moved.append([
+            lax.ppermute(
+                packed[d], "segment",
+                [(i, (i + d) % segments) for i in range(parity, segments, 2)],
+            )
+            for d in range(1, segments)
+        ])
+
+    def layer_kernel(layer):
+        options = [packed[0]] + moved[layer % 2]
+        result = options[0]
+        shift = (seg - layer) % segments
+        for d in range(1, segments):
+            result = jnp.where(shift == d, options[d], result)
+        return result
+
+    cells = lax.dynamic_slice_in_dim(inputs, seg * per_chunk, per_chunk, 1)
+    cells = jnp.transpose(cells, (1, 0, 2, 3)).reshape(per_chunk * batch * depth, cols)
+    cots = lax.dynamic_slice_in_dim(cotangent, seg * per_chunk, per_chunk, 1)
+    cots = jnp.transpose(cots, (1, 0, 2)).reshape(per_chunk * batch, cols)
+    weight_rows = c * c // space // cols
+    share = lax.dynamic_index_in_dim(
+        point_weight.reshape(space, weight_rows, cols), place, 0, keepdims=False
+    )
+    high = lax.reduce_precision(layer_bias[0], 8, 7)
+    mid = lax.reduce_precision(layer_bias[0] - high, 8, 7)
+    rest = layer_bias[0] - high - mid
+    bias_row = jnp.concatenate([high, mid, rest, jnp.zeros((cols - 3 * c,), f32)]).astype(bf16)
+    chunk = jnp.concatenate([cells, cots, share, bias_row[None]], axis=0)
+    cot_row = per_chunk * batch * depth
+    share_row = cot_row + per_chunk * batch
+    bias_at = share_row + weight_rows
+    chunk = jnp.pad(chunk, ((0, -chunk.shape[0] % 16), (0, 0)))
+
+    def to_all(block):
+        return lax.all_to_all(
+            jnp.broadcast_to(block[None], (chunks,) + block.shape), both, 0, 0, tiled=True
+        )
+
+    grid_in = to_all(chunk)
+    points = grid_in[:, share_row:bias_at].reshape(segments, c, c)
+    bias_parts = grid_in[::space, bias_at, : 3 * c].astype(f32).reshape(segments, 3, c)
+    biases = bias_parts[:, 0] + bias_parts[:, 1] + bias_parts[:, 2]
+    blank = jnp.zeros((segments, c, c), bf16)
+
+    def doubled(mats):
+        return jnp.concatenate(
+            [jnp.concatenate([mats, blank], axis=2), jnp.concatenate([blank, mats], axis=2)], axis=1
+        )
+
+    point_back = doubled(points)
+    point_fwd = doubled(jnp.transpose(points, (0, 2, 1)))
+    bias_cols = jnp.concatenate([biases] * batch, axis=1)[:, :, None]
+
+    y_forward, y_inverse = np_y_tables(cols, mode_count)
+    x_forward, x_inverse = np_x_tables(x_count, kx // 2)
+    order = [(k % space) * owned + k // space for k in range(chunks)]
+
+    def gathered(table):
+        return jnp.asarray(table[order].reshape(2 * chunks, cols), bf16)
+
+    def analysis(table):
+        full = np.zeros((chunks, 16, cols))
+        for k in range(chunks):
+            s = k % space
+            full[k, : 2 * owned] = table[s * owned : (s + 1) * owned].reshape(2 * owned, cols)
+            full[k, 8:10] = table[order[k]]
+        return lax.dynamic_index_in_dim(
+            jnp.asarray(full, bf16), seg * space + place, 0, keepdims=False
+        )
+
+    inv_table, fwd_table = (gathered(y_inverse), gathered(y_forward))
+    act_table, grad_table = (analysis(y_forward), analysis(y_inverse))
+    xf = x_forward.transpose(0, 1, 3, 2).reshape(kx, 2, 2 * x_count)
+    lx = np.concatenate(
+        [np.concatenate([xf[:, 0], -xf[:, 1]], 1), np.concatenate([xf[:, 1], xf[:, 0]], 1)], 0
+    )
+    xz = xf.transpose(1, 0, 2).reshape(2 * kx, 2 * x_count)
+    xi = x_inverse.transpose(1, 0, 3, 2).reshape(2 * x_count, 2 * kx)
+    lx, xz, xi, xa, xb = (jnp.asarray(t, f32) for t in (lx, xz, xi, xi.T.copy(), xz.T.copy()))
+
+    def whole(array):
+        rank = len(array.shape)
+        return pl.BlockSpec(array.shape, lambda *i: (0,) * rank)
+
+    def call(kernel, args, blocked, outs, scratch, steps, name):
+        def spec(array, is_blocked):
+            if is_blocked:
+                return pl.BlockSpec((array.shape[0] // steps,) + array.shape[1:], lambda i: (i, 0, 0))
+            return whole(array)
+
+        return pl.pallas_call(
+            kernel,
+            grid=(steps,),
+            in_specs=[spec(a, n in blocked) for n, a in enumerate(args)],
+            out_specs=[spec(a, is_blocked) for a, is_blocked in outs],
+            out_shape=[a for a, _ in outs],
+            scratch_shapes=scratch,
+            compiler_params=pltpu.CompilerParams(vmem_limit_bytes=VMEM_LIMIT),
+            name=name,
+        )(*args)
+
+    field = jax.ShapeDtypeStruct((x_count, bc, cols), bf16)
+    ycoef = jax.ShapeDtypeStruct((x_count * 16, bc), f32)
+    sent = jax.ShapeDtypeStruct((2 * x_count, bc), bf16)
+    point = jax.ShapeDtypeStruct((bc, bc), f32)
+    mode_scratch = [pltpu.VMEM((2 * batch * kx, 2 * c), f32)] * 2
+    row_scratch = [pltpu.VMEM((chunks * 2 * x_count, bc), f32)]
+    steps = 4
+
+    zero = jnp.zeros_like(lift_weight.T)
+    lift = jnp.concatenate(
+        [jnp.concatenate([lift_weight.T, zero], 1), jnp.concatenate([zero, lift_weight.T], 1)], 0
+    )
+    lift_col = jnp.concatenate([lift_bias] * batch)[:, None]
+    act, y0 = call(
+        partial(lift_kernel, space=space, per_chunk=per_chunk, depth=batch * depth),
+        (grid_in, lift, lift_col, act_table), (), [(field, False), (ycoef, False)], [], 1, "lift",
+    )
+    acts, slopes, ya = ([act], [], [y0])
+    kernels = [layer_kernel(layer) for layer in range(segments)]
+    (mine,) = call(
+        first_modes_kernel, (y0, kernels[0], lx, xi), (), [(sent, False)], mode_scratch, 1, "modes"
+    )
+    for layer in range(1, segments):
+        recv = to_all(mine)
+        act, slope, y, mine = call(
+            forward_kernel,
+            (recv, acts[-1], point_fwd[layer - 1], bias_cols[layer - 1], inv_table, act_table,
+             kernels[layer], lx, xi),
+            (1,), [(field, True), (field, True), (ycoef, False), (sent, False)],
+            row_scratch + mode_scratch, steps, "forward",
+        )
+        acts.append(act)
+        slopes.append(slope)
+        ya.append(y)
+
+    recv = to_all(mine)
+    last = segments - 1
+    pre_grad, y, pg, mine = call(
+        partial(top_kernel, space=space, per_chunk=per_chunk, first_row=cot_row, batch=batch),
+        (recv, acts[last], grid_in, point_fwd[last], bias_cols[last], inv_table,
+         proj_weight.T, proj_bias[:, None], proj_weight, out_weight.astype(f32)[:, None],
+         grad_table, kernels[last], xa, xb),
+        (1,), [(field, True), (ycoef, False), (point, False), (sent, False)],
+        row_scratch + mode_scratch, steps, "top",
+    )
+    yg, pgs = ([y], [pg])
+    for layer in reversed(range(last)):
+        recv = to_all(mine)
+        pre_grad, y, pg, mine = call(
+            partial(backward_kernel, send=layer > 0),
+            (recv, pre_grad, slopes[layer], acts[layer], point_back[layer + 1], fwd_table,
+             grad_table, kernels[layer], xa, xb),
+            (1, 2, 3), [(field, True), (ycoef, False), (point, False), (sent, False)],
+            row_scratch + mode_scratch, steps, "backward",
+        )
+        yg.insert(0, y)
+        pgs.insert(0, pg)
+
+    scale = 1.0 / math.sqrt(batch * x_count * cols)
+    pieces = ya + yg + pgs + [xz, xa]
+    spectral, point_out = pl.pallas_call(
+        partial(grads_kernel, layers=segments, scale=scale),
+        grid=(owned,),
+        in_specs=[pl.BlockSpec(memory_space=pltpu.SMEM)] + [whole(a) for a in pieces],
+        out_specs=[
+            pl.BlockSpec((1, kx, 2, c, c), lambda m: (m, 0, 0, 0, 0)),
+            pl.BlockSpec((c, c), lambda m: (0, 0)),
+        ],
+        out_shape=[
+            jax.ShapeDtypeStruct((owned, kx, 2, c, c), f32),
+            jax.ShapeDtypeStruct((c, c), f32),
+        ],
+        scratch_shapes=[pltpu.VMEM((x_count * 16, bc), f32)] * 2
+        + [pltpu.VMEM((2 * batch * kx, bc), f32)] * 2,
+        compiler_params=pltpu.CompilerParams(vmem_limit_bytes=VMEM_LIMIT),
+        name="grads",
+    )(seg.astype(jnp.int32).reshape(1), *pieces)
+    return (spectral[None], point_out[None])
+
+
+def fits_replicated(mesh, inputs, point_weight, spectral_weight):
+    segments, space = (mesh.shape["segment"], mesh.shape["space"])
+    batch = inputs.shape[0] // mesh.shape["groups"]
+    _, rows, depth, cols = inputs.shape
+    layers, c, _ = point_weight.shape
+    modes, kx = spectral_weight.shape[1:3]
+    return (
+        batch == 2
+        and batch * c == 128
+        and layers == segments
+        and segments * space <= 16
+        and modes == segments * space
+        and modes // space <= 4
+        and rows % (segments * space) == 0
+        and rows % 32 == 0
+        and rows <= 64
+        and kx % 16 == 0
+        and kx <= 64
+        and batch * depth == 16
+        and cols % 128 == 0
+        and cols >= 3 * c
+        and c * c % (space * cols) == 0
+    )
+
+
 def solution(mesh):
     in_specs = (
         P("groups", "space", None, None),
@@ -245,6 +782,15 @@
         P(("groups", "segment"), "space", None, None, None, None),
         P(("groups", "segment"), None, None),
     )
-    return jax.shard_map(
-        on_device, mesh=mesh, in_specs=in_specs, out_specs=out_specs, check_vma=False
-    )
+
+    def step(inputs, cotangent, lift_weight, lift_bias, point_weight, layer_bias, spectral_weight, *rest):
+        fits = fits_replicated(mesh, inputs, point_weight, spectral_weight)
+        mapped = jax.shard_map(
+            replicated if fits else on_device,
+            mesh=mesh, in_specs=in_specs, out_specs=out_specs, check_vma=False,
+        )
+        return mapped(
+            inputs, cotangent, lift_weight, lift_bias, point_weight, layer_bias, spectral_weight, *rest
+        )
+
+    return step

time: 621 us -> 252 us (0.41)
  matrix products: 293 us -> 0 us
  Pallas kernels: 0 us -> 92.4 us
  other arithmetic: 86.2 us -> 7.02 us
  waiting for transfers between devices: 95 us -> 48.9 us
  starting transfers between devices: 87.9 us -> 43.1 us
  blocking collectives: 16 us -> 26.4 us
  loops' own time: 8.3 us -> 0 us
    dot_general x100 -> x0, matrix products: 293 us -> none  [the longest x10 45.7 us: mode_mult(): real_out = product(real_in, real_kernel) - product(imag_in, imag_kernel)]
    pallas_call x0 -> x10, Pallas kernels: none -> 92.4 us  [the longest x9 87 us: call(): pl.pallas_call(kernel, grid=(steps,), in_specs=[spec(a, n in blocked) for...]
    add x5 -> x1, other arithmetic: 44.7 us -> 0.01 us  [replicated(): biases = bias_parts[:, 0] + bias_parts[:, 1] + bias_parts[:, 2]]
    all_to_all x20 -> x6, starting transfers between devices: 70.7 us -> 29.9 us  [to_all(): lax.all_to_all(jnp.broadcast_to(block[None], (chunks,) + block.shape), bo...]
    ppermute x10 -> x6, waiting for transfers between devices: 39.3 us -> 8.7 us  [replicated(): lax.ppermute(packed[d], 'segment', [(i, (i + d) % segments) for i in rang...]
    all_to_all x0 -> x2, blocking collectives: none -> 26.4 us  [to_all(): lax.all_to_all(jnp.broadcast_to(block[None], (chunks,) + block.shape), bo...]
    another operation x17 -> x1, other arithmetic: 23.3 us -> 0.01 us  [step(): mapped(inputs, cotangent, lift_weight, lift_bias, point_weight, layer_bia...]
    unnamed x11 -> x72, local copies, waits for them, and re-layouts: 0.04 us -> 18.5 us
  transfers between devices with their start and end apart: 30 -> 12, of which waited for: 20 -> 6; matrix products, arithmetic and copies ran while one was open for 12% -> 4% of each run, Pallas kernels for 0% -> 0%
where the time goes in v1:
time: 252 us; the launch traced here: 249 us
  Pallas kernels  92.4 us (37%)
  waiting for transfers between devices  48.9 us (19%)
  starting transfers between devices  43.1 us (17%)
  local copies, waits for them, and re-layouts  29.7 us (12%)
  blocking collectives  26.4 us (10%)
  other arithmetic  7.02 us (3%)
    pallas_call x9, Pallas kernels, call(): pl.pallas_call(kernel, grid=(steps,), in_specs=[spec(a, n in blocked) for...  87 us
    all_to_all x6, waiting for transfers between devices, to_all(): lax.all_to_all(jnp.broadcast_to(block[None], (chunks,) + block.shape), bo...  40.2 us
    all_to_all x6, starting transfers between devices, to_all(): lax.all_to_all(jnp.broadcast_to(block[None], (chunks,) + block.shape), bo...  29.9 us
    all_to_all x2, blocking collectives, to_all(): lax.all_to_all(jnp.broadcast_to(block[None], (chunks,) + block.shape), bo...  26.4 us
    unnamed x72, local copies, waits for them, and re-layouts  18.5 us
    ppermute x6, starting transfers between devices, replicated(): lax.ppermute(packed[d], 'segment', [(i, (i + d) % segments) for i in rang...  13.2 us
    ppermute x6, waiting for transfers between devices, replicated(): lax.ppermute(packed[d], 'segment', [(i, (i + d) % segments) for i in rang...  8.7 us
    pallas_call x1, Pallas kernels, replicated(): pl.pallas_call(partial(grads_kernel, layers=segments, scale=scale), grid=...  5.34 us
  transfers between devices with their start and end apart: 12, of which 6 were waited for; matrix products, arithmetic and copies ran while one was open for 4% of the time, Pallas kernels for 0%

profile of v1, /device:TPU:3, one launch (start us, length us, event | category | flops | bytes accessed | tf_op | source)
XLA Modules:
  0.0 248.8 jit_solution(8911024607048549137)
XLA Ops:
  0.7 2.7 %dynamic-slice_bitcast_fusion.1 = (bf16[16,128,64]{2,1,0:T(8,128)(2,1)S(1)}, bf16[16,128,64]{2,1,0:T(8,128)(2,1)S(1)}, bf16[16,128,64]{2,1,0:T(8,128)(2,1)S(1)},...) fusion(bf16[4,2,16,128,64]{4,3,2,1,0:T(8,128)(2,1)} %bitcast.64, ...), kind=kLoop, calls=%fused_computation.1 | loop fusion | bytes 4194324 | tf_op jit(solution)/shard_map/squeeze | solution.py:553
  8.2 4.5 %collective-permute-start.4 = (bf16[16,128,128]{2,1,0:T(8,128)(2,1)}, bf16[16,128,128]{2,1,0:T(8,128)(2,1)S(1)}, u32[]{:S(2)}, u32[]{:S(2)}) collective-permute-start(bf16[16,128,128]{2,1,0:T(8,128)(2,1)} %pad_maximum_fusion.1), channel_id=1, source_target_pairs={{4,12},{12,4},{5,13},{13,5},{6,14},{14,6},{7,15},{15,7},{20,28},{2... | collective-permute-start | bytes 1572872 | tf_op jit(solution)/shard_map/ppermute | solution.py:562
  12.8 1.5 collective-permute-start.1
  15.3 3.3 %collective-permute-start.3 = (bf16[16,128,128]{2,1,0:T(8,128)(2,1)}, bf16[16,128,128]{2,1,0:T(8,128)(2,1)S(1)}, u32[]{:S(2)}, u32[]{:S(2)}) collective-permute-start(bf16[16,128,128]{2,1,0:T(8,128)(2,1)} %pad_maximum_fusion), channel_id=1, source_target_pairs={{4,0},{12,8},{5,1},{13,9},{6,2},{14,10},{7,3},{15,11},{20,16},{28,... | collective-permute-start | bytes 1572872 | tf_op jit(solution)/shard_map/ppermute | solution.py:562
  20.5 6.1 %all-to-all-start = ((bf16[16,48,256]{2,1,0:T(8,128)(2,1)}), bf16[16,48,256]{2,1,0:T(8,128)(2,1)S(1)}, u32[]{:S(2)}, u32[]{:S(2)}) async-start(bf16[16,48,256]{2,1,0:T(8,128)(2,1)} %broadcast_in_dim.31), calls=%async_computation | async-start | bytes 786432 | tf_op jit(solution)/shard_map/all_to_all | solution.py:596
  30.4 8.7 %collective-permute-done = bf16[16,128,128]{2,1,0:T(8,128)(2,1)} collective-permute-done((bf16[16,128,128]{2,1,0:T(8,128)(2,1)}, bf16[16,128,128]{2,1,0:T(8,128)(2,1)}, u32[]{:S(2)}, u32[]{:S(2)}) %collective-permute-start) | collective-permute-done | bytes 524320 | tf_op jit(solution)/shard_map/ppermute | solution.py:562
  39.1 1.8 select_select_fusion.1
  45.1 5.6 %all-to-all-start.1 = ((bf16[16,64,128]{2,1,0:T(8,128)(2,1)}), bf16[16,64,128]{2,1,0:T(8,128)(2,1)S(1)}, u32[]{:S(2)}, u32[]{:S(2)}) async-start(bf16[16,64,128]{2,1,0:T(8,128)(2,1)} %broadcast_in_dim.33), calls=%async_computation.1 | async-start | bytes 524288 | tf_op jit(solution)/shard_map/all_to_all | solution.py:596
  51.9 7.7 %all-to-all-done.1.recv_ref = bf16[16,64,128]{2,1,0:T(8,128)(2,1)S(1)} async-done(((bf16[16,64,128]{2,1,0:T(8,128)(2,1)}), bf16[16,64,128]{2,1,0:T(8,128)(2,1)S(1)}, u32[]{:S(2)}, u32[]{:S(2)}) %all-to-all-start.1) | async-done | bytes 262176 | tf_op jit(solution)/shard_map/all_to_all | solution.py:596
  59.5 10.0 %forward.3 = (bf16[32,128,256]{2,1,0:T(8,128)(2,1)S(1)}, bf16[32,128,256]{2,1,0:T(8,128)(2,1)S(1)}, f32[512,128]{1,0:T(8,128)S(1)}, bf16[64,128]{1,0:T(8,128)(2,1)S(1)}) custom-call(bf16[16,64,128]{2,1,0:T(8,128)(2,1)S(1)} %all-to-all-done.1.recv_ref, bf16[32,128,256]{2,1,0:T(8,128)(2,1)} %copy-done.1, bf16[128,128]{1,0:T(8,128)(2,1)S(1)} %copy.56.pw_ref, ...), custom_call_target="tpu_custom_call" | custom-call | tf_op jit(solution)/shard_map/forward/pallas_call | solution.py:652
  73.7 4.6 %all-to-all-start.2 = ((bf16[16,64,128]{2,1,0:T(8,128)(2,1)}), bf16[16,64,128]{2,1,0:T(8,128)(2,1)S(1)}, u32[]{:S(2)}, u32[]{:S(2)}) async-start(bf16[16,64,128]{2,1,0:T(8,128)(2,1)} %broadcast_in_dim.34), calls=%async_computation.2 | async-start | bytes 524288 | tf_op jit(solution)/shard_map/all_to_all | solution.py:596
  78.5 8.6 %all-to-all-done.2.recv_ref = bf16[16,64,128]{2,1,0:T(8,128)(2,1)S(1)} async-done(((bf16[16,64,128]{2,1,0:T(8,128)(2,1)}), bf16[16,64,128]{2,1,0:T(8,128)(2,1)S(1)}, u32[]{:S(2)}, u32[]{:S(2)}) %all-to-all-start.2) | async-done | bytes 262176 | tf_op jit(solution)/shard_map/all_to_all | solution.py:596
  87.1 10.0 %forward.4 = (bf16[32,128,256]{2,1,0:T(8,128)(2,1)S(1)}, bf16[32,128,256]{2,1,0:T(8,128)(2,1)S(1)}, f32[512,128]{1,0:T(8,128)S(1)}, bf16[64,128]{1,0:T(8,128)(2,1)S(1)}) custom-call(bf16[16,64,128]{2,1,0:T(8,128)(2,1)S(1)} %all-to-all-done.2.recv_ref, bf16[32,128,256]{2,1,0:T(8,128)(2,1)} %copy-done.2, bf16[128,128]{1,0:T(8,128)(2,1)S(1)} %copy.58.pw_ref, ...), custom_call_target="tpu_custom_call" | custom-call | tf_op jit(solution)/shard_map/forward/pallas_call | solution.py:652
  97.1 1.4 copy-done.3
  101.3 4.6 %all-to-all-start.3 = ((bf16[16,64,128]{2,1,0:T(8,128)(2,1)}), bf16[16,64,128]{2,1,0:T(8,128)(2,1)S(1)}, u32[]{:S(2)}, u32[]{:S(2)}) async-start(bf16[16,64,128]{2,1,0:T(8,128)(2,1)} %broadcast_in_dim.35), calls=%async_computation.3 | async-start | bytes 524288 | tf_op jit(solution)/shard_map/all_to_all | solution.py:596
  106.1 8.6 %all-to-all-done.3.recv_ref = bf16[16,64,128]{2,1,0:T(8,128)(2,1)S(1)} async-done(((bf16[16,64,128]{2,1,0:T(8,128)(2,1)}), bf16[16,64,128]{2,1,0:T(8,128)(2,1)S(1)}, u32[]{:S(2)}, u32[]{:S(2)}) %all-to-all-start.3) | async-done | bytes 262176 | tf_op jit(solution)/shard_map/all_to_all | solution.py:596
  114.7 10.0 %forward.5 = (bf16[32,128,256]{2,1,0:T(8,128)(2,1)S(1)}, bf16[32,128,256]{2,1,0:T(8,128)(2,1)S(1)}, f32[512,128]{1,0:T(8,128)S(1)}, bf16[64,128]{1,0:T(8,128)(2,1)S(1)}) custom-call(bf16[16,64,128]{2,1,0:T(8,128)(2,1)S(1)} %all-to-all-done.3.recv_ref, bf16[32,128,256]{2,1,0:T(8,128)(2,1)} %copy-done.3, bf16[128,128]{1,0:T(8,128)(2,1)S(1)} %copy.60.pw_ref, ...), custom_call_target="tpu_custom_call" | custom-call | tf_op jit(solution)/shard_map/forward/pallas_call | solution.py:652
  124.7 1.4 copy-done.5
  128.9 4.6 %all-to-all-start.4 = ((bf16[16,64,128]{2,1,0:T(8,128)(2,1)}), bf16[16,64,128]{2,1,0:T(8,128)(2,1)S(1)}, u32[]{:S(2)}, u32[]{:S(2)}) async-start(bf16[16,64,128]{2,1,0:T(8,128)(2,1)} %broadcast_in_dim.36), calls=%async_computation.4 | async-start | bytes 524288 | tf_op jit(solution)/shard_map/all_to_all | solution.py:596
  134.8 7.5 %all-to-all-done.4.recv_ref = bf16[16,64,128]{2,1,0:T(8,128)(2,1)S(1)} async-done(((bf16[16,64,128]{2,1,0:T(8,128)(2,1)}), bf16[16,64,128]{2,1,0:T(8,128)(2,1)S(1)}, u32[]{:S(2)}, u32[]{:S(2)}) %all-to-all-start.4) | async-done | bytes 262176 | tf_op jit(solution)/shard_map/all_to_all | solution.py:596
  142.3 1.6 copy-done.6
  143.9 28.0 %top.1 = (bf16[32,128,256]{2,1,0:T(8,128)(2,1)S(1)}, f32[512,128]{1,0:T(8,128)S(1)}, f32[128,128]{1,0:T(8,128)S(1)}, bf16[64,128]{1,0:T(8,128)(2,1)S(1)}) custom-call(bf16[16,64,128]{2,1,0:T(8,128)(2,1)S(1)} %all-to-all-done.4.recv_ref, bf16[32,128,256]{2,1,0:T(8,128)(2,1)S(1)} %copy-done.6, bf16[16,48,256]{2,1,0:T(8,128)(2,1)S(1)} %all-to-all-done.in_ref, ...), custom_call_target="tpu_custom_call" | custom-call | tf_op jit(solution)/shard_map/top/pallas_call | solution.py:652
  171.9 1.4 copy-done.10
  174.8 4.6 %all-to-all-start.5 = ((bf16[16,64,128]{2,1,0:T(8,128)(2,1)}), bf16[16,64,128]{2,1,0:T(8,128)(2,1)S(1)}, u32[]{:S(2)}, u32[]{:S(2)}) async-start(bf16[16,64,128]{2,1,0:T(8,128)(2,1)} %broadcast_in_dim.40), calls=%async_computation.5 | async-start | bytes 524288 | tf_op jit(solution)/shard_map/all_to_all | solution.py:596
  180.3 7.8 %all-to-all-done.5.recv_ref = bf16[16,64,128]{2,1,0:T(8,128)(2,1)S(1)} async-done(((bf16[16,64,128]{2,1,0:T(8,128)(2,1)}), bf16[16,64,128]{2,1,0:T(8,128)(2,1)S(1)}, u32[]{:S(2)}, u32[]{:S(2)}) %all-to-all-start.5) | async-done | bytes 262176 | tf_op jit(solution)/shard_map/all_to_all | solution.py:596
  188.2 1.6 copy-done.11
  189.8 9.0 %backward.3 = (bf16[32,128,256]{2,1,0:T(8,128)(2,1)S(1)}, f32[512,128]{1,0:T(8,128)S(1)}, f32[128,128]{1,0:T(8,128)S(1)}, bf16[64,128]{1,0:T(8,128)(2,1)S(1)}) custom-call(bf16[16,64,128]{2,1,0:T(8,128)(2,1)S(1)} %all-to-all-done.5.recv_ref, bf16[32,128,256]{2,1,0:T(8,128)(2,1)S(1)} %copy-done.11, bf16[32,128,256]{2,1,0:T(8,128)(2,1)} %copy-done.9, ...), custom_call_target="tpu_custom_call" | custom-call | tf_op jit(solution)/shard_map/backward/pallas_call | solution.py:652
  198.8 13.2 %all_to_all.40.recv_ref = bf16[16,64,128]{2,1,0:T(8,128)(2,1)S(1)} all-to-all(bf16[16,64,128]{2,1,0:T(8,128)(2,1)S(1)} %broadcast_in_dim.41), channel_id=1, replica_groups=mesh['groups'=2,'segment'=4,'space'=4] {'segment','space'}, dimensions={0} | all-to-all | bytes 524288 | tf_op jit(solution)/shard_map/all_to_all | solution.py:596
  212.0 9.0 %backward.4 = (bf16[32,128,256]{2,1,0:T(8,128)(2,1)S(1)}, f32[512,128]{1,0:T(8,128)S(1)}, f32[128,128]{1,0:T(8,128)S(1)}, bf16[64,128]{1,0:T(8,128)(2,1)S(1)}) custom-call(bf16[16,64,128]{2,1,0:T(8,128)(2,1)S(1)} %all_to_all.40.recv_ref, bf16[32,128,256]{2,1,0:T(8,128)(2,1)S(1)} %get-tuple-element.47.grad_ref, bf16[32,128,256]{2,1,0:T(8,128)(2,1)} %copy-done.8, ...), custom_call_target="tpu_custom_call" | custom-call | tf_op jit(solution)/shard_map/backward/pallas_call | solution.py:652
  221.1 13.2 %all_to_all.41.recv_ref = bf16[16,64,128]{2,1,0:T(8,128)(2,1)S(1)} all-to-all(bf16[16,64,128]{2,1,0:T(8,128)(2,1)S(1)} %broadcast_in_dim.84), channel_id=1, replica_groups=mesh['groups'=2,'segment'=4,'space'=4] {'segment','space'}, dimensions={0} | all-to-all | bytes 524288 | tf_op jit(solution)/shard_map/all_to_all | solution.py:596
  234.3 9.1 %backward.5 = (bf16[32,128,256]{2,1,0:T(8,128)(2,1)}, f32[512,128]{1,0:T(8,128)S(1)}, f32[128,128]{1,0:T(8,128)S(1)}, bf16[64,128]{1,0:T(8,128)(2,1)}) custom-call(bf16[16,64,128]{2,1,0:T(8,128)(2,1)S(1)} %all_to_all.41.recv_ref, bf16[32,128,256]{2,1,0:T(8,128)(2,1)S(1)} %get-tuple-element.50.grad_ref, bf16[32,128,256]{2,1,0:T(8,128)(2,1)} %copy-done.7, ...), custom_call_target="tpu_custom_call" | custom-call | tf_op jit(solution)/shard_map/backward/pallas_call | solution.py:652
  243.4 5.3 %grads.1 = (f32[4,32,2,64,64]{4,3,2,1,0:T(8,128)}, f32[64,64]{1,0:T(8,128)}) custom-call(s32[1]{0:T(128)} %bitcast.seg_ref, f32[512,128]{1,0:T(8,128)S(1)} %get-tuple-element.32.y_ref.refs_0_, f32[512,128]{1,0:T(8,128)S(1)} %copy-done.16, f32[512,128]{1,0:T(8,128)S(1)} %copy-done.18, f32[512,128]{1,0:T(8,128)S(1)} %copy-done.20, ...), custom_call_target="tpu_custom_call" | custom-call | tf_op jit(solution)/shard_map/grads/pallas_call | solution.py:723
  (127 shorter events, 30.9 us)
Async XLA Ops:
  0.6 18.1 %copy-start = (bf16[2,8,8,256]{3,2,1,0:T(8,128)(2,1)S(1)}, bf16[2,8,8,256]{3,2,1,0:T(8,128)(2,1)}, u32[]{:S(2)}) copy-start(bf16[2,8,8,256]{3,2,1,0:T(8,128)(2,1)} %param.19) | copy-start | bytes 196612
  3.4 16.1 %copy-start.29 = (bf16[1,64,64]{2,1,0:T(8,128)(2,1)S(1)}, bf16[1,64,64]{2,1,0:T(8,128)(2,1)}, u32[]{:S(2)}) copy-start(bf16[1,64,64]{2,1,0:T(8,128)(2,1)} %param.23) | copy-start | bytes 24580
  3.4 16.2 %copy-start.32 = (f32[1,64]{1,0:T(1,128)S(1)}, f32[1,64]{1,0:T(1,128)}, u32[]{:S(2)}) copy-start(f32[1,64]{1,0:T(1,128)} %param.24) | copy-start | bytes 772
  4.5 22.0 %collective-permute-start.5 = (bf16[16,128,128]{2,1,0:T(8,128)(2,1)}, bf16[16,128,128]{2,1,0:T(8,128)(2,1)S(1)}, u32[]{:S(2)}, u32[]{:S(2)}) collective-permute-start(bf16[16,128,128]{2,1,0:T(8,128)(2,1)} %pad_maximum_fusion.2), channel_id=1, source_target_pairs={{4,8},{12,0},{5,9},{13,1},{6,10},{14,2},{7,11},{15,3},{20,24},{28,... | collective-permute-start | bytes 1572872 | tf_op jit(solution)/shard_map/ppermute | solution.py:562
  5.8 24.5 %collective-permute-start.2 = (bf16[16,128,128]{2,1,0:T(8,128)(2,1)}, bf16[16,128,128]{2,1,0:T(8,128)(2,1)}, u32[]{:S(2)}, u32[]{:S(2)}) collective-permute-start(bf16[16,128,128]{2,1,0:T(8,128)(2,1)} %pad_maximum_fusion.2), channel_id=1, source_target_pairs={{0,4},{8,12},{1,5},{9,13},{2,6},{10,14},{3,7},{11,15},{16,20},{24,... | collective-permute-start | bytes 1572872 | tf_op jit(solution)/shard_map/ppermute | solution.py:562
  7.1 20.7 %copy-start.33 = (f32[64]{0:T(128)S(1)}, f32[64]{0:T(128)}, u32[]{:S(2)}) copy-start(f32[64]{0:T(128)} %param.22) | copy-start | bytes 772
  7.1 20.9 %copy-start.30 = (bf16[8,64]{1,0:T(8,128)(2,1)S(1)}, bf16[8,64]{1,0:T(8,128)(2,1)}, u32[]{:S(2)}) copy-start(bf16[8,64]{1,0:T(8,128)(2,1)} %param.21) | copy-start | bytes 3076
  8.2 20.7 %collective-permute-start.4 = (bf16[16,128,128]{2,1,0:T(8,128)(2,1)}, bf16[16,128,128]{2,1,0:T(8,128)(2,1)S(1)}, u32[]{:S(2)}, u32[]{:S(2)}) collective-permute-start(bf16[16,128,128]{2,1,0:T(8,128)(2,1)} %pad_maximum_fusion.1), channel_id=1, source_target_pairs={{4,12},{12,4},{5,13},{13,5},{6,14},{14,6},{7,15},{15,7},{20,28},{2... | collective-permute-start | bytes 1572872 | tf_op jit(solution)/shard_map/ppermute | solution.py:562
  12.8 17.6 %collective-permute-start.1 = (bf16[16,128,128]{2,1,0:T(8,128)(2,1)}, bf16[16,128,128]{2,1,0:T(8,128)(2,1)}, u32[]{:S(2)}, u32[]{:S(2)}) collective-permute-start(bf16[16,128,128]{2,1,0:T(8,128)(2,1)} %pad_maximum_fusion.1), channel_id=1, source_target_pairs={{0,8},{8,0},{1,9},{9,1},{2,10},{10,2},{3,11},{11,3},{16,24},{24,16... | collective-permute-start | bytes 1572872 | tf_op jit(solution)/shard_map/ppermute | solution.py:562
  15.3 13.6 %collective-permute-start.3 = (bf16[16,128,128]{2,1,0:T(8,128)(2,1)}, bf16[16,128,128]{2,1,0:T(8,128)(2,1)S(1)}, u32[]{:S(2)}, u32[]{:S(2)}) collective-permute-start(bf16[16,128,128]{2,1,0:T(8,128)(2,1)} %pad_maximum_fusion), channel_id=1, source_target_pairs={{4,0},{12,8},{5,1},{13,9},{6,2},{14,10},{7,3},{15,11},{20,16},{28,... | collective-permute-start | bytes 1572872 | tf_op jit(solution)/shard_map/ppermute | solution.py:562
  20.5 20.4 %all-to-all-start = ((bf16[16,48,256]{2,1,0:T(8,128)(2,1)}), bf16[16,48,256]{2,1,0:T(8,128)(2,1)S(1)}, u32[]{:S(2)}, u32[]{:S(2)}) async-start(bf16[16,48,256]{2,1,0:T(8,128)(2,1)} %broadcast_in_dim.31), calls=%async_computation | async-start | bytes 786432 | tf_op jit(solution)/shard_map/all_to_all | solution.py:596
  26.5 12.5 %collective-permute-start = (bf16[16,128,128]{2,1,0:T(8,128)(2,1)}, bf16[16,128,128]{2,1,0:T(8,128)(2,1)}, u32[]{:S(2)}, u32[]{:S(2)}) collective-permute-start(bf16[16,128,128]{2,1,0:T(8,128)(2,1)} %pad_maximum_fusion), channel_id=1, source_target_pairs={{0,12},{8,4},{1,13},{9,5},{2,14},{10,6},{3,15},{11,7},{16,28},{24,... | collective-permute-start | bytes 1572872 | tf_op jit(solution)/shard_map/ppermute | solution.py:562
  29.0 10.1 %copy-start.25 = (bf16[16,128,128]{2,1,0:T(8,128)(2,1)}, bf16[16,128,128]{2,1,0:T(8,128)(2,1)S(1)}, u32[]{:S(2)}) copy-start(bf16[16,128,128]{2,1,0:T(8,128)(2,1)S(1)} %collective-permute-done.4) | copy-start | bytes 1572868
  29.8 9.3 %copy-start.27 = (bf16[16,128,128]{2,1,0:T(8,128)(2,1)S(1)}, bf16[16,128,128]{2,1,0:T(8,128)(2,1)}, u32[]{:S(2)}) copy-start(bf16[16,128,128]{2,1,0:T(8,128)(2,1)} %copy-done.26) | copy-start | bytes 1572868
  39.1 4.4 %copy-start.4 = (f32[64,64]{1,0:T(8,128)S(1)}, f32[64,64]{1,0:T(8,128)}, u32[]{:S(2)}) copy-start(f32[64,64]{1,0:T(8,128)} %constant.107.clone.xi_ref.xf_ref) | copy-start | bytes 49156
  39.1 4.4 %copy-start.13 = (f32[64,128]{1,0:T(8,128)S(1)}, f32[64,128]{1,0:T(8,128)}, u32[]{:S(2)}) copy-start(f32[64,128]{1,0:T(8,128)} %constant.105.clone.lx_ref) | copy-start | bytes 98308
  40.8 18.7 %copy-start.14 = (bf16[32,256]{1,0:T(8,128)(2,1)S(1)}, bf16[32,256]{1,0:T(8,128)(2,1)}, u32[]{:S(2)}) copy-start(bf16[32,256]{1,0:T(8,128)(2,1)} %constant.101.clone.inv_ref) | copy-start | bytes 49156
  45.1 14.4 %all-to-all-start.1 = ((bf16[16,64,128]{2,1,0:T(8,128)(2,1)}), bf16[16,64,128]{2,1,0:T(8,128)(2,1)S(1)}, u32[]{:S(2)}, u32[]{:S(2)}) async-start(bf16[16,64,128]{2,1,0:T(8,128)(2,1)} %broadcast_in_dim.33), calls=%async_computation.1 | async-start | bytes 524288 | tf_op jit(solution)/shard_map/all_to_all | solution.py:596
  73.7 13.4 %all-to-all-start.2 = ((bf16[16,64,128]{2,1,0:T(8,128)(2,1)}), bf16[16,64,128]{2,1,0:T(8,128)(2,1)S(1)}, u32[]{:S(2)}, u32[]{:S(2)}) async-start(bf16[16,64,128]{2,1,0:T(8,128)(2,1)} %broadcast_in_dim.34), calls=%async_computation.2 | async-start | bytes 524288 | tf_op jit(solution)/shard_map/all_to_all | solution.py:596
  101.3 13.4 %all-to-all-start.3 = ((bf16[16,64,128]{2,1,0:T(8,128)(2,1)}), bf16[16,64,128]{2,1,0:T(8,128)(2,1)S(1)}, u32[]{:S(2)}, u32[]{:S(2)}) async-start(bf16[16,64,128]{2,1,0:T(8,128)(2,1)} %broadcast_in_dim.35), calls=%async_computation.3 | async-start | bytes 524288 | tf_op jit(solution)/shard_map/all_to_all | solution.py:596
  105.8 27.6 %copy-start.34 = (bf16[128]{0:T(256)(128)(2,1)S(1)}, bf16[128]{0:T(256)(128)(2,1)}, u32[]{:S(2)}) copy-start(bf16[128]{0:T(256)(128)(2,1)} %param.28) | copy-start | bytes 772
  105.9 27.7 %copy-start.31 = (f32[128]{0:T(128)S(1)}, f32[128]{0:T(128)}, u32[]{:S(2)}) copy-start(f32[128]{0:T(128)} %param.27) | copy-start | bytes 1540
  105.9 27.8 %copy-start.24 = (bf16[64,128]{1,0:T(8,128)(2,1)S(1)}, bf16[64,128]{1,0:T(8,128)(2,1)}, u32[]{:S(2)}) copy-start(bf16[64,128]{1,0:T(8,128)(2,1)} %down_ref.1) | copy-start | bytes 49156
  114.7 27.6 %copy-start.12 = (f32[64,64]{1,0:T(8,128)S(1)}, f32[64,64]{1,0:T(8,128)}, u32[]{:S(2)}) copy-start(f32[64,64]{1,0:T(8,128)} %constant.106.clone.xa_ref.refs_12_.refs_13_) | copy-start | bytes 49156
  128.9 13.4 %all-to-all-start.4 = ((bf16[16,64,128]{2,1,0:T(8,128)(2,1)}), bf16[16,64,128]{2,1,0:T(8,128)(2,1)S(1)}, u32[]{:S(2)}, u32[]{:S(2)}) async-start(bf16[16,64,128]{2,1,0:T(8,128)(2,1)} %broadcast_in_dim.36), calls=%async_computation.4 | async-start | bytes 524288 | tf_op jit(solution)/shard_map/all_to_all | solution.py:596
  142.3 1.6 copy-start.6
  143.9 44.3 %copy-start.23 = (bf16[32,256]{1,0:T(8,128)(2,1)S(1)}, bf16[32,256]{1,0:T(8,128)(2,1)}, u32[]{:S(2)}) copy-start(bf16[32,256]{1,0:T(8,128)(2,1)} %constant.102.clone.fwd_ref) | copy-start | bytes 49156
  174.8 13.4 %all-to-all-start.5 = ((bf16[16,64,128]{2,1,0:T(8,128)(2,1)}), bf16[16,64,128]{2,1,0:T(8,128)(2,1)S(1)}, u32[]{:S(2)}, u32[]{:S(2)}) async-start(bf16[16,64,128]{2,1,0:T(8,128)(2,1)} %broadcast_in_dim.40), calls=%async_computation.5 | async-start | bytes 524288 | tf_op jit(solution)/shard_map/all_to_all | solution.py:596
  234.3 9.1 %copy-start.16 = (f32[512,128]{1,0:T(8,128)S(1)}, f32[512,128]{1,0:T(8,128)}, u32[]{:S(2)}) copy-start(f32[512,128]{1,0:T(8,128)} %copy-done.15) | copy-start | bytes 786436
  234.3 9.1 %copy-start.18 = (f32[512,128]{1,0:T(8,128)S(1)}, f32[512,128]{1,0:T(8,128)}, u32[]{:S(2)}) copy-start(f32[512,128]{1,0:T(8,128)} %copy-done.17) | copy-start | bytes 786436
  234.3 9.1 %copy-start.20 = (f32[512,128]{1,0:T(8,128)S(1)}, f32[512,128]{1,0:T(8,128)}, u32[]{:S(2)}) copy-start(f32[512,128]{1,0:T(8,128)} %copy-done.19) | copy-start | bytes 786436
  234.3 9.1 %copy-start.22 = (f32[512,128]{1,0:T(8,128)S(1)}, f32[512,128]{1,0:T(8,128)}, u32[]{:S(2)}) copy-start(f32[512,128]{1,0:T(8,128)} %copy-done.21) | copy-start | bytes 786436
  (15 other events, 16.8 us)

commit v2 on v1

--- a/solution.py
+++ b/solution.py
@@ -233,6 +233,8 @@
 
 f32, bf16 = (jnp.float32, jnp.bfloat16)
 NT = (((1,), (1,)), ((), ()))
+NN = (((1,), (0,)), ((), ()))
+STEPS = 2
 VMEM_LIMIT = 48 << 20
 
 
@@ -263,20 +265,14 @@
     return jnp.dot(a, b, precision=highest, preferred_element_type=f32)
 
 
-def split_rows(a):
-    hi = a.astype(bf16)
-    lo = (a - hi.astype(f32)).astype(bf16)
-    return jnp.concatenate([hi, lo], axis=0)
-
-
-def gelu_both(v, with_value=True):
+def gelu_both(v):
     k0 = math.sqrt(2.0 / math.pi)
     k1 = k0 * 0.044715
     v2 = v * v
-    t = jnp.tanh(v * (k0 + k1 * v2))
-    half = 0.5 * v
-    slope = (0.5 + 0.5 * t) + half * (1.0 - t * t) * (k0 + (3.0 * k1) * v2)
-    return (half + half * t if with_value else None, slope)
+    share = 0.5 + 0.5 * jnp.tanh(v * (k0 + k1 * v2))
+    value = v * share
+    slope = share + value * (1.0 - share) * (2.0 * k0 + (6.0 * k1) * v2)
+    return (value, slope)
 
 
 def low_half(shape):
@@ -287,58 +283,127 @@
     return pltpu.roll(a, a.shape[1] // 2, 1)
 
 
-def own_rows(y_ref, row, x_count):
-    return jnp.concatenate(
-        [y_ref[pl.ds(row + p, x_count, stride=16), :] for p in range(2)], axis=0
-    )
-
-
-def forward_modes(y_ref, w_ref, lx_ref, xi_ref, t_ref, m_ref, out_ref):
-    pairs, lanes = (w_ref.shape[0], w_ref.shape[2])
-    x_count = y_ref.shape[0] // 16
-    half = t_ref.shape[0] // 2
-    ys = own_rows(y_ref, 8, x_count)
+def cross(a, b):
+    low = low_half(a.shape)
+    return (jnp.where(low, a, swap_halves(b)), jnp.where(low, swap_halves(a), b))
+
+
+def grid_rows(first_ref, first, second_ref, second, x_half):
+    parts = []
+    for p in range(2):
+        parts += cross(
+            first_ref[pl.ds(first + p, x_half, stride=16), :],
+            second_ref[pl.ds(second + p, x_half, stride=16), :],
+        )
+    return jnp.concatenate(parts, axis=0)
+
+
+def own_grid(y_ref, row=8):
+    return grid_rows(y_ref, row, y_ref, row + 2, y_ref.shape[0] // 16)
+
+
+def put_chunk(grid, out_ref, first=0):
+    x_half = grid.shape[0] // 4
+    for p in range(2):
+        base = 2 * p * x_half
+        pair = cross(grid[base : base + x_half], grid[base + x_half : base + 2 * x_half])
+        for mode in range(2):
+            at = first + (2 * mode + p) * x_half
+            block = pair[mode].astype(bf16)
+            for k in range(out_ref.shape[0]):
+                out_ref[k, at : at + x_half] = block
+
+
+def put_split(t_ref, mode, rows):
+    count = rows.shape[0]
+    high = rows.astype(bf16).astype(f32)
+    t_ref[2 * mode * count : (2 * mode + 1) * count] = high
+    t_ref[(2 * mode + 1) * count : (2 * mode + 2) * count] = rows - high
+
+
+def mode_products(t_ref, w_ref, m_ref, dims, start=0):
+    pairs = w_ref.shape[1]
+    for j in range(pairs):
+        for mode in range(2):
+            at = pl.ds(mode * 8 * pairs + j, 8, stride=pairs)
+            m_ref[at, :] = lax.dot_general(
+                t_ref[at, :].astype(bf16), w_ref[start + mode, j], dims, preferred_element_type=f32
+            )
+    count = 4 * pairs
+    return [
+        m_ref[2 * mode * count : (2 * mode + 1) * count]
+        + m_ref[(2 * mode + 1) * count : (2 * mode + 2) * count]
+        for mode in range(2)
+    ]
+
+
+def first_kx(shape, pairs):
+    return (lax.broadcasted_iota(jnp.int32, shape, 0) // pairs) % 2 == 0
+
+
+def forward_modes(y_ref, w_ref, lx_ref, xi_ref, t_ref, m_ref, out_ref, row=8, start=0):
+    pairs = w_ref.shape[1]
+    ys = own_grid(y_ref, row)
     sw = swap_halves(ys)
     low = low_half(ys.shape)
     zero = jnp.zeros_like(ys)
-    rhs0 = jnp.concatenate([jnp.where(low, ys, zero), jnp.where(low, zero, sw)], axis=0)
-    rhs1 = jnp.concatenate([jnp.where(low, sw, zero), jnp.where(low, zero, ys)], axis=0)
-    t_ref[:half] = hdot(lx_ref[...], rhs0)
-    t_ref[half:] = hdot(lx_ref[...], rhs1)
-    for j in range(pairs):
-        rows = split_rows(t_ref[pl.ds(j, 8, stride=pairs), :])
-        prod = jnp.dot(rows, w_ref[j], preferred_element_type=f32)
-        m_ref[pl.ds(j, 8, stride=pairs), :] = prod[:8] + prod[8:]
-    m0, m1 = (m_ref[:half], m_ref[half:])
-    lowm = low_half(m0.shape)
-    first = (lax.broadcasted_iota(jnp.int32, m0.shape, 0) // pairs) % 2 == 0
+    put_split(t_ref, 0, hdot(lx_ref[...], jnp.concatenate([jnp.where(low, ys, zero), jnp.where(low, zero, sw)], axis=0)))
+    put_split(t_ref, 1, hdot(lx_ref[...], jnp.concatenate([jnp.where(low, sw, zero), jnp.where(low, zero, ys)], axis=0)))
+    m0, m1 = mode_products(t_ref, w_ref, m_ref, NN, start)
+    first = first_kx(m0.shape, pairs)
     s0 = jnp.where(first, m0, swap_halves(m0))
     s1 = jnp.where(first, swap_halves(m1), m1)
-    out_ref[...] = hdot(xi_ref[...], jnp.where(lowm, s0, s1)).astype(bf16)
+    first_row = start * out_ref.shape[1] // w_ref.shape[0]
+    put_chunk(hdot(xi_ref[...], jnp.where(low_half(m0.shape), s0, s1)), out_ref, first_row)
 
 
 def backward_modes(y_ref, w_ref, xa_ref, xf_ref, t_ref, m_ref, out_ref):
-    pairs = w_ref.shape[0]
-    x_count = y_ref.shape[0] // 16
-    half = t_ref.shape[0] // 2
-    g = hdot(xa_ref[...], own_rows(y_ref, 8, x_count))
+    pairs = w_ref.shape[1]
+    g = hdot(xa_ref[...], own_grid(y_ref))
     sw = swap_halves(g)
-    low = low_half(g.shape)
-    first = (lax.broadcasted_iota(jnp.int32, g.shape, 0) // pairs) % 2 == 0
-    keep = low == first
+    first = first_kx(g.shape, pairs)
+    keep = low_half(g.shape) == first
     zero = jnp.zeros_like(g)
-    t_ref[:half] = jnp.where(keep, jnp.where(first, g, sw), zero)
-    t_ref[half:] = jnp.where(keep, jnp.where(first, sw, g), zero)
-    for j in range(pairs):
-        rows = split_rows(t_ref[pl.ds(j, 8, stride=pairs), :])
-        prod = lax.dot_general(rows, w_ref[j], NT, preferred_element_type=f32)
-        m_ref[pl.ds(j, 8, stride=pairs), :] = prod[:8] + prod[8:]
-    quarter = half // 2
-    pr0, pi0, pr1, pi1 = (m_ref[i * quarter : (i + 1) * quarter] for i in range(4))
-    lowq = low_half(pr0.shape)
-    real = jnp.where(lowq, pr0 + swap_halves(pi0), swap_halves(pr1) + pi1)
-    imag = jnp.where(lowq, pi0 - swap_halves(pr0), swap_halves(pi1) - pr1)
-    out_ref[...] = hdot(xf_ref[...], jnp.concatenate([real, imag], axis=0)).astype(bf16)
+    put_split(t_ref, 0, jnp.where(keep, jnp.where(first, g, sw), zero))
+    put_split(t_ref, 1, jnp.where(keep, jnp.where(first, sw, g), zero))
+    m0, m1 = mode_products(t_ref, w_ref, m_ref, NT)
+    half = 2 * pairs
+    pr0, pi0, pr1, pi1 = (m0[:half], m0[half:], m1[:half], m1[half:])
+    low = low_half(pr0.shape)
+    real = jnp.where(low, pr0 + swap_halves(pi0), swap_halves(pr1) + pi1)
+    imag = jnp.where(low, pi0 - swap_halves(pr0), swap_halves(pi1) - pr1)
+    put_chunk(hdot(xf_ref[...], jnp.concatenate([real, imag], axis=0)), out_ref)
+
+
+def choose_kernel(seg_ref, layer, w_refs, w_ref, sem, start):
+    for seg in range(4):
+        pair = seg // 2
+        source = w_refs[(0 if seg % 2 == layer % 2 else 1) + (0 if pair == layer // 2 else 2)]
+        if pair == layer // 2:
+            source = source.at[2 * pair : 2 * pair + 2]
+
+        @pl.when(seg_ref[0] == seg)
+        def _(source=source):
+            copy = pltpu.make_async_copy(source, w_ref, sem)
+            if start:
+                copy.start()
+            else:
+                copy.wait()
+
+
+def choose_all(seg_ref, w_refs, w_ref, sem, start):
+    for lane in range(2):
+        @pl.when(seg_ref[0] % 2 == lane)
+        def _(lane=lane):
+            copy = pltpu.make_async_copy(w_refs[lane], w_ref, sem)
+            if start:
+                copy.start()
+            else:
+                copy.wait()
+
+
+def pack_kernel(in_ref, out_ref):
+    out_ref[...] = jnp.concatenate([in_ref[:, 0], in_ref[:, 1]], axis=-1)
 
 
 def widen(recv_ref, r_ref):
@@ -347,45 +412,56 @@
         r_ref[k * rows : (k + 1) * rows] = recv_ref[k].astype(f32)
 
 
-def row_product(weight, field, r_ref, table, x, x_count):
-    rows = r_ref[pl.ds(x, table.shape[0], stride=x_count), :]
+def row_product(weight, field, r_ref, table, x, x_half):
+    rows = r_ref[pl.ds(x, table.shape[0], stride=x_half), :]
     lhs = jnp.concatenate([weight, rows.T.astype(bf16)], axis=1)
     return jnp.dot(lhs, jnp.concatenate([field, table], axis=0), preferred_element_type=f32)
 
 
-def lift_kernel(in_ref, lw_ref, lb_ref, tab_ref, act_ref, y_ref, *, space, per_chunk, depth):
-    chunks = in_ref.shape[0]
-    for k in range(chunks):
-        base = (k % space) * (chunks // space) * per_chunk + (k // space) * per_chunk
-        for i in range(per_chunk):
-            cells = in_ref[k, i * depth : (i + 1) * depth, :]
-            act = jnp.dot(lw_ref[...], cells, preferred_element_type=f32) + lb_ref[...]
-            act = act.astype(bf16)
-            act_ref[base + i] = act
-            y_ref[(base + i) * 16 : (base + i + 1) * 16] = lax.dot_general(
-                tab_ref[...], act, NT, preferred_element_type=f32
-            )
-
-
-def first_modes_kernel(y_ref, w_ref, lx_ref, xi_ref, out_ref, t_ref, m_ref):
-    forward_modes(y_ref, w_ref, lx_ref, xi_ref, t_ref, m_ref, out_ref)
+def chunk_of(x, half_side, space, rows, per_chunk):
+    inner = x % rows
+    return ((inner // per_chunk) * space + half_side * (space // 2) + x // rows, inner % per_chunk)
+
+
+def lift_kernel(in_ref, lw_ref, lb_ref, tab_ref, act_ref, y_ref, *, space, rows, per_chunk, depth):
+    for x in range(act_ref.shape[0]):
+        cells = []
+        for side in range(2):
+            k, i = chunk_of(x, side, space, rows, per_chunk)
+            cells.append(in_ref[k, i * depth : (i + 1) * depth, :])
+        cells = jnp.concatenate(cells, axis=0)
+        act = jnp.dot(lw_ref[...], cells, preferred_element_type=f32) + lb_ref[...]
+        act = act.astype(bf16)
+        act_ref[x] = act
+        y_ref[x * 16 : (x + 1) * 16] = lax.dot_general(
+            tab_ref[...], act, NT, preferred_element_type=f32
+        )
+
+
+def first_modes_kernel(seg_ref, y_ref, lx_ref, xi_ref, w0, w1, out_ref, w_ref, sem, t_ref, m_ref):
+    choose_all(seg_ref, (w0, w1), w_ref, sem, True)
+    choose_all(seg_ref, (w0, w1), w_ref, sem, False)
+    for start in range(0, w_ref.shape[0], 2):
+        forward_modes(y_ref, w_ref, lx_ref, xi_ref, t_ref, m_ref, out_ref, 2 * start, start)
 
 
 def forward_kernel(
-    recv_ref, act_ref, pw_ref, pb_ref, inv_ref, tab_ref, w_ref, lx_ref, xi_ref,
-    next_ref, slope_ref, y_ref, out_ref, r_ref, t_ref, m_ref,
+    seg_ref, recv_ref, act_ref, pw_ref, pb_ref, inv_ref, tab_ref, lx_ref, xi_ref, w0, w1, w2, w3,
+    next_ref, slope_ref, y_ref, out_ref, w_ref, sem, t_ref, m_ref, r_ref, *, layer,
 ):
     step = pl.program_id(0)
     block = act_ref.shape[0]
-    x_count = y_ref.shape[0] // 16
+    x_half = y_ref.shape[0] // 16
 
     @pl.when(step == 0)
     def _():
+        choose_kernel(seg_ref, layer, (w0, w1, w2, w3), w_ref, sem, True)
         widen(recv_ref, r_ref)
 
     def one(i, carry):
         x = step * block + i
-        pre = row_product(pw_ref[...], act_ref[i], r_ref, inv_ref[...], x, x_count) + pb_ref[...]
+        pre = row_product(pw_ref[layer - 1], act_ref[i], r_ref, inv_ref[...], x, x_half)
+        pre = pre + pb_ref[layer - 1]
         value, slope = gelu_both(pre)
         value = value.astype(bf16)
         next_ref[i] = value
@@ -399,6 +475,7 @@
 
     @pl.when(step == pl.num_programs(0) - 1)
     def _():
+        choose_kernel(seg_ref, layer, (w0, w1, w2, w3), w_ref, sem, False)
         forward_modes(y_ref, w_ref, lx_ref, xi_ref, t_ref, m_ref, out_ref)
 
 
@@ -413,42 +490,45 @@
 
 
 def top_kernel(
-    recv_ref, act_ref, in_ref, pw_ref, pb_ref, inv_ref, up_ref, hb_ref, down_ref, ow_ref, tab_ref,
-    w_ref, xa_ref, xf_ref,
-    pre_ref, y_ref, point_ref, out_ref, r_ref, t_ref, m_ref, *, space, per_chunk, first_row, batch,
+    seg_ref, recv_ref, act_ref, in_ref, pw_ref, pb_ref, inv_ref, up_ref, hb_ref, down_ref, ow_ref,
+    tab_ref, xa_ref, xf_ref, w0, w1, w2, w3,
+    pre_ref, y_ref, point_ref, out_ref, w_ref, sem, t_ref, m_ref, r_ref,
+    *, layer, space, rows, per_chunk, first_row,
 ):
     step = pl.program_id(0)
     block = act_ref.shape[0]
-    x_count = y_ref.shape[0] // 16
-    parts = in_ref.shape[0] // space
+    x_half = y_ref.shape[0] // 16
 
     @pl.when(step == 0)
     def _():
+        choose_kernel(seg_ref, layer, (w0, w1, w2, w3), w_ref, sem, True)
         widen(recv_ref, r_ref)
         point_ref[...] = jnp.zeros_like(point_ref)
 
     def one(i, carry):
         x = step * block + i
         act = act_ref[i]
-        pre = row_product(pw_ref[...], act, r_ref, inv_ref[...], x, x_count) + pb_ref[...]
+        pre = row_product(pw_ref[layer], act, r_ref, inv_ref[...], x, x_half) + pb_ref[layer]
         value, slope = gelu_both(pre)
         value = value.astype(bf16)
-        pair = x // per_chunk
-        chunk = (pair % parts) * space + pair // parts
-        within = x % per_chunk
-        cots = in_ref[chunk, first_row : first_row + per_chunk * batch, :].astype(f32)
         grads = []
-        size = value.shape[0] // batch
-        for b in range(batch):
-            hidden = jnp.dot(up_ref[...], value[b * size : (b + 1) * size], preferred_element_type=f32)
-            _, hidden_slope = gelu_both(hidden + hb_ref[...], False)
-            cot = cots[b : b + 1]
+        size = value.shape[0] // 2
+        for side in range(2):
+            hidden = jnp.dot(
+                up_ref[...], value[side * size : (side + 1) * size], preferred_element_type=f32
+            )
+            _, hidden_slope = gelu_both(hidden + hb_ref[...])
+            chunk, within = chunk_of(x, side, space, rows, per_chunk)
+            cots = in_ref[chunk, first_row : first_row + per_chunk, :].astype(f32)
+            cot = cots[:1]
             for other in range(1, per_chunk):
-                row = other * batch + b
-                cot = jnp.where(within == other, cots[row : row + 1], cot)
-            hidden_grad = (hidden_slope * (ow_ref[...] * cot)).astype(bf16)
-            grads.append(jnp.dot(down_ref[...], hidden_grad, preferred_element_type=f32))
-        grad = jnp.concatenate(grads, axis=0).astype(bf16).astype(f32)
+                cot = jnp.where(within == other, cots[other : other + 1], cot)
+            grads.append(
+                cot * jnp.dot(
+                    down_ref[...], (hidden_slope * ow_ref[...]).astype(bf16), preferred_element_type=f32
+                )
+            )
+        grad = jnp.concatenate(grads, axis=0)
         adjoint_rows(x, i, grad * slope, act, tab_ref, pre_ref, y_ref, point_ref)
         return carry
 
@@ -456,62 +536,77 @@
 
     @pl.when(step == pl.num_programs(0) - 1)
     def _():
+        choose_kernel(seg_ref, layer, (w0, w1, w2, w3), w_ref, sem, False)
         backward_modes(y_ref, w_ref, xa_ref, xf_ref, t_ref, m_ref, out_ref)
 
 
 def backward_kernel(
-    recv_ref, grad_ref, slope_ref, act_ref, pw_ref, fwd_ref, tab_ref, w_ref, xa_ref, xf_ref,
-    pre_ref, y_ref, point_ref, out_ref, r_ref, t_ref, m_ref, *, send,
+    seg_ref, recv_ref, grad_ref, slope_ref, act_ref, pw_ref, fwd_ref, tab_ref, xa_ref, xf_ref,
+    w0, w1, w2, w3,
+    pre_ref, y_ref, point_ref, out_ref, w_ref, sem, t_ref, m_ref, r_ref, *, layer,
 ):
     step = pl.program_id(0)
     block = act_ref.shape[0]
-    x_count = y_ref.shape[0] // 16
+    x_half = y_ref.shape[0] // 16
 
     @pl.when(step == 0)
     def _():
+        if layer:
+            choose_kernel(seg_ref, layer, (w0, w1, w2, w3), w_ref, sem, True)
         widen(recv_ref, r_ref)
         point_ref[...] = jnp.zeros_like(point_ref)
 
     def one(i, carry):
         x = step * block + i
-        grad = row_product(pw_ref[...], grad_ref[i], r_ref, fwd_ref[...], x, x_count)
-        grad = grad.astype(bf16).astype(f32) * slope_ref[i].astype(f32)
-        adjoint_rows(x, i, grad, act_ref[i], tab_ref, pre_ref, y_ref, point_ref)
+        grad = row_product(pw_ref[layer + 1], grad_ref[i], r_ref, fwd_ref[...], x, x_half)
+        adjoint_rows(
+            x, i, grad * slope_ref[i].astype(f32), act_ref[i], tab_ref, pre_ref, y_ref, point_ref
+        )
         return carry
 
     lax.fori_loop(0, block, one, 0, unroll=2)
 
     @pl.when(step == pl.num_programs(0) - 1)
     def _():
-        if send:
+        if layer:
+            choose_kernel(seg_ref, layer, (w0, w1, w2, w3), w_ref, sem, False)
             backward_modes(y_ref, w_ref, xa_ref, xf_ref, t_ref, m_ref, out_ref)
         else:
             out_ref[...] = jnp.zeros_like(out_ref)
 
 
-def grads_kernel(seg_ref, *refs, layers, scale):
+def pick_kernel(seg_ref, *refs, layers):
     ya_refs, yg_refs, pg_refs = (refs[:layers], refs[layers : 2 * layers], refs[2 * layers : 3 * layers])
-    xz_ref, xa_ref, out_ref, point_ref, ya, yg, a_ref, b_ref = refs[3 * layers :]
+    count = ya_refs[0].shape[0]
+    seg = seg_ref[0]
+    partner = seg + 1 - 2 * (seg % 2)
+    for out_ref, wanted in zip(refs[3 * layers :], (seg, partner)):
+        for layer in range(layers):
+            @pl.when(wanted == layer)
+            def _(layer=layer, out_ref=out_ref):
+                out_ref[:count] = ya_refs[layer][...]
+                out_ref[count : 2 * count] = yg_refs[layer][...]
+                pg = pg_refs[layer][...]
+                half = pg.shape[0] // 2
+                out_ref[2 * count :] = pg[:half] + swap_halves(pg[half:])
+
+
+def grads_kernel(mine_ref, theirs_ref, xz_ref, xa_ref, out_ref, point_ref, a_ref, b_ref, *, scale):
     mode = pl.program_id(0)
-    x_count = ya.shape[0] // 16
+    c = point_ref.shape[0]
+    count = (mine_ref.shape[0] - c) // 2
+    x_half = count // 16
 
     @pl.when(mode == 0)
     def _():
-        for layer in range(layers):
-            @pl.when(seg_ref[0] == layer)
-            def _():
-                ya[...] = ya_refs[layer][...]
-                yg[...] = yg_refs[layer][...]
-                pg = pg_refs[layer][...]
-                c = point_ref.shape[0]
-                point_ref[...] = (pg[:c, :c] + pg[c:, c:]) * scale
-
-    z = hdot(xz_ref[...], own_rows(ya, 2 * mode, x_count))
-    g = hdot(xa_ref[...], own_rows(yg, 2 * mode, x_count))
+        point_ref[...] = (mine_ref[2 * count :, :c] + theirs_ref[2 * count :, :c]) * scale
+
+    z = hdot(xz_ref[...], grid_rows(mine_ref, 2 * mode, theirs_ref, 2 * mode, x_half))
+    at = count + 2 * mode
+    g = hdot(xa_ref[...], grid_rows(mine_ref, at, theirs_ref, at, x_half))
     rows = z.shape[0]
     kx = rows // 2
     zs, gs = (swap_halves(z), swap_halves(g))
-    c = z.shape[1] // 2
     a_ref[:rows] = z
     a_ref[rows:] = zs
     low = low_half((kx, z.shape[1]))
@@ -522,11 +617,9 @@
     for j in range(kx):
         a = a_ref[pl.ds(j, 4, stride=kx), :][:, :c]
         b = b_ref[pl.ds(j, 4, stride=kx), :]
-        ah, bh = (a.astype(bf16), b.astype(bf16))
-        al, bl = ((a - ah.astype(f32)).astype(bf16), (b - bh.astype(f32)).astype(bf16))
-        left = jnp.concatenate([ah.astype(f32), al.astype(f32), ah.astype(f32)], axis=0)
-        right = jnp.concatenate([bh.astype(f32), bh.astype(f32), bl.astype(f32)], axis=0).astype(bf16)
-        left = left.T.astype(bf16)
+        ah, bh = (a.astype(bf16).astype(f32), b.astype(bf16).astype(f32))
+        left = jnp.concatenate([ah, a - ah, ah], axis=0).T.astype(bf16)
+        right = jnp.concatenate([bh, bh, b - bh], axis=0).astype(bf16)
         out_ref[0, j, 0] = jnp.dot(left, right[:, :c], preferred_element_type=f32)
         out_ref[0, j, 1] = jnp.dot(left, right[:, c:], preferred_element_type=f32)
 
@@ -538,46 +631,35 @@
     batch, row_count, depth, cols = inputs.shape
     segments, space = (lax.axis_size("segment"), lax.axis_size("space"))
     seg, place = (lax.axis_index("segment"), lax.axis_index("space"))
+    pair = seg // 2
     both = ("segment", "space")
-    chunks = segments * space
     owned, kx = spectral_weight.shape[1:3]
     c = point_weight.shape[1]
-    bc = batch * c
     x_count = row_count * space
+    x_half = x_count // 2
     mode_count = owned * space
     per_chunk = row_count // segments
     pairs = kx // 2
+    group = segments // 2 * space
 
     stack = spectral_weight[0].reshape(owned, 2, pairs, 2 * c, c)
-    packed = [
-        jnp.concatenate([w[0], w[1]], axis=-1)
-        for w in (
-            lax.dynamic_index_in_dim(stack, (seg + d) % segments, 0, keepdims=False)
-            for d in range(segments)
-        )
-    ]
-    moved = []
-    for parity in range(2):
-        moved.append([
-            lax.ppermute(
-                packed[d], "segment",
-                [(i, (i + d) % segments) for i in range(parity, segments, 2)],
-            )
-            for d in range(1, segments)
-        ])
-
-    def layer_kernel(layer):
-        options = [packed[0]] + moved[layer % 2]
-        result = options[0]
-        shift = (seg - layer) % segments
-        for d in range(1, segments):
-            result = jnp.where(shift == d, options[d], result)
-        return result
+    own = pl.pallas_call(
+        pack_kernel,
+        grid=(owned,),
+        in_specs=[pl.BlockSpec((1, 2, pairs, 2 * c, c), lambda m: (m, 0, 0, 0, 0))],
+        out_specs=pl.BlockSpec((1, pairs, 2 * c, 2 * c), lambda m: (m, 0, 0, 0)),
+        out_shape=jax.ShapeDtypeStruct((owned, pairs, 2 * c, 2 * c), bf16),
+        compiler_params=pltpu.CompilerParams(vmem_limit_bytes=VMEM_LIMIT),
+        name="pack",
+    )(stack)
+    swap = [(0, 1), (1, 0), (2, 3), (3, 2)]
+    neighbour = lax.ppermute(own, "segment", swap)
+    away = lax.dynamic_slice_in_dim(own, 2 * (1 - pair), 2, 0)
+    across_odd = lax.ppermute(away, "segment", [(1, 3), (3, 1)])
 
     cells = lax.dynamic_slice_in_dim(inputs, seg * per_chunk, per_chunk, 1)
-    cells = jnp.transpose(cells, (1, 0, 2, 3)).reshape(per_chunk * batch * depth, cols)
+    cells = cells.reshape(batch, per_chunk * depth, cols)
     cots = lax.dynamic_slice_in_dim(cotangent, seg * per_chunk, per_chunk, 1)
-    cots = jnp.transpose(cots, (1, 0, 2)).reshape(per_chunk * batch, cols)
     weight_rows = c * c // space // cols
     share = lax.dynamic_index_in_dim(
         point_weight.reshape(space, weight_rows, cols), place, 0, keepdims=False
@@ -586,18 +668,23 @@
     mid = lax.reduce_precision(layer_bias[0] - high, 8, 7)
     rest = layer_bias[0] - high - mid
     bias_row = jnp.concatenate([high, mid, rest, jnp.zeros((cols - 3 * c,), f32)]).astype(bf16)
-    chunk = jnp.concatenate([cells, cots, share, bias_row[None]], axis=0)
-    cot_row = per_chunk * batch * depth
-    share_row = cot_row + per_chunk * batch
+    common = jnp.concatenate([share, bias_row[None]], axis=0)
+    chunk = jnp.concatenate([cells, cots, jnp.broadcast_to(common[None], (batch,) + common.shape)], axis=1)
+    cot_row = per_chunk * depth
+    share_row = cot_row + per_chunk
     bias_at = share_row + weight_rows
-    chunk = jnp.pad(chunk, ((0, -chunk.shape[0] % 16), (0, 0)))
-
-    def to_all(block):
-        return lax.all_to_all(
-            jnp.broadcast_to(block[None], (chunks,) + block.shape), both, 0, 0, tiled=True
-        )
-
-    grid_in = to_all(chunk)
+    chunk = jnp.pad(chunk, ((0, 0), (0, -chunk.shape[1] % 8), (0, 0)))
+    chunk = jnp.broadcast_to(chunk[None, :, None], (segments // 2, batch, space) + chunk.shape[1:])
+    grid_in = lax.all_to_all(
+        chunk.reshape((segments * space,) + chunk.shape[3:]), both, 0, 0, tiled=True
+    )
+    across_odd_on = lax.ppermute(across_odd, "segment", [(1, 0), (3, 2)])
+
+    def weights_of(layer):
+        if layer % 2:
+            return (own, neighbour, across_odd, across_odd_on)
+        return (own, neighbour, across_even, across_even_on)
+
     points = grid_in[:, share_row:bias_at].reshape(segments, c, c)
     bias_parts = grid_in[::space, bias_at, : 3 * c].astype(f32).reshape(segments, 3, c)
     biases = bias_parts[:, 0] + bias_parts[:, 1] + bias_parts[:, 2]
@@ -610,23 +697,24 @@
 
     point_back = doubled(points)
     point_fwd = doubled(jnp.transpose(points, (0, 2, 1)))
-    bias_cols = jnp.concatenate([biases] * batch, axis=1)[:, :, None]
+    bias_cols = jnp.concatenate([biases] * 2, axis=1)[:, :, None]
 
     y_forward, y_inverse = np_y_tables(cols, mode_count)
     x_forward, x_inverse = np_x_tables(x_count, kx // 2)
-    order = [(k % space) * owned + k // space for k in range(chunks)]
+    firsts = [k % space * owned + k // space * 2 for k in range(group)]
+    order = [first + i for first in firsts for i in range(2)]
 
     def gathered(table):
-        return jnp.asarray(table[order].reshape(2 * chunks, cols), bf16)
+        return jnp.asarray(table[order].reshape(4 * group, cols), bf16)
 
     def analysis(table):
-        full = np.zeros((chunks, 16, cols))
-        for k in range(chunks):
+        full = np.zeros((group, 16, cols))
+        for k in range(group):
             s = k % space
             full[k, : 2 * owned] = table[s * owned : (s + 1) * owned].reshape(2 * owned, cols)
-            full[k, 8:10] = table[order[k]]
+            full[k, 8:12] = table[firsts[k] : firsts[k] + 2].reshape(4, cols)
         return lax.dynamic_index_in_dim(
-            jnp.asarray(full, bf16), seg * space + place, 0, keepdims=False
+            jnp.asarray(full, bf16), pair * space + place, 0, keepdims=False
         )
 
     inv_table, fwd_table = (gathered(y_inverse), gathered(y_forward))
@@ -639,91 +727,131 @@
     xi = x_inverse.transpose(1, 0, 3, 2).reshape(2 * x_count, 2 * kx)
     lx, xz, xi, xa, xb = (jnp.asarray(t, f32) for t in (lx, xz, xi, xi.T.copy(), xz.T.copy()))
 
+    device_lists = [
+        [(2 * k + lane) * space + s for k in range(segments // 2) for s in range(space)]
+        for lane in range(2)
+    ]
+
+    def to_all(block):
+        return lax.all_to_all(block, both, 0, 0, tiled=True, axis_index_groups=device_lists)
+
     def whole(array):
         rank = len(array.shape)
         return pl.BlockSpec(array.shape, lambda *i: (0,) * rank)
 
-    def call(kernel, args, blocked, outs, scratch, steps, name):
+    seg_scalar = seg.astype(jnp.int32).reshape(1)
+
+    def call(kernel, args, blocked, weights, outs, scratch, steps, name):
         def spec(array, is_blocked):
             if is_blocked:
                 return pl.BlockSpec((array.shape[0] // steps,) + array.shape[1:], lambda i: (i, 0, 0))
+            if array.shape == sent_first.shape and steps > 1:
+                return pl.BlockSpec((space,) + array.shape[1:], lambda i: (0, 0, 0))
             return whole(array)
 
         return pl.pallas_call(
             kernel,
             grid=(steps,),
-            in_specs=[spec(a, n in blocked) for n, a in enumerate(args)],
+            in_specs=[pl.BlockSpec(memory_space=pltpu.SMEM)]
+            + [spec(a, n in blocked) for n, a in enumerate(args)]
+            + [pl.BlockSpec(memory_space=pl.ANY)] * len(weights),
             out_specs=[spec(a, is_blocked) for a, is_blocked in outs],
             out_shape=[a for a, _ in outs],
             scratch_shapes=scratch,
             compiler_params=pltpu.CompilerParams(vmem_limit_bytes=VMEM_LIMIT),
             name=name,
-        )(*args)
-
-    field = jax.ShapeDtypeStruct((x_count, bc, cols), bf16)
-    ycoef = jax.ShapeDtypeStruct((x_count * 16, bc), f32)
-    sent = jax.ShapeDtypeStruct((2 * x_count, bc), bf16)
-    point = jax.ShapeDtypeStruct((bc, bc), f32)
-    mode_scratch = [pltpu.VMEM((2 * batch * kx, 2 * c), f32)] * 2
-    row_scratch = [pltpu.VMEM((chunks * 2 * x_count, bc), f32)]
-    steps = 4
+        )(seg_scalar, *args, *weights)
+
+    lanes = 2 * c
+    field = jax.ShapeDtypeStruct((x_half, lanes, cols), bf16)
+    ycoef = jax.ShapeDtypeStruct((x_half * 16, lanes), f32)
+    sent = jax.ShapeDtypeStruct((group, 2 * x_count, lanes), bf16)
+    sent_first = jax.ShapeDtypeStruct((group, 4 * x_count, lanes), bf16)
+    point = jax.ShapeDtypeStruct((lanes, lanes), f32)
+    mode_scratch = [
+        pltpu.VMEM((2,) + own.shape[1:], bf16), pltpu.SemaphoreType.DMA(()),
+        pltpu.VMEM((8 * kx, lanes), f32), pltpu.VMEM((8 * kx, lanes), f32),
+    ]
+    row_scratch = [pltpu.VMEM((group * 2 * x_count, lanes), f32)]
 
     zero = jnp.zeros_like(lift_weight.T)
     lift = jnp.concatenate(
         [jnp.concatenate([lift_weight.T, zero], 1), jnp.concatenate([zero, lift_weight.T], 1)], 0
     )
-    lift_col = jnp.concatenate([lift_bias] * batch)[:, None]
-    act, y0 = call(
-        partial(lift_kernel, space=space, per_chunk=per_chunk, depth=batch * depth),
-        (grid_in, lift, lift_col, act_table), (), [(field, False), (ycoef, False)], [], 1, "lift",
-    )
+    lift_col = jnp.concatenate([lift_bias] * 2)[:, None]
+    where = dict(space=space, rows=row_count, per_chunk=per_chunk)
+    act, y0 = pl.pallas_call(
+        partial(lift_kernel, depth=depth, **where),
+        out_shape=[field, ycoef],
+        compiler_params=pltpu.CompilerParams(vmem_limit_bytes=VMEM_LIMIT),
+        name="lift",
+    )(grid_in, lift, lift_col, act_table)
     acts, slopes, ya = ([act], [], [y0])
-    kernels = [layer_kernel(layer) for layer in range(segments)]
     (mine,) = call(
-        first_modes_kernel, (y0, kernels[0], lx, xi), (), [(sent, False)], mode_scratch, 1, "modes"
+        first_modes_kernel, (y0, lx, xi), (), (own, neighbour), [(sent_first, False)],
+        [pltpu.VMEM(own.shape, bf16)] + mode_scratch[1:], 1, "modes",
+    )
+    across_even = lax.ppermute(
+        lax.optimization_barrier((away, mine))[0], "segment", [(2, 0)]
     )
     for layer in range(1, segments):
         recv = to_all(mine)
+        table = inv_table
+        if layer == 1:
+            table = jnp.asarray(y_inverse.reshape(2 * mode_count, cols), bf16)
         act, slope, y, mine = call(
-            forward_kernel,
-            (recv, acts[-1], point_fwd[layer - 1], bias_cols[layer - 1], inv_table, act_table,
-             kernels[layer], lx, xi),
-            (1,), [(field, True), (field, True), (ycoef, False), (sent, False)],
-            row_scratch + mode_scratch, steps, "forward",
+            partial(forward_kernel, layer=layer),
+            (recv, acts[-1], point_fwd, bias_cols, table, act_table, lx, xi),
+            (1,), weights_of(layer), [(field, True), (field, True), (ycoef, False), (sent, False)],
+            mode_scratch + row_scratch, STEPS, "forward",
         )
         acts.append(act)
         slopes.append(slope)
         ya.append(y)
+        if layer == 1:
+            across_even_on = lax.ppermute(
+                lax.optimization_barrier((across_even, mine))[0], "segment", [(0, 1)]
+            )
 
     recv = to_all(mine)
     last = segments - 1
     pre_grad, y, pg, mine = call(
-        partial(top_kernel, space=space, per_chunk=per_chunk, first_row=cot_row, batch=batch),
-        (recv, acts[last], grid_in, point_fwd[last], bias_cols[last], inv_table,
+        partial(top_kernel, layer=last, first_row=cot_row, **where),
+        (recv, acts[last], grid_in, point_fwd, bias_cols, inv_table,
          proj_weight.T, proj_bias[:, None], proj_weight, out_weight.astype(f32)[:, None],
-         grad_table, kernels[last], xa, xb),
-        (1,), [(field, True), (ycoef, False), (point, False), (sent, False)],
-        row_scratch + mode_scratch, steps, "top",
+         grad_table, xa, xb),
+        (1,), weights_of(last), [(field, True), (ycoef, False), (point, False), (sent, False)],
+        mode_scratch + row_scratch, STEPS, "top",
     )
     yg, pgs = ([y], [pg])
     for layer in reversed(range(last)):
         recv = to_all(mine)
         pre_grad, y, pg, mine = call(
-            partial(backward_kernel, send=layer > 0),
-            (recv, pre_grad, slopes[layer], acts[layer], point_back[layer + 1], fwd_table,
-             grad_table, kernels[layer], xa, xb),
-            (1, 2, 3), [(field, True), (ycoef, False), (point, False), (sent, False)],
-            row_scratch + mode_scratch, steps, "backward",
+            partial(backward_kernel, layer=layer),
+            (recv, pre_grad, slopes[layer], acts[layer], point_back, fwd_table,
+             grad_table, xa, xb),
+            (1, 2, 3), weights_of(layer),
+            [(field, True), (ycoef, False), (point, False), (sent, False)],
+            mode_scratch + row_scratch, STEPS, "backward",
         )
         yg.insert(0, y)
         pgs.insert(0, pg)
 
-    scale = 1.0 / math.sqrt(batch * x_count * cols)
-    pieces = ya + yg + pgs + [xz, xa]
+    pieces = ya + yg + pgs
+    summary = jax.ShapeDtypeStruct((2 * x_half * 16 + c, lanes), f32)
+    mine, theirs = pl.pallas_call(
+        partial(pick_kernel, layers=segments),
+        in_specs=[pl.BlockSpec(memory_space=pltpu.SMEM)] + [pl.BlockSpec()] * len(pieces),
+        out_shape=[summary, summary],
+        compiler_params=pltpu.CompilerParams(vmem_limit_bytes=VMEM_LIMIT),
+        name="pick",
+    )(seg_scalar, *pieces)
+    theirs = lax.ppermute(theirs, "segment", [(0, 1), (1, 0), (2, 3), (3, 2)])
+    pieces = [mine, theirs, xz, xa]
     spectral, point_out = pl.pallas_call(
-        partial(grads_kernel, layers=segments, scale=scale),
+        partial(grads_kernel, scale=1.0 / math.sqrt(batch * x_count * cols)),
         grid=(owned,),
-        in_specs=[pl.BlockSpec(memory_space=pltpu.SMEM)] + [whole(a) for a in pieces],
+        in_specs=[whole(a) for a in pieces],
         out_specs=[
             pl.BlockSpec((1, kx, 2, c, c), lambda m: (m, 0, 0, 0, 0)),
             pl.BlockSpec((c, c), lambda m: (0, 0)),
@@ -732,11 +860,10 @@
             jax.ShapeDtypeStruct((owned, kx, 2, c, c), f32),
             jax.ShapeDtypeStruct((c, c), f32),
         ],
-        scratch_shapes=[pltpu.VMEM((x_count * 16, bc), f32)] * 2
-        + [pltpu.VMEM((2 * batch * kx, bc), f32)] * 2,
+        scratch_shapes=[pltpu.VMEM((4 * kx, lanes), f32)] * 2,
         compiler_params=pltpu.CompilerParams(vmem_limit_bytes=VMEM_LIMIT),
         name="grads",
-    )(seg.astype(jnp.int32).reshape(1), *pieces)
+    )(*pieces)
     return (spectral[None], point_out[None])
 
 
@@ -748,17 +875,15 @@
     modes, kx = spectral_weight.shape[1:3]
     return (
         batch == 2
-        and batch * c == 128
-        and layers == segments
-        and segments * space <= 16
-        and modes == segments * space
-        and modes // space <= 4
+        and 2 * c == 128
+        and layers == segments == 4
+        and modes == 4 * space
+        and space in (2, 4)
         and rows % (segments * space) == 0
         and rows % 32 == 0
         and rows <= 64
-        and kx % 16 == 0
-        and kx <= 64
-        and batch * depth == 16
+        and kx == 32
+        and depth == 8
         and cols % 128 == 0
         and cols >= 3 * c
         and c * c % (space * cols) == 0

time: 252 us -> 179 us (0.71)
  Pallas kernels: 92.4 us -> 57.8 us
  waiting for transfers between devices: 48.9 us -> 24.6 us
  local copies, waits for them, and re-layouts: 29.7 us -> 17.8 us
  blocking collectives: 26.4 us -> 35.6 us
  other arithmetic: 7.02 us -> 0.55 us
  starting transfers between devices: 43.1 us -> 38.4 us
    pallas_call x10 -> x12, Pallas kernels: 92.4 us -> 57.8 us  [the longest x8 47.9 us: call(): pl.pallas_call(kernel, grid=(steps,), in_specs=[pl.BlockSpec(memory_space...]
    all_to_all x6 -> x4, waiting for transfers between devices: 40.2 us -> 23.3 us  [the longest x3 16.9 us: to_all(): lax.all_to_all(block, both, 0, 0, tiled=True, axis_index_groups=device_li...]
    all_to_all x2 -> x4, blocking collectives: 26.4 us -> 35.6 us  [to_all(): lax.all_to_all(block, both, 0, 0, tiled=True, axis_index_groups=device_li...]
    all_to_all x6 -> x4, starting transfers between devices: 29.9 us -> 21.5 us  [the longest x3 15.2 us: to_all(): lax.all_to_all(block, both, 0, 0, tiled=True, axis_index_groups=device_li...]
    ppermute x6, waiting for transfers between devices: 8.7 us -> 1.22 us  [the longest x1 1.21 us: replicated(): theirs = lax.ppermute(theirs, 'segment', [(0, 1), (1, 0), (2, 3), (3, 2)])]
    unnamed x72 -> x95, local copies, waits for them, and re-layouts: 18.5 us -> 12.2 us
    broadcast_in_dim x9 -> x4, local copies, waits for them, and re-layouts: 4.81 us -> 0.95 us  [the longest x1 0.69 us: replicated(): jnp.broadcast_to(chunk[None, :, None], (segments // 2, batch, space) + ch...]
    ppermute x6, starting transfers between devices: 13.2 us -> 16.9 us  [the longest x1 8.61 us: replicated(): theirs = lax.ppermute(theirs, 'segment', [(0, 1), (1, 0), (2, 3), (3, 2)])]
  transfers between devices with their start and end apart: 12 -> 10, of which waited for: 6 -> 5; matrix products, arithmetic and copies ran while one was open for 4% -> 4% of each run, Pallas kernels for 0% -> 5%
where the time goes in v2:
time: 179 us; the launch traced here: 176 us
  Pallas kernels  57.8 us (32%)
  starting transfers between devices  38.4 us (21%)
  blocking collectives  35.6 us (20%)
  waiting for transfers between devices  24.6 us (14%)
  local copies, waits for them, and re-layouts  17.8 us (10%)
    pallas_call x8, Pallas kernels, call(): pl.pallas_call(kernel, grid=(steps,), in_specs=[pl.BlockSpec(memory_space...  47.9 us
    all_to_all x4, blocking collectives, to_all(): lax.all_to_all(block, both, 0, 0, tiled=True, axis_index_groups=device_li...  35.6 us
    all_to_all x3, waiting for transfers between devices, to_all(): lax.all_to_all(block, both, 0, 0, tiled=True, axis_index_groups=device_li...  16.9 us
    all_to_all x3, starting transfers between devices, to_all(): lax.all_to_all(block, both, 0, 0, tiled=True, axis_index_groups=device_li...  15.2 us
    unnamed x95, local copies, waits for them, and re-layouts  12.2 us
    ppermute x1, starting transfers between devices, replicated(): theirs = lax.ppermute(theirs, 'segment', [(0, 1), (1, 0), (2, 3), (3, 2)])  8.61 us
    all_to_all x1, waiting for transfers between devices, replicated(): lax.all_to_all(chunk.reshape((segments * space,) + chunk.shape[3:]), both...  6.41 us
    all_to_all x1, starting transfers between devices, replicated(): lax.all_to_all(chunk.reshape((segments * space,) + chunk.shape[3:]), both...  6.35 us
  transfers between devices with their start and end apart: 10, of which 5 were waited for; matrix products, arithmetic and copies ran while one was open for 4% of the time, Pallas kernels for 5%

profile of v2, /device:TPU:3, one launch (start us, length us, event | category | flops | bytes accessed | tf_op | source)
XLA Modules:
  0.0 175.7 jit_solution(10448273746096536957)
XLA Ops:
  0.6 3.3 %pack.1.w0 = bf16[4,16,128,128]{3,2,1,0:T(8,128)(2,1)S(1)} custom-call(bf16[4,2,16,128,64]{4,3,2,1,0:T(8,128)(2,1)} %bitcast.26), custom_call_target="tpu_custom_call" | custom-call | tf_op jit(solution)/shard_map/pack/pallas_call | solution.py:646
  4.8 1.1 constant_dynamic-slice_fusion
  5.8 1.9 %collective-permute-start.1 = (bf16[2,16,128,128]{3,2,1,0:T(8,128)(2,1)}, bf16[2,16,128,128]{3,2,1,0:T(8,128)(2,1)S(1)}, u32[]{:S(2)}, u32[]{:S(2)}) collective-permute-start(bf16[2,16,128,128]{3,2,1,0:T(8,128)(2,1)} %constant_dynamic-slice_fusion), channel_id=1, source_target_pairs={{4,12},{12,4},{5,13},{13,5},{6,14},{14,6},{7,15},{15,7},{20,28},{2... | collective-permute-start | bytes 3145736 | tf_op jit(solution)/shard_map/ppermute | solution.py:658
  9.4 6.3 %all-to-all-start = ((bf16[16,24,256]{2,1,0:T(8,128)(2,1)}), bf16[16,24,256]{2,1,0:T(8,128)(2,1)S(1)}, u32[]{:S(2)}, u32[]{:S(2)}) async-start(bf16[16,24,256]{2,1,0:T(8,128)(2,1)} %bitcast.27), calls=%async_computation | async-start | bytes 393216 | tf_op jit(solution)/shard_map/all_to_all | solution.py:678
  17.4 6.4 %all-to-all-done.in_ref = bf16[16,24,256]{2,1,0:T(8,128)(2,1)S(1)} async-done(((bf16[16,24,256]{2,1,0:T(8,128)(2,1)}), bf16[16,24,256]{2,1,0:T(8,128)(2,1)S(1)}, u32[]{:S(2)}, u32[]{:S(2)}) %all-to-all-start) | async-done | bytes 196640 | tf_op jit(solution)/shard_map/all_to_all | solution.py:678
  25.4 3.3 %collective-permute-start.2 = (bf16[2,16,128,128]{3,2,1,0:T(8,128)(2,1)S(1)}, bf16[2,16,128,128]{3,2,1,0:T(8,128)(2,1)}, u32[]{:S(2)}, u32[]{:S(2)}) collective-permute-start(bf16[2,16,128,128]{3,2,1,0:T(8,128)(2,1)S(1)} %collective-permute-done.1.w2), channel_id=1, source_target_pairs={{4,0},{12,8},{5,1},{13,9},{6,2},{14,10},{7,3},{15,11},{20,16},{28,... | collective-permute-start | bytes 3145736 | tf_op jit(solution)/shard_map/ppermute | solution.py:681
  28.7 3.5 %modes.1 = bf16[8,128,128]{2,1,0:T(8,128)(2,1)S(1)} custom-call(s32[1]{0:T(128)} %bitcast.seg_ref, f32[256,128]{1,0:T(8,128)S(1)} %get-tuple-element.36.y_ref.refs_0_, f32[64,128]{1,0:T(8,128)S(1)} %copy-done.23, f32[64,64]{1,0:T(8,128)S(1)} %copy-done.10, bf16[4,16,128,128]{3,2,1,0:T(8,128)(2,1)S(1)} %pack.1.w0, ...), custom_call_target="tpu_custom_call" | custom-call | tf_op jit(solution)/shard_map/modes/pallas_call | solution.py:752
  32.9 1.6 collective-permute-start.3
  34.7 5.9 %all-to-all-start.1 = ((bf16[8,128,128]{2,1,0:T(8,128)(2,1)}), bf16[8,128,128]{2,1,0:T(8,128)(2,1)S(1)}, u32[]{:S(2)}, u32[]{:S(2)}) async-start(bf16[8,128,128]{2,1,0:T(8,128)(2,1)} %copy-done.14), calls=%async_computation.1 | async-start | bytes 524288 | tf_op jit(solution)/shard_map/all_to_all | solution.py:736
  41.2 7.7 %all-to-all-done.1.recv_ref = bf16[8,128,128]{2,1,0:T(8,128)(2,1)S(1)} async-done(((bf16[8,128,128]{2,1,0:T(8,128)(2,1)}), bf16[8,128,128]{2,1,0:T(8,128)(2,1)S(1)}, u32[]{:S(2)}, u32[]{:S(2)}) %all-to-all-start.1) | async-done | bytes 262176 | tf_op jit(solution)/shard_map/all_to_all | solution.py:736
  49.0 5.0 %forward.3 = (bf16[16,128,256]{2,1,0:T(8,128)(2,1)S(1)}, bf16[16,128,256]{2,1,0:T(8,128)(2,1)S(1)}, f32[256,128]{1,0:T(8,128)S(1)}, bf16[8,64,128]{2,1,0:T(8,128)(2,1)S(1)}) custom-call(s32[1]{0:T(128)} %bitcast.seg_ref, bf16[8,128,128]{2,1,0:T(8,128)(2,1)S(1)} %all-to-all-done.1.recv_ref, bf16[16,128,256]{2,1,0:T(8,128)(2,1)S(1)} %copy-done.4, ...), custom_call_target="tpu_custom_call" | custom-call | tf_op jit(solution)/shard_map/forward/pallas_call | solution.py:752
  56.4 9.3 %all_to_all.40.recv_ref = bf16[8,64,128]{2,1,0:T(8,128)(2,1)S(1)} all-to-all(bf16[8,64,128]{2,1,0:T(8,128)(2,1)S(1)} %get-tuple-element.39), channel_id=1, replica_groups={{0,1,2,3,8,9,10,11},{4,5,6,7,12,13,14,15},{16,17,18,19,24,25,26,27},{20..., dimensions={0} | all-to-all | bytes 262144 | tf_op jit(solution)/shard_map/all_to_all | solution.py:736
  65.7 4.9 %forward.4 = (bf16[16,128,256]{2,1,0:T(8,128)(2,1)S(1)}, bf16[16,128,256]{2,1,0:T(8,128)(2,1)S(1)}, f32[256,128]{1,0:T(8,128)S(1)}, bf16[8,64,128]{2,1,0:T(8,128)(2,1)S(1)}) custom-call(s32[1]{0:T(128)} %bitcast.seg_ref, bf16[8,64,128]{2,1,0:T(8,128)(2,1)S(1)} %all_to_all.40.recv_ref, bf16[16,128,256]{2,1,0:T(8,128)(2,1)S(1)} %get-tuple-element.40.act_ref, ...), custom_call_target="tpu_custom_call" | custom-call | tf_op jit(solution)/shard_map/forward/pallas_call | solution.py:752
  71.2 8.8 %all_to_all.41.recv_ref = bf16[8,64,128]{2,1,0:T(8,128)(2,1)S(1)} all-to-all(bf16[8,64,128]{2,1,0:T(8,128)(2,1)S(1)} %get-tuple-element.44), channel_id=1, replica_groups={{0,1,2,3,8,9,10,11},{4,5,6,7,12,13,14,15},{16,17,18,19,24,25,26,27},{20..., dimensions={0} | all-to-all | bytes 262144 | tf_op jit(solution)/shard_map/all_to_all | solution.py:736
  80.1 5.5 %forward.5 = (bf16[16,128,256]{2,1,0:T(8,128)(2,1)S(1)}, bf16[16,128,256]{2,1,0:T(8,128)(2,1)S(1)}, f32[256,128]{1,0:T(8,128)S(1)}, bf16[8,64,128]{2,1,0:T(8,128)(2,1)}) custom-call(s32[1]{0:T(128)} %bitcast.seg_ref, bf16[8,64,128]{2,1,0:T(8,128)(2,1)S(1)} %all_to_all.41.recv_ref, bf16[16,128,256]{2,1,0:T(8,128)(2,1)S(1)} %get-tuple-element.45.act_ref, ...), custom_call_target="tpu_custom_call" | custom-call | tf_op jit(solution)/shard_map/forward/pallas_call | solution.py:752
  85.6 1.0 copy-done.12
  87.7 4.7 %all-to-all-start.4 = ((bf16[8,64,128]{2,1,0:T(8,128)(2,1)}), bf16[8,64,128]{2,1,0:T(8,128)(2,1)S(1)}, u32[]{:S(2)}, u32[]{:S(2)}) async-start(bf16[8,64,128]{2,1,0:T(8,128)(2,1)} %get-tuple-element.47), calls=%async_computation.4 | async-start | bytes 262144 | tf_op jit(solution)/shard_map/all_to_all | solution.py:736
  93.4 4.1 %all-to-all-done.4.recv_ref = bf16[8,64,128]{2,1,0:T(8,128)(2,1)S(1)} async-done(((bf16[8,64,128]{2,1,0:T(8,128)(2,1)}), bf16[8,64,128]{2,1,0:T(8,128)(2,1)S(1)}, u32[]{:S(2)}, u32[]{:S(2)}) %all-to-all-start.4) | async-done | bytes 131104 | tf_op jit(solution)/shard_map/all_to_all | solution.py:736
  98.1 1.2 copy-done.13
  100.3 15.2 %top.1 = (bf16[16,128,256]{2,1,0:T(8,128)(2,1)S(1)}, f32[256,128]{1,0:T(8,128)S(1)}, f32[128,128]{1,0:T(8,128)S(1)}, bf16[8,64,128]{2,1,0:T(8,128)(2,1)}) custom-call(s32[1]{0:T(128)} %bitcast.seg_ref, bf16[8,64,128]{2,1,0:T(8,128)(2,1)S(1)} %copy-done.25, bf16[16,128,256]{2,1,0:T(8,128)(2,1)S(1)} %copy-done.13, ...), custom_call_target="tpu_custom_call" | custom-call | tf_op jit(solution)/shard_map/top/pallas_call | solution.py:752
  116.6 4.6 %all-to-all-start.5 = ((bf16[8,64,128]{2,1,0:T(8,128)(2,1)}), bf16[8,64,128]{2,1,0:T(8,128)(2,1)S(1)}, u32[]{:S(2)}, u32[]{:S(2)}) async-start(bf16[8,64,128]{2,1,0:T(8,128)(2,1)} %get-tuple-element.49), calls=%async_computation.5 | async-start | bytes 262144 | tf_op jit(solution)/shard_map/all_to_all | solution.py:736
  121.2 5.1 %all-to-all-done.5.recv_ref = bf16[8,64,128]{2,1,0:T(8,128)(2,1)S(1)} async-done(((bf16[8,64,128]{2,1,0:T(8,128)(2,1)}), bf16[8,64,128]{2,1,0:T(8,128)(2,1)S(1)}, u32[]{:S(2)}, u32[]{:S(2)}) %all-to-all-start.5) | async-done | bytes 131104 | tf_op jit(solution)/shard_map/all_to_all | solution.py:736
  126.3 1.2 copy-done.20
  127.5 1.2 copy-done.22
  128.8 4.7 %backward.3 = (bf16[16,128,256]{2,1,0:T(8,128)(2,1)S(1)}, f32[256,128]{1,0:T(8,128)S(1)}, f32[128,128]{1,0:T(8,128)S(1)}, bf16[8,64,128]{2,1,0:T(8,128)(2,1)S(1)}) custom-call(s32[1]{0:T(128)} %bitcast.seg_ref, bf16[8,64,128]{2,1,0:T(8,128)(2,1)S(1)} %all-to-all-done.5.recv_ref, bf16[16,128,256]{2,1,0:T(8,128)(2,1)S(1)} %copy-done.22, ...), custom_call_target="tpu_custom_call" | custom-call | tf_op jit(solution)/shard_map/backward/pallas_call | solution.py:752
  133.5 8.8 %all_to_all.42.recv_ref = bf16[8,64,128]{2,1,0:T(8,128)(2,1)S(1)} all-to-all(bf16[8,64,128]{2,1,0:T(8,128)(2,1)S(1)} %get-tuple-element.52), channel_id=1, replica_groups={{0,1,2,3,8,9,10,11},{4,5,6,7,12,13,14,15},{16,17,18,19,24,25,26,27},{20..., dimensions={0} | all-to-all | bytes 262144 | tf_op jit(solution)/shard_map/all_to_all | solution.py:736
  142.3 4.8 %backward.4 = (bf16[16,128,256]{2,1,0:T(8,128)(2,1)S(1)}, f32[256,128]{1,0:T(8,128)S(1)}, f32[128,128]{1,0:T(8,128)S(1)}, bf16[8,64,128]{2,1,0:T(8,128)(2,1)S(1)}) custom-call(s32[1]{0:T(128)} %bitcast.seg_ref, bf16[8,64,128]{2,1,0:T(8,128)(2,1)S(1)} %all_to_all.42.recv_ref, bf16[16,128,256]{2,1,0:T(8,128)(2,1)S(1)} %get-tuple-element.53.grad_ref, ...), custom_call_target="tpu_custom_call" | custom-call | tf_op jit(solution)/shard_map/backward/pallas_call | solution.py:752
  147.1 8.7 %all_to_all.43.recv_ref = bf16[8,64,128]{2,1,0:T(8,128)(2,1)S(1)} all-to-all(bf16[8,64,128]{2,1,0:T(8,128)(2,1)S(1)} %get-tuple-element.55), channel_id=1, replica_groups={{0,1,2,3,8,9,10,11},{4,5,6,7,12,13,14,15},{16,17,18,19,24,25,26,27},{20..., dimensions={0} | all-to-all | bytes 262144 | tf_op jit(solution)/shard_map/all_to_all | solution.py:736
  155.8 4.3 %backward.5 = (bf16[16,128,256]{2,1,0:T(8,128)(2,1)}, f32[256,128]{1,0:T(8,128)S(1)}, f32[128,128]{1,0:T(8,128)S(1)}, bf16[8,64,128]{2,1,0:T(8,128)(2,1)}) custom-call(s32[1]{0:T(128)} %bitcast.seg_ref, bf16[8,64,128]{2,1,0:T(8,128)(2,1)S(1)} %all_to_all.43.recv_ref, bf16[16,128,256]{2,1,0:T(8,128)(2,1)S(1)} %get-tuple-element.56.grad_ref, ...), custom_call_target="tpu_custom_call" | custom-call | tf_op jit(solution)/shard_map/backward/pallas_call | solution.py:752
  160.3 8.6 %collective-permute-start.5 = (f32[576,128]{1,0:T(8,128)S(1)}, f32[576,128]{1,0:T(8,128)S(1)}, u32[]{:S(2)}, u32[]{:S(2)}) collective-permute-start(f32[576,128]{1,0:T(8,128)S(1)} %get-tuple-element.67), channel_id=1, source_target_pairs={{0,4},{4,0},{8,12},{12,8},{1,5},{5,1},{9,13},{13,9},{2,6},{6,2},{1... | collective-permute-start | bytes 884744 | tf_op jit(solution)/shard_map/ppermute | solution.py:849
  168.9 1.2 collective-permute-done.5.theirs_ref
  170.1 5.6 %grads.1 = (f32[4,32,2,64,64]{4,3,2,1,0:T(8,128)}, f32[64,64]{1,0:T(8,128)}) custom-call(f32[576,128]{1,0:T(8,128)S(1)} %get-tuple-element.66.mine_ref, f32[576,128]{1,0:T(8,128)S(1)} %collective-permute-done.5.theirs_ref, f32[64,64]{1,0:T(8,128)S(1)} %copy-done.11, f32[64,64]{1,0:T(8,128)S(1)} %copy-done.11), custom_call_target="tpu_custom_call" | custom-call | tf_op jit(solution)/shard_map/grads/pallas_call | solution.py:851
  (129 shorter events, 15.0 us)
Async XLA Ops:
  4.0 28.3 %copy-start.1 = (bf16[4,16,128,128]{3,2,1,0:T(8,128)(2,1)}, bf16[4,16,128,128]{3,2,1,0:T(8,128)(2,1)S(1)}, u32[]{:S(2)}) copy-start(bf16[4,16,128,128]{3,2,1,0:T(8,128)(2,1)S(1)} %pack.1.w0) | copy-start | bytes 6291460
  4.0 11.9 %copy-start.42 = (bf16[8,64]{1,0:T(8,128)(2,1)S(1)}, bf16[8,64]{1,0:T(8,128)(2,1)}, u32[]{:S(2)}) copy-start(bf16[8,64]{1,0:T(8,128)(2,1)} %param.22) | copy-start | bytes 3076
  4.0 24.7 %copy-start.10 = (f32[64,64]{1,0:T(8,128)S(1)}, f32[64,64]{1,0:T(8,128)}, u32[]{:S(2)}) copy-start(f32[64,64]{1,0:T(8,128)} %constant.66.clone.xi_ref.xf_ref) | copy-start | bytes 49156
  4.0 24.7 %copy-start.23 = (f32[64,128]{1,0:T(8,128)S(1)}, f32[64,128]{1,0:T(8,128)}, u32[]{:S(2)}) copy-start(f32[64,128]{1,0:T(8,128)} %constant.64.clone.lx_ref) | copy-start | bytes 98308
  4.0 24.7 %collective-permute-start = (bf16[4,16,128,128]{3,2,1,0:T(8,128)(2,1)S(1)}, bf16[4,16,128,128]{3,2,1,0:T(8,128)(2,1)}, u32[]{:S(2)}, u32[]{:S(2)}) collective-permute-start(bf16[4,16,128,128]{3,2,1,0:T(8,128)(2,1)S(1)} %pack.1.w0), channel_id=1, source_target_pairs={{0,4},{4,0},{8,12},{12,8},{1,5},{5,1},{9,13},{13,9},{2,6},{6,2},{1... | collective-permute-start | bytes 6291464 | tf_op jit(solution)/shard_map/ppermute | solution.py:656
  5.8 19.6 %collective-permute-start.1 = (bf16[2,16,128,128]{3,2,1,0:T(8,128)(2,1)}, bf16[2,16,128,128]{3,2,1,0:T(8,128)(2,1)S(1)}, u32[]{:S(2)}, u32[]{:S(2)}) collective-permute-start(bf16[2,16,128,128]{3,2,1,0:T(8,128)(2,1)} %constant_dynamic-slice_fusion), channel_id=1, source_target_pairs={{4,12},{12,4},{5,13},{13,5},{6,14},{14,6},{7,15},{15,7},{20,28},{2... | collective-permute-start | bytes 3145736 | tf_op jit(solution)/shard_map/ppermute | solution.py:658
  9.4 14.5 %all-to-all-start = ((bf16[16,24,256]{2,1,0:T(8,128)(2,1)}), bf16[16,24,256]{2,1,0:T(8,128)(2,1)S(1)}, u32[]{:S(2)}, u32[]{:S(2)}) async-start(bf16[16,24,256]{2,1,0:T(8,128)(2,1)} %bitcast.27), calls=%async_computation | async-start | bytes 393216 | tf_op jit(solution)/shard_map/all_to_all | solution.py:678
  25.4 15.8 %collective-permute-start.2 = (bf16[2,16,128,128]{3,2,1,0:T(8,128)(2,1)S(1)}, bf16[2,16,128,128]{3,2,1,0:T(8,128)(2,1)}, u32[]{:S(2)}, u32[]{:S(2)}) collective-permute-start(bf16[2,16,128,128]{3,2,1,0:T(8,128)(2,1)S(1)} %collective-permute-done.1.w2), channel_id=1, source_target_pairs={{4,0},{12,8},{5,1},{13,9},{6,2},{14,10},{7,3},{15,11},{20,16},{28,... | collective-permute-start | bytes 3145736 | tf_op jit(solution)/shard_map/ppermute | solution.py:681
  28.7 20.3 %copy-start.38 = (bf16[32,256]{1,0:T(8,128)(2,1)S(1)}, bf16[32,256]{1,0:T(8,128)(2,1)}, u32[]{:S(2)}) copy-start(bf16[32,256]{1,0:T(8,128)(2,1)} %constant.67.clone.inv_ref) | copy-start | bytes 49156
  32.9 22.7 %collective-permute-start.3 = (bf16[2,16,128,128]{3,2,1,0:T(8,128)(2,1)}, bf16[2,16,128,128]{3,2,1,0:T(8,128)(2,1)}, u32[]{:S(2)}, u32[]{:S(2)}) collective-permute-start(bf16[2,16,128,128]{3,2,1,0:T(8,128)(2,1)} %constant_dynamic-slice_fusion), channel_id=1, source_target_pairs={{8,0},{9,1},{10,2},{11,3},{24,16},{25,17},{26,18},{27,19}} | collective-permute-start | bytes 3145736 | tf_op jit(solution)/shard_map/ppermute | solution.py:794
  34.6 14.4 %copy-start.4 = (bf16[16,128,256]{2,1,0:T(8,128)(2,1)S(1)}, bf16[16,128,256]{2,1,0:T(8,128)(2,1)}, u32[]{:S(2)}) copy-start(bf16[16,128,256]{2,1,0:T(8,128)(2,1)} %copy-done.3) | copy-start | bytes 3145732
  34.7 14.3 %copy-start.39 = (bf16[4,64,64]{2,1,0:T(8,128)(2,1)}, bf16[4,64,64]{2,1,0:T(8,128)(2,1)S(1)}, u32[]{:S(2)}) copy-start(bf16[4,64,64]{2,1,0:T(8,128)(2,1)S(1)} %reshape.71) | copy-start | bytes 98308
  34.7 14.3 %all-to-all-start.1 = ((bf16[8,128,128]{2,1,0:T(8,128)(2,1)}), bf16[8,128,128]{2,1,0:T(8,128)(2,1)S(1)}, u32[]{:S(2)}, u32[]{:S(2)}) async-start(bf16[8,128,128]{2,1,0:T(8,128)(2,1)} %copy-done.14), calls=%async_computation.1 | async-start | bytes 524288 | tf_op jit(solution)/shard_map/all_to_all | solution.py:736
  49.0 16.7 %copy-start.29 = (bf16[32,256]{1,0:T(8,128)(2,1)S(1)}, bf16[32,256]{1,0:T(8,128)(2,1)}, u32[]{:S(2)}) copy-start(bf16[32,256]{1,0:T(8,128)(2,1)} %constant.60.clone.inv_ref) | copy-start | bytes 49156
  55.6 14.9 %copy-start.6 = (bf16[16,128,256]{2,1,0:T(8,128)(2,1)}, bf16[16,128,256]{2,1,0:T(8,128)(2,1)S(1)}, u32[]{:S(2)}) copy-start(bf16[16,128,256]{2,1,0:T(8,128)(2,1)S(1)} %get-tuple-element.40.act_ref) | copy-start | bytes 3145732
  55.6 10.0 %collective-permute-start.4 = (bf16[2,16,128,128]{3,2,1,0:T(8,128)(2,1)}, bf16[2,16,128,128]{3,2,1,0:T(8,128)(2,1)S(1)}, u32[]{:S(2)}, u32[]{:S(2)}) collective-permute-start(bf16[2,16,128,128]{3,2,1,0:T(8,128)(2,1)} %collective-permute-done.3.w2), channel_id=1, source_target_pairs={{0,4},{1,5},{2,6},{3,7},{16,20},{17,21},{18,22},{19,23}} | collective-permute-start | bytes 3145736 | tf_op jit(solution)/shard_map/ppermute | solution.py:812
  71.2 14.4 %copy-start.8 = (bf16[16,128,256]{2,1,0:T(8,128)(2,1)}, bf16[16,128,256]{2,1,0:T(8,128)(2,1)S(1)}, u32[]{:S(2)}) copy-start(bf16[16,128,256]{2,1,0:T(8,128)(2,1)S(1)} %get-tuple-element.45.act_ref) | copy-start | bytes 3145732
  71.2 14.4 %copy-start.17 = (bf16[16,128,256]{2,1,0:T(8,128)(2,1)}, bf16[16,128,256]{2,1,0:T(8,128)(2,1)S(1)}, u32[]{:S(2)}) copy-start(bf16[16,128,256]{2,1,0:T(8,128)(2,1)S(1)} %get-tuple-element.54.slope_ref) | copy-start | bytes 3145732
  80.1 12.3 %copy-start.46 = (bf16[128]{0:T(256)(128)(2,1)S(1)}, bf16[128]{0:T(256)(128)(2,1)}, u32[]{:S(2)}) copy-start(bf16[128]{0:T(256)(128)(2,1)} %param.29) | copy-start | bytes 772
  80.1 12.4 %copy-start.43 = (f32[128]{0:T(128)S(1)}, f32[128]{0:T(128)}, u32[]{:S(2)}) copy-start(f32[128]{0:T(128)} %param.28) | copy-start | bytes 1540
  80.1 12.5 %copy-start.37 = (bf16[64,128]{1,0:T(8,128)(2,1)S(1)}, bf16[64,128]{1,0:T(8,128)(2,1)}, u32[]{:S(2)}) copy-start(bf16[64,128]{1,0:T(8,128)(2,1)} %down_ref.1) | copy-start | bytes 49156
  80.1 18.1 %copy-start.11 = (f32[64,64]{1,0:T(8,128)S(1)}, f32[64,64]{1,0:T(8,128)}, u32[]{:S(2)}) copy-start(f32[64,64]{1,0:T(8,128)} %constant.65.clone.xa_ref.xz_ref) | copy-start | bytes 49156
  87.7 9.8 %all-to-all-start.4 = ((bf16[8,64,128]{2,1,0:T(8,128)(2,1)}), bf16[8,64,128]{2,1,0:T(8,128)(2,1)S(1)}, u32[]{:S(2)}, u32[]{:S(2)}) async-start(bf16[8,64,128]{2,1,0:T(8,128)(2,1)} %get-tuple-element.47), calls=%async_computation.4 | async-start | bytes 262144 | tf_op jit(solution)/shard_map/all_to_all | solution.py:736
  100.3 20.9 %copy-start.40 = (bf16[4,64,64]{2,1,0:T(8,128)(2,1)S(1)}, bf16[4,64,64]{2,1,0:T(8,128)(2,1)}, u32[]{:S(2)}) copy-start(bf16[4,64,64]{2,1,0:T(8,128)(2,1)} %copy-done.39) | copy-start | bytes 98308
  100.3 26.0 %copy-start.9 = (bf16[16,128,256]{2,1,0:T(8,128)(2,1)S(1)}, bf16[16,128,256]{2,1,0:T(8,128)(2,1)}, u32[]{:S(2)}) copy-start(bf16[16,128,256]{2,1,0:T(8,128)(2,1)} %copy-done.8) | copy-start | bytes 3145732
  100.3 26.0 %copy-start.28 = (bf16[32,256]{1,0:T(8,128)(2,1)S(1)}, bf16[32,256]{1,0:T(8,128)(2,1)}, u32[]{:S(2)}) copy-start(bf16[32,256]{1,0:T(8,128)(2,1)} %constant.61.clone.fwd_ref) | copy-start | bytes 49156
  116.6 9.8 %all-to-all-start.5 = ((bf16[8,64,128]{2,1,0:T(8,128)(2,1)}), bf16[8,64,128]{2,1,0:T(8,128)(2,1)S(1)}, u32[]{:S(2)}, u32[]{:S(2)}) async-start(bf16[8,64,128]{2,1,0:T(8,128)(2,1)} %get-tuple-element.49), calls=%async_computation.5 | async-start | bytes 262144 | tf_op jit(solution)/shard_map/all_to_all | solution.py:736
  128.8 13.5 %copy-start.7 = (bf16[16,128,256]{2,1,0:T(8,128)(2,1)S(1)}, bf16[16,128,256]{2,1,0:T(8,128)(2,1)}, u32[]{:S(2)}) copy-start(bf16[16,128,256]{2,1,0:T(8,128)(2,1)} %copy-done.6) | copy-start | bytes 3145732
  128.8 13.5 %copy-start.18 = (bf16[16,128,256]{2,1,0:T(8,128)(2,1)S(1)}, bf16[16,128,256]{2,1,0:T(8,128)(2,1)}, u32[]{:S(2)}) copy-start(bf16[16,128,256]{2,1,0:T(8,128)(2,1)} %copy-done.17) | copy-start | bytes 3145732
  142.2 13.5 %copy-start.5 = (bf16[16,128,256]{2,1,0:T(8,128)(2,1)S(1)}, bf16[16,128,256]{2,1,0:T(8,128)(2,1)}, u32[]{:S(2)}) copy-start(bf16[16,128,256]{2,1,0:T(8,128)(2,1)} %copy-done.3) | copy-start | bytes 3145732
  142.2 13.5 %copy-start.16 = (bf16[16,128,256]{2,1,0:T(8,128)(2,1)S(1)}, bf16[16,128,256]{2,1,0:T(8,128)(2,1)}, u32[]{:S(2)}) copy-start(bf16[16,128,256]{2,1,0:T(8,128)(2,1)} %copy-done.15) | copy-start | bytes 3145732
  160.3 9.8 %collective-permute-start.5 = (f32[576,128]{1,0:T(8,128)S(1)}, f32[576,128]{1,0:T(8,128)S(1)}, u32[]{:S(2)}, u32[]{:S(2)}) collective-permute-start(f32[576,128]{1,0:T(8,128)S(1)} %get-tuple-element.67), channel_id=1, source_target_pairs={{0,4},{4,0},{8,12},{12,8},{1,5},{5,1},{9,13},{13,9},{2,6},{6,2},{1... | collective-permute-start | bytes 884744 | tf_op jit(solution)/shard_map/ppermute | solution.py:849
  (25 other events, 87.3 us)

commit v3 on v2

--- a/solution.py
+++ b/solution.py
@@ -234,7 +234,6 @@
 f32, bf16 = (jnp.float32, jnp.bfloat16)
 NT = (((1,), (1,)), ((), ()))
 NN = (((1,), (0,)), ((), ()))
-STEPS = 2
 VMEM_LIMIT = 48 << 20
 
 
@@ -407,8 +406,8 @@
 
 
 def widen(recv_ref, r_ref):
-    chunks, rows, _ = recv_ref.shape
-    for k in range(chunks):
+    rows = recv_ref.shape[1]
+    for k in range(r_ref.shape[0] // rows):
         r_ref[k * rows : (k + 1) * rows] = recv_ref[k].astype(f32)
 
 
@@ -423,7 +422,8 @@
     return ((inner // per_chunk) * space + half_side * (space // 2) + x // rows, inner % per_chunk)
 
 
-def lift_kernel(in_ref, lw_ref, lb_ref, tab_ref, act_ref, y_ref, *, space, rows, per_chunk, depth):
+def lift_kernel(seg_ref, in_ref, lw_ref, lb_ref, tab_ref, act_ref, y_ref, *, space, rows, per_chunk, depth):
+    table = tab_ref[seg_ref[1]]
     for x in range(act_ref.shape[0]):
         cells = []
         for side in range(2):
@@ -434,7 +434,7 @@
         act = act.astype(bf16)
         act_ref[x] = act
         y_ref[x * 16 : (x + 1) * 16] = lax.dot_general(
-            tab_ref[...], act, NT, preferred_element_type=f32
+            table, act, NT, preferred_element_type=f32
         )
 
 
@@ -445,47 +445,55 @@
         forward_modes(y_ref, w_ref, lx_ref, xi_ref, t_ref, m_ref, out_ref, 2 * start, start)
 
 
+def in_pairs(count, start, finish, scratch):
+    start(0, scratch[0])
+
+    def two(i, carry):
+        x = 2 * i
+        start(x + 1, scratch[1])
+        finish(x, scratch[0])
+        start(jnp.minimum(x + 2, count - 1), scratch[0])
+        finish(x + 1, scratch[1])
+        return carry
+
+    lax.fori_loop(0, count // 2, two, 0)
+
+
+def put_rows(y_ref, x, rows):
+    y_ref[pl.ds(pl.multiple_of(x * 16, 16), 16), :] = rows
+
+
 def forward_kernel(
     seg_ref, recv_ref, act_ref, pw_ref, pb_ref, inv_ref, tab_ref, lx_ref, xi_ref, w0, w1, w2, w3,
-    next_ref, slope_ref, y_ref, out_ref, w_ref, sem, t_ref, m_ref, r_ref, *, layer,
+    next_ref, slope_ref, y_ref, out_ref, w_ref, sem, t_ref, m_ref, r_ref, p0_ref, p1_ref, *, layer,
 ):
-    step = pl.program_id(0)
-    block = act_ref.shape[0]
-    x_half = y_ref.shape[0] // 16
-
-    @pl.when(step == 0)
-    def _():
-        choose_kernel(seg_ref, layer, (w0, w1, w2, w3), w_ref, sem, True)
-        widen(recv_ref, r_ref)
-
-    def one(i, carry):
-        x = step * block + i
-        pre = row_product(pw_ref[layer - 1], act_ref[i], r_ref, inv_ref[...], x, x_half)
-        pre = pre + pb_ref[layer - 1]
-        value, slope = gelu_both(pre)
+    x_half = act_ref.shape[0]
+    choose_kernel(seg_ref, layer, (w0, w1, w2, w3), w_ref, sem, True)
+    widen(recv_ref, r_ref)
+    table = tab_ref.at[seg_ref[1]]
+
+    def start(x, ref):
+        ref[...] = row_product(pw_ref[layer - 1], act_ref[x], r_ref, inv_ref[...], x, x_half)
+
+    def finish(x, ref):
+        value, slope = gelu_both(ref[...] + pb_ref[layer - 1])
         value = value.astype(bf16)
-        next_ref[i] = value
-        slope_ref[i] = slope.astype(bf16)
-        y_ref[pl.ds(pl.multiple_of(x * 16, 16), 16), :] = lax.dot_general(
-            tab_ref[...], value, NT, preferred_element_type=f32
-        )
-        return carry
-
-    lax.fori_loop(0, block, one, 0, unroll=2)
-
-    @pl.when(step == pl.num_programs(0) - 1)
-    def _():
-        choose_kernel(seg_ref, layer, (w0, w1, w2, w3), w_ref, sem, False)
-        forward_modes(y_ref, w_ref, lx_ref, xi_ref, t_ref, m_ref, out_ref)
-
-
-def adjoint_rows(x, i, grad, act, tab_ref, pre_ref, y_ref, point_ref):
+        next_ref[x] = value
+        slope_ref[x] = slope.astype(bf16)
+        put_rows(y_ref, x, lax.dot_general(table[...], value, NT, preferred_element_type=f32))
+
+    in_pairs(x_half, start, finish, (p0_ref, p1_ref))
+    choose_kernel(seg_ref, layer, (w0, w1, w2, w3), w_ref, sem, False)
+    forward_modes(y_ref, w_ref, lx_ref, xi_ref, t_ref, m_ref, out_ref)
+
+
+def adjoint_rows(x, grad, act, table, pre_ref, y_ref, point_ref):
     pre_grad = grad.astype(bf16)
-    pre_ref[i] = pre_grad
+    pre_ref[x] = pre_grad
     both = lax.dot_general(
-        jnp.concatenate([tab_ref[...], act], axis=0), pre_grad, NT, preferred_element_type=f32
-    )
-    y_ref[pl.ds(pl.multiple_of(x * 16, 16), 16), :] = both[:16]
+        jnp.concatenate([table[...], act], axis=0), pre_grad, NT, preferred_element_type=f32
+    )
+    put_rows(y_ref, x, both[:16])
     point_ref[...] += both[16:]
 
 
@@ -493,30 +501,33 @@
     seg_ref, recv_ref, act_ref, in_ref, pw_ref, pb_ref, inv_ref, up_ref, hb_ref, down_ref, ow_ref,
     tab_ref, xa_ref, xf_ref, w0, w1, w2, w3,
     pre_ref, y_ref, point_ref, out_ref, w_ref, sem, t_ref, m_ref, r_ref,
+    p0_ref, p1_ref, s0_ref, s1_ref, h0_ref, h1_ref,
     *, layer, space, rows, per_chunk, first_row,
 ):
-    step = pl.program_id(0)
-    block = act_ref.shape[0]
-    x_half = y_ref.shape[0] // 16
-
-    @pl.when(step == 0)
-    def _():
-        choose_kernel(seg_ref, layer, (w0, w1, w2, w3), w_ref, sem, True)
-        widen(recv_ref, r_ref)
-        point_ref[...] = jnp.zeros_like(point_ref)
-
-    def one(i, carry):
-        x = step * block + i
-        act = act_ref[i]
-        pre = row_product(pw_ref[layer], act, r_ref, inv_ref[...], x, x_half) + pb_ref[layer]
-        value, slope = gelu_both(pre)
+    x_half = act_ref.shape[0]
+    choose_kernel(seg_ref, layer, (w0, w1, w2, w3), w_ref, sem, True)
+    widen(recv_ref, r_ref)
+    point_ref[...] = jnp.zeros_like(point_ref)
+    table = tab_ref.at[seg_ref[1]]
+    hidden_count = up_ref.shape[0]
+    size = act_ref.shape[1] // 2
+
+    def start(x, ref):
+        ref[...] = row_product(pw_ref[layer], act_ref[x], r_ref, inv_ref[...], x, x_half)
+
+    def middle(ref, slope_ref, hidden_ref):
+        value, slope = gelu_both(ref[...] + pb_ref[layer])
+        slope_ref[...] = slope
         value = value.astype(bf16)
-        grads = []
-        size = value.shape[0] // 2
         for side in range(2):
-            hidden = jnp.dot(
+            hidden_ref[side * hidden_count : (side + 1) * hidden_count] = jnp.dot(
                 up_ref[...], value[side * size : (side + 1) * size], preferred_element_type=f32
             )
+
+    def finish(x, slope_ref, hidden_ref):
+        grads = []
+        for side in range(2):
+            hidden = hidden_ref[side * hidden_count : (side + 1) * hidden_count]
             _, hidden_slope = gelu_both(hidden + hb_ref[...])
             chunk, within = chunk_of(x, side, space, rows, per_chunk)
             cots = in_ref[chunk, first_row : first_row + per_chunk, :].astype(f32)
@@ -528,51 +539,54 @@
                     down_ref[...], (hidden_slope * ow_ref[...]).astype(bf16), preferred_element_type=f32
                 )
             )
-        grad = jnp.concatenate(grads, axis=0)
-        adjoint_rows(x, i, grad * slope, act, tab_ref, pre_ref, y_ref, point_ref)
+        grad = jnp.concatenate(grads, axis=0) * slope_ref[...]
+        adjoint_rows(x, grad, act_ref[x], table, pre_ref, y_ref, point_ref)
+
+    last = x_half - 1
+    start(0, p0_ref)
+    middle(p0_ref, s0_ref, h0_ref)
+    start(1, p1_ref)
+
+    def two(i, carry):
+        x = 2 * i
+        start(jnp.minimum(x + 2, last), p0_ref)
+        middle(p1_ref, s1_ref, h1_ref)
+        finish(x, s0_ref, h0_ref)
+        start(jnp.minimum(x + 3, last), p1_ref)
+        middle(p0_ref, s0_ref, h0_ref)
+        finish(x + 1, s1_ref, h1_ref)
         return carry
 
-    lax.fori_loop(0, block, one, 0)
-
-    @pl.when(step == pl.num_programs(0) - 1)
-    def _():
-        choose_kernel(seg_ref, layer, (w0, w1, w2, w3), w_ref, sem, False)
-        backward_modes(y_ref, w_ref, xa_ref, xf_ref, t_ref, m_ref, out_ref)
+    lax.fori_loop(0, x_half // 2, two, 0)
+    choose_kernel(seg_ref, layer, (w0, w1, w2, w3), w_ref, sem, False)
+    backward_modes(y_ref, w_ref, xa_ref, xf_ref, t_ref, m_ref, out_ref)
 
 
 def backward_kernel(
     seg_ref, recv_ref, grad_ref, slope_ref, act_ref, pw_ref, fwd_ref, tab_ref, xa_ref, xf_ref,
     w0, w1, w2, w3,
-    pre_ref, y_ref, point_ref, out_ref, w_ref, sem, t_ref, m_ref, r_ref, *, layer,
+    pre_ref, y_ref, point_ref, out_ref, w_ref, sem, t_ref, m_ref, r_ref, p0_ref, p1_ref, *, layer,
 ):
-    step = pl.program_id(0)
-    block = act_ref.shape[0]
-    x_half = y_ref.shape[0] // 16
-
-    @pl.when(step == 0)
-    def _():
-        if layer:
-            choose_kernel(seg_ref, layer, (w0, w1, w2, w3), w_ref, sem, True)
-        widen(recv_ref, r_ref)
-        point_ref[...] = jnp.zeros_like(point_ref)
-
-    def one(i, carry):
-        x = step * block + i
-        grad = row_product(pw_ref[layer + 1], grad_ref[i], r_ref, fwd_ref[...], x, x_half)
-        adjoint_rows(
-            x, i, grad * slope_ref[i].astype(f32), act_ref[i], tab_ref, pre_ref, y_ref, point_ref
-        )
-        return carry
-
-    lax.fori_loop(0, block, one, 0, unroll=2)
-
-    @pl.when(step == pl.num_programs(0) - 1)
-    def _():
-        if layer:
-            choose_kernel(seg_ref, layer, (w0, w1, w2, w3), w_ref, sem, False)
-            backward_modes(y_ref, w_ref, xa_ref, xf_ref, t_ref, m_ref, out_ref)
-        else:
-            out_ref[...] = jnp.zeros_like(out_ref)
+    x_half = act_ref.shape[0]
+    if layer:
+        choose_kernel(seg_ref, layer, (w0, w1, w2, w3), w_ref, sem, True)
+    widen(recv_ref, r_ref)
+    point_ref[...] = jnp.zeros_like(point_ref)
+    table = tab_ref.at[seg_ref[1]]
+
+    def start(x, ref):
+        ref[...] = row_product(pw_ref[layer + 1], grad_ref[x], r_ref, fwd_ref[...], x, x_half)
+
+    def finish(x, ref):
+        grad = ref[...] * slope_ref[x].astype(f32)
+        adjoint_rows(x, grad, act_ref[x], table, pre_ref, y_ref, point_ref)
+
+    in_pairs(x_half, start, finish, (p0_ref, p1_ref))
+    if layer:
+        choose_kernel(seg_ref, layer, (w0, w1, w2, w3), w_ref, sem, False)
+        backward_modes(y_ref, w_ref, xa_ref, xf_ref, t_ref, m_ref, out_ref)
+    else:
+        out_ref[...] = jnp.zeros_like(out_ref)
 
 
 def pick_kernel(seg_ref, *refs, layers):
@@ -642,21 +656,6 @@
     pairs = kx // 2
     group = segments // 2 * space
 
-    stack = spectral_weight[0].reshape(owned, 2, pairs, 2 * c, c)
-    own = pl.pallas_call(
-        pack_kernel,
-        grid=(owned,),
-        in_specs=[pl.BlockSpec((1, 2, pairs, 2 * c, c), lambda m: (m, 0, 0, 0, 0))],
-        out_specs=pl.BlockSpec((1, pairs, 2 * c, 2 * c), lambda m: (m, 0, 0, 0)),
-        out_shape=jax.ShapeDtypeStruct((owned, pairs, 2 * c, 2 * c), bf16),
-        compiler_params=pltpu.CompilerParams(vmem_limit_bytes=VMEM_LIMIT),
-        name="pack",
-    )(stack)
-    swap = [(0, 1), (1, 0), (2, 3), (3, 2)]
-    neighbour = lax.ppermute(own, "segment", swap)
-    away = lax.dynamic_slice_in_dim(own, 2 * (1 - pair), 2, 0)
-    across_odd = lax.ppermute(away, "segment", [(1, 3), (3, 1)])
-
     cells = lax.dynamic_slice_in_dim(inputs, seg * per_chunk, per_chunk, 1)
     cells = cells.reshape(batch, per_chunk * depth, cols)
     cots = lax.dynamic_slice_in_dim(cotangent, seg * per_chunk, per_chunk, 1)
@@ -675,6 +674,22 @@
     bias_at = share_row + weight_rows
     chunk = jnp.pad(chunk, ((0, 0), (0, -chunk.shape[1] % 8), (0, 0)))
     chunk = jnp.broadcast_to(chunk[None, :, None], (segments // 2, batch, space) + chunk.shape[1:])
+    stack = spectral_weight[0].reshape(owned, 2, pairs, 2 * c, c)
+    pack = pl.pallas_call(
+        pack_kernel,
+        grid=(owned,),
+        in_specs=[pl.BlockSpec((1, 2, pairs, 2 * c, c), lambda m: (m, 0, 0, 0, 0))],
+        out_specs=pl.BlockSpec((1, pairs, 2 * c, 2 * c), lambda m: (m, 0, 0, 0)),
+        out_shape=jax.ShapeDtypeStruct((owned, pairs, 2 * c, 2 * c), bf16),
+        compiler_params=pltpu.CompilerParams(vmem_limit_bytes=VMEM_LIMIT),
+        name="pack",
+    )
+    own = pack(stack)
+    swap = [(0, 1), (1, 0), (2, 3), (3, 2)]
+    neighbour = lax.ppermute(own, "segment", swap)
+    away = lax.dynamic_slice_in_dim(own, 2 * (1 - pair), 2, 0)
+    across_odd = lax.ppermute(away, "segment", [(1, 3), (3, 1)])
+
     grid_in = lax.all_to_all(
         chunk.reshape((segments * space,) + chunk.shape[3:]), both, 0, 0, tiled=True
     )
@@ -713,9 +728,7 @@
             s = k % space
             full[k, : 2 * owned] = table[s * owned : (s + 1) * owned].reshape(2 * owned, cols)
             full[k, 8:12] = table[firsts[k] : firsts[k] + 2].reshape(4, cols)
-        return lax.dynamic_index_in_dim(
-            jnp.asarray(full, bf16), pair * space + place, 0, keepdims=False
-        )
+        return jnp.asarray(full, bf16)
 
     inv_table, fwd_table = (gathered(y_inverse), gathered(y_forward))
     act_table, grad_table = (analysis(y_forward), analysis(y_inverse))
@@ -739,28 +752,25 @@
         rank = len(array.shape)
         return pl.BlockSpec(array.shape, lambda *i: (0,) * rank)
 
-    seg_scalar = seg.astype(jnp.int32).reshape(1)
-
-    def call(kernel, args, blocked, weights, outs, scratch, steps, name):
-        def spec(array, is_blocked):
-            if is_blocked:
-                return pl.BlockSpec((array.shape[0] // steps,) + array.shape[1:], lambda i: (i, 0, 0))
-            if array.shape == sent_first.shape and steps > 1:
-                return pl.BlockSpec((space,) + array.shape[1:], lambda i: (0, 0, 0))
-            return whole(array)
-
+    def placed(kernel):
+        def body(*refs):
+            own_seg = lax.axis_index("segment")
+            kernel((own_seg, own_seg // 2 * space + lax.axis_index("space")), *refs)
+
+        return body
+
+
+    def call(kernel, args, weights, outs, scratch):
+        near = pl.BlockSpec(memory_space=pltpu.VMEM)
         return pl.pallas_call(
-            kernel,
-            grid=(steps,),
-            in_specs=[pl.BlockSpec(memory_space=pltpu.SMEM)]
-            + [spec(a, n in blocked) for n, a in enumerate(args)]
+            placed(kernel),
+            in_specs=[near] * len(args)
             + [pl.BlockSpec(memory_space=pl.ANY)] * len(weights),
-            out_specs=[spec(a, is_blocked) for a, is_blocked in outs],
-            out_shape=[a for a, _ in outs],
+            out_specs=[near] * len(outs),
+            out_shape=outs,
             scratch_shapes=scratch,
             compiler_params=pltpu.CompilerParams(vmem_limit_bytes=VMEM_LIMIT),
-            name=name,
-        )(seg_scalar, *args, *weights)
+        )(*args, *weights)
 
     lanes = 2 * c
     field = jax.ShapeDtypeStruct((x_half, lanes, cols), bf16)
@@ -772,7 +782,9 @@
         pltpu.VMEM((2,) + own.shape[1:], bf16), pltpu.SemaphoreType.DMA(()),
         pltpu.VMEM((8 * kx, lanes), f32), pltpu.VMEM((8 * kx, lanes), f32),
     ]
-    row_scratch = [pltpu.VMEM((group * 2 * x_count, lanes), f32)]
+    row = pltpu.VMEM((lanes, cols), f32)
+    row_scratch = [pltpu.VMEM((group * 2 * x_count, lanes), f32), row, row]
+    top_scratch = [row, row] + [pltpu.VMEM((2 * proj_weight.shape[1], cols), f32)] * 2
 
     zero = jnp.zeros_like(lift_weight.T)
     lift = jnp.concatenate(
@@ -781,15 +793,15 @@
     lift_col = jnp.concatenate([lift_bias] * 2)[:, None]
     where = dict(space=space, rows=row_count, per_chunk=per_chunk)
     act, y0 = pl.pallas_call(
-        partial(lift_kernel, depth=depth, **where),
+        placed(partial(lift_kernel, depth=depth, **where)),
         out_shape=[field, ycoef],
         compiler_params=pltpu.CompilerParams(vmem_limit_bytes=VMEM_LIMIT),
         name="lift",
     )(grid_in, lift, lift_col, act_table)
     acts, slopes, ya = ([act], [], [y0])
     (mine,) = call(
-        first_modes_kernel, (y0, lx, xi), (), (own, neighbour), [(sent_first, False)],
-        [pltpu.VMEM(own.shape, bf16)] + mode_scratch[1:], 1, "modes",
+        first_modes_kernel, (y0, lx, xi), (own, neighbour), [sent_first],
+        [pltpu.VMEM(own.shape, bf16)] + mode_scratch[1:],
     )
     across_even = lax.ppermute(
         lax.optimization_barrier((away, mine))[0], "segment", [(2, 0)]
@@ -802,8 +814,7 @@
         act, slope, y, mine = call(
             partial(forward_kernel, layer=layer),
             (recv, acts[-1], point_fwd, bias_cols, table, act_table, lx, xi),
-            (1,), weights_of(layer), [(field, True), (field, True), (ycoef, False), (sent, False)],
-            mode_scratch + row_scratch, STEPS, "forward",
+            weights_of(layer), [field, field, ycoef, sent], mode_scratch + row_scratch,
         )
         acts.append(act)
         slopes.append(slope)
@@ -820,8 +831,7 @@
         (recv, acts[last], grid_in, point_fwd, bias_cols, inv_table,
          proj_weight.T, proj_bias[:, None], proj_weight, out_weight.astype(f32)[:, None],
          grad_table, xa, xb),
-        (1,), weights_of(last), [(field, True), (ycoef, False), (point, False), (sent, False)],
-        mode_scratch + row_scratch, STEPS, "top",
+        weights_of(last), [field, ycoef, point, sent], mode_scratch + row_scratch + top_scratch,
     )
     yg, pgs = ([y], [pg])
     for layer in reversed(range(last)):
@@ -830,9 +840,7 @@
             partial(backward_kernel, layer=layer),
             (recv, pre_grad, slopes[layer], acts[layer], point_back, fwd_table,
              grad_table, xa, xb),
-            (1, 2, 3), weights_of(layer),
-            [(field, True), (ycoef, False), (point, False), (sent, False)],
-            mode_scratch + row_scratch, STEPS, "backward",
+            weights_of(layer), [field, ycoef, point, sent], mode_scratch + row_scratch,
         )
         yg.insert(0, y)
         pgs.insert(0, pg)
@@ -840,12 +848,11 @@
     pieces = ya + yg + pgs
     summary = jax.ShapeDtypeStruct((2 * x_half * 16 + c, lanes), f32)
     mine, theirs = pl.pallas_call(
-        partial(pick_kernel, layers=segments),
-        in_specs=[pl.BlockSpec(memory_space=pltpu.SMEM)] + [pl.BlockSpec()] * len(pieces),
+        placed(partial(pick_kernel, layers=segments)),
         out_shape=[summary, summary],
         compiler_params=pltpu.CompilerParams(vmem_limit_bytes=VMEM_LIMIT),
         name="pick",
-    )(seg_scalar, *pieces)
+    )(*pieces)
     theirs = lax.ppermute(theirs, "segment", [(0, 1), (1, 0), (2, 3), (3, 2)])
     pieces = [mine, theirs, xz, xa]
     spectral, point_out = pl.pallas_call(

time: 179 us -> 176 us (0.983)
  Pallas kernels: 57.8 us -> 50.5 us
  local copies, waits for them, and re-layouts: 17.8 us -> 21.5 us
    pallas_call x11, Pallas kernels: 52.1 us -> 44.9 us  [the longest x8 40.6 us: call(): pl.pallas_call(placed(kernel), in_specs=[near] * len(args) + [pl.BlockSpe...]
    unnamed x95 -> x101, local copies, waits for them, and re-layouts: 12.2 us -> 16.7 us
  transfers between devices with their start and end apart: 10 -> 10, of which waited for: 5 -> 5; matrix products, arithmetic and copies ran while one was open for 4% -> 3% of each run, Pallas kernels for 5% -> 5%
where the time goes in v3:
time: 176 us; the launch traced here: 173 us
  Pallas kernels  50.5 us (29%)
  starting transfers between devices  38.4 us (22%)
  blocking collectives  35.6 us (20%)
  waiting for transfers between devices  25.3 us (14%)
  local copies, waits for them, and re-layouts  21.5 us (12%)
    pallas_call x8, Pallas kernels, call(): pl.pallas_call(placed(kernel), in_specs=[near] * len(args) + [pl.BlockSpe...  40.6 us
    all_to_all x4, blocking collectives, to_all(): lax.all_to_all(block, both, 0, 0, tiled=True, axis_index_groups=device_li...  35.6 us
    all_to_all x3, waiting for transfers between devices, to_all(): lax.all_to_all(block, both, 0, 0, tiled=True, axis_index_groups=device_li...  17.6 us
    unnamed x101, local copies, waits for them, and re-layouts  16.7 us
    all_to_all x3, starting transfers between devices, to_all(): lax.all_to_all(block, both, 0, 0, tiled=True, axis_index_groups=device_li...  15.1 us
    ppermute x1, starting transfers between devices, replicated(): theirs = lax.ppermute(theirs, 'segment', [(0, 1), (1, 0), (2, 3), (3, 2)])  8.63 us
    all_to_all x1, waiting for transfers between devices, replicated(): lax.all_to_all(chunk.reshape((segments * space,) + chunk.shape[3:]), both...  6.47 us
    all_to_all x1, starting transfers between devices, replicated(): lax.all_to_all(chunk.reshape((segments * space,) + chunk.shape[3:]), both...  6.35 us
  transfers between devices with their start and end apart: 10, of which 5 were waited for; matrix products, arithmetic and copies ran while one was open for 3% of the time, Pallas kernels for 5%

profile of v3, /device:TPU:3, one launch (start us, length us, event | category | flops | bytes accessed | tf_op | source)
XLA Modules:
  0.0 173.0 jit_solution(2251019962880369374)
XLA Ops:
  0.6 3.3 %pack.1.refs_3_.refs_8_.refs_13_.refs_9_ = bf16[4,16,128,128]{3,2,1,0:T(8,128)(2,1)S(1)} custom-call(bf16[4,2,16,128,64]{4,3,2,1,0:T(8,128)(2,1)} %bitcast.21), custom_call_target="tpu_custom_call" | custom-call | tf_op jit(solution)/shard_map/pack/pallas_call | solution.py:687
  4.8 1.1 constant_dynamic-slice_fusion
  5.9 1.9 %collective-permute-start.1 = (bf16[2,16,128,128]{3,2,1,0:T(8,128)(2,1)}, bf16[2,16,128,128]{3,2,1,0:T(8,128)(2,1)S(1)}, u32[]{:S(2)}, u32[]{:S(2)}) collective-permute-start(bf16[2,16,128,128]{3,2,1,0:T(8,128)(2,1)} %constant_dynamic-slice_fusion), channel_id=1, source_target_pairs={{4,12},{12,4},{5,13},{13,5},{6,14},{14,6},{7,15},{15,7},{20,28},{2... | collective-permute-start | bytes 3145736 | tf_op jit(solution)/shard_map/ppermute | solution.py:691
  9.4 6.3 %all-to-all-start = ((bf16[16,24,256]{2,1,0:T(8,128)(2,1)}), bf16[16,24,256]{2,1,0:T(8,128)(2,1)S(1)}, u32[]{:S(2)}, u32[]{:S(2)}) async-start(bf16[16,24,256]{2,1,0:T(8,128)(2,1)} %bitcast.22), calls=%async_computation | async-start | bytes 393216 | tf_op jit(solution)/shard_map/all_to_all | solution.py:693
  17.4 6.5 %all-to-all-done.refs_0_.refs_2_ = bf16[16,24,256]{2,1,0:T(8,128)(2,1)S(1)} async-done(((bf16[16,24,256]{2,1,0:T(8,128)(2,1)}), bf16[16,24,256]{2,1,0:T(8,128)(2,1)S(1)}, u32[]{:S(2)}, u32[]{:S(2)}) %all-to-all-start) | async-done | bytes 196640 | tf_op jit(solution)/shard_map/all_to_all | solution.py:693
  26.3 3.3 %collective-permute-start.2 = (bf16[2,16,128,128]{3,2,1,0:T(8,128)(2,1)S(1)}, bf16[2,16,128,128]{3,2,1,0:T(8,128)(2,1)}, u32[]{:S(2)}, u32[]{:S(2)}) collective-permute-start(bf16[2,16,128,128]{3,2,1,0:T(8,128)(2,1)S(1)} %collective-permute-done.1.refs_10_.refs_15_.refs_11_), channel_id=1, source_target_pairs={{4,0},{12,8},{5,1},{13,9},{6,2},{14,10},{7,3},{15,11},{20,16},{28,... | collective-permute-start | bytes 3145736 | tf_op jit(solution)/shard_map/ppermute | solution.py:696
  29.6 3.5 %shard_map.203 = bf16[8,128,128]{2,1,0:T(8,128)(2,1)S(1)} custom-call(f32[256,128]{1,0:T(8,128)S(1)} %get-tuple-element.36.refs_0_, f32[64,128]{1,0:T(8,128)S(1)} %copy-done.26, f32[64,64]{1,0:T(8,128)S(1)} %copy-done.10, bf16[4,16,128,128]{3,2,1,0:T(8,128)(2,1)S(1)} %pack.1.refs_3_.refs_8_.refs_13_.refs_9_, ...), custom_call_target="tpu_custom_call" | custom-call | tf_op jit(solution)/shard_map/pallas_call | solution.py:765
  33.8 1.6 collective-permute-start.3
  35.6 5.9 %all-to-all-start.1 = ((bf16[8,128,128]{2,1,0:T(8,128)(2,1)}), bf16[8,128,128]{2,1,0:T(8,128)(2,1)S(1)}, u32[]{:S(2)}, u32[]{:S(2)}) async-start(bf16[8,128,128]{2,1,0:T(8,128)(2,1)} %copy-done.23), calls=%async_computation.1 | async-start | bytes 524288 | tf_op jit(solution)/shard_map/all_to_all | solution.py:749
  42.1 7.7 %all-to-all-done.1.refs_0_ = bf16[8,128,128]{2,1,0:T(8,128)(2,1)S(1)} async-done(((bf16[8,128,128]{2,1,0:T(8,128)(2,1)}), bf16[8,128,128]{2,1,0:T(8,128)(2,1)S(1)}, u32[]{:S(2)}, u32[]{:S(2)}) %all-to-all-start.1) | async-done | bytes 262176 | tf_op jit(solution)/shard_map/all_to_all | solution.py:749
  50.5 4.7 %shard_map.204 = (bf16[16,128,256]{2,1,0:T(8,128)(2,1)S(1)}, bf16[16,128,256]{2,1,0:T(8,128)(2,1)S(1)}, f32[256,128]{1,0:T(8,128)S(1)}, bf16[8,64,128]{2,1,0:T(8,128)(2,1)S(1)}) custom-call(bf16[8,128,128]{2,1,0:T(8,128)(2,1)S(1)} %all-to-all-done.1.refs_0_, bf16[16,128,256]{2,1,0:T(8,128)(2,1)S(1)} %copy-done.8, ...), custom_call_target="tpu_custom_call" | custom-call | tf_op jit(solution)/shard_map/pallas_call | solution.py:765
  57.7 9.3 %all_to_all.40.refs_0_ = bf16[8,64,128]{2,1,0:T(8,128)(2,1)S(1)} all-to-all(bf16[8,64,128]{2,1,0:T(8,128)(2,1)S(1)} %get-tuple-element.39), channel_id=1, replica_groups={{0,1,2,3,8,9,10,11},{4,5,6,7,12,13,14,15},{16,17,18,19,24,25,26,27},{20..., dimensions={0} | all-to-all | bytes 262144 | tf_op jit(solution)/shard_map/all_to_all | solution.py:749
  67.0 4.7 %shard_map.205 = (bf16[16,128,256]{2,1,0:T(8,128)(2,1)S(1)}, bf16[16,128,256]{2,1,0:T(8,128)(2,1)S(1)}, f32[256,128]{1,0:T(8,128)S(1)}, bf16[8,64,128]{2,1,0:T(8,128)(2,1)S(1)}) custom-call(bf16[8,64,128]{2,1,0:T(8,128)(2,1)S(1)} %all_to_all.40.refs_0_, bf16[16,128,256]{2,1,0:T(8,128)(2,1)S(1)} %get-tuple-element.40.refs_1_.refs_3_, ...), custom_call_target="tpu_custom_call" | custom-call | tf_op jit(solution)/shard_map/pallas_call | solution.py:765
  73.3 8.8 %all_to_all.41.refs_0_ = bf16[8,64,128]{2,1,0:T(8,128)(2,1)S(1)} all-to-all(bf16[8,64,128]{2,1,0:T(8,128)(2,1)S(1)} %get-tuple-element.44), channel_id=1, replica_groups={{0,1,2,3,8,9,10,11},{4,5,6,7,12,13,14,15},{16,17,18,19,24,25,26,27},{20..., dimensions={0} | all-to-all | bytes 262144 | tf_op jit(solution)/shard_map/all_to_all | solution.py:749
  82.2 5.3 %shard_map.206 = (bf16[16,128,256]{2,1,0:T(8,128)(2,1)S(1)}, bf16[16,128,256]{2,1,0:T(8,128)(2,1)S(1)}, f32[256,128]{1,0:T(8,128)S(1)}, bf16[8,64,128]{2,1,0:T(8,128)(2,1)}) custom-call(bf16[8,64,128]{2,1,0:T(8,128)(2,1)S(1)} %all_to_all.41.refs_0_, bf16[16,128,256]{2,1,0:T(8,128)(2,1)S(1)} %get-tuple-element.45.refs_1_.refs_3_, ...), custom_call_target="tpu_custom_call" | custom-call | tf_op jit(solution)/shard_map/pallas_call | solution.py:765
  89.6 4.7 %all-to-all-start.4 = ((bf16[8,64,128]{2,1,0:T(8,128)(2,1)}), bf16[8,64,128]{2,1,0:T(8,128)(2,1)S(1)}, u32[]{:S(2)}, u32[]{:S(2)}) async-start(bf16[8,64,128]{2,1,0:T(8,128)(2,1)} %get-tuple-element.47), calls=%async_computation.4 | async-start | bytes 262144 | tf_op jit(solution)/shard_map/all_to_all | solution.py:749
  94.6 4.8 %all-to-all-done.4.refs_0_ = bf16[8,64,128]{2,1,0:T(8,128)(2,1)S(1)} async-done(((bf16[8,64,128]{2,1,0:T(8,128)(2,1)}), bf16[8,64,128]{2,1,0:T(8,128)(2,1)S(1)}, u32[]{:S(2)}, u32[]{:S(2)}) %all-to-all-start.4) | async-done | bytes 131104 | tf_op jit(solution)/shard_map/all_to_all | solution.py:749
  100.1 1.2 copy-done.25
  102.9 8.8 %shard_map.207 = (bf16[16,128,256]{2,1,0:T(8,128)(2,1)S(1)}, f32[256,128]{1,0:T(8,128)S(1)}, f32[128,128]{1,0:T(8,128)S(1)}, bf16[8,64,128]{2,1,0:T(8,128)(2,1)}) custom-call(bf16[8,64,128]{2,1,0:T(8,128)(2,1)S(1)} %copy-done.28, bf16[16,128,256]{2,1,0:T(8,128)(2,1)S(1)} %copy-done.25, bf16[16,24,256]{2,1,0:T(8,128)(2,1)S(1)} %all-to-all-done.refs_0_.refs_2_, ...), custom_call_target="tpu_custom_call" | custom-call | tf_op jit(solution)/shard_map/pallas_call | solution.py:765
  112.7 4.6 %all-to-all-start.5 = ((bf16[8,64,128]{2,1,0:T(8,128)(2,1)}), bf16[8,64,128]{2,1,0:T(8,128)(2,1)S(1)}, u32[]{:S(2)}, u32[]{:S(2)}) async-start(bf16[8,64,128]{2,1,0:T(8,128)(2,1)} %get-tuple-element.49), calls=%async_computation.5 | async-start | bytes 262144 | tf_op jit(solution)/shard_map/all_to_all | solution.py:749
  117.4 5.1 %all-to-all-done.5.refs_0_ = bf16[8,64,128]{2,1,0:T(8,128)(2,1)S(1)} async-done(((bf16[8,64,128]{2,1,0:T(8,128)(2,1)}), bf16[8,64,128]{2,1,0:T(8,128)(2,1)S(1)}, u32[]{:S(2)}, u32[]{:S(2)}) %all-to-all-start.5) | async-done | bytes 131104 | tf_op jit(solution)/shard_map/all_to_all | solution.py:749
  122.5 1.2 copy-done.6
  123.7 1.2 copy-done.20
  124.9 1.2 copy-done.22
  126.1 4.7 %shard_map.208 = (bf16[16,128,256]{2,1,0:T(8,128)(2,1)S(1)}, f32[256,128]{1,0:T(8,128)S(1)}, f32[128,128]{1,0:T(8,128)S(1)}, bf16[8,64,128]{2,1,0:T(8,128)(2,1)S(1)}) custom-call(bf16[8,64,128]{2,1,0:T(8,128)(2,1)S(1)} %all-to-all-done.5.refs_0_, bf16[16,128,256]{2,1,0:T(8,128)(2,1)S(1)} %copy-done.22, bf16[16,128,256]{2,1,0:T(8,128)(2,1)S(1)} %copy-done.20, ...), custom_call_target="tpu_custom_call" | custom-call | tf_op jit(solution)/shard_map/pallas_call | solution.py:765
  130.8 8.8 %all_to_all.42.refs_0_ = bf16[8,64,128]{2,1,0:T(8,128)(2,1)S(1)} all-to-all(bf16[8,64,128]{2,1,0:T(8,128)(2,1)S(1)} %get-tuple-element.52), channel_id=1, replica_groups={{0,1,2,3,8,9,10,11},{4,5,6,7,12,13,14,15},{16,17,18,19,24,25,26,27},{20..., dimensions={0} | all-to-all | bytes 262144 | tf_op jit(solution)/shard_map/all_to_all | solution.py:749
  139.6 4.8 %shard_map.209 = (bf16[16,128,256]{2,1,0:T(8,128)(2,1)S(1)}, f32[256,128]{1,0:T(8,128)S(1)}, f32[128,128]{1,0:T(8,128)S(1)}, bf16[8,64,128]{2,1,0:T(8,128)(2,1)S(1)}) custom-call(bf16[8,64,128]{2,1,0:T(8,128)(2,1)S(1)} %all_to_all.42.refs_0_, bf16[16,128,256]{2,1,0:T(8,128)(2,1)S(1)} %get-tuple-element.53.refs_1_, bf16[16,128,256]{2,1,0:T(8,128)(2,1)S(1)} %copy-done.18, ...), custom_call_target="tpu_custom_call" | custom-call | tf_op jit(solution)/shard_map/pallas_call | solution.py:765
  144.4 8.7 %all_to_all.43.refs_0_ = bf16[8,64,128]{2,1,0:T(8,128)(2,1)S(1)} all-to-all(bf16[8,64,128]{2,1,0:T(8,128)(2,1)S(1)} %get-tuple-element.55), channel_id=1, replica_groups={{0,1,2,3,8,9,10,11},{4,5,6,7,12,13,14,15},{16,17,18,19,24,25,26,27},{20..., dimensions={0} | all-to-all | bytes 262144 | tf_op jit(solution)/shard_map/all_to_all | solution.py:749
  153.1 4.2 %shard_map.210 = (bf16[16,128,256]{2,1,0:T(8,128)(2,1)}, f32[256,128]{1,0:T(8,128)S(1)}, f32[128,128]{1,0:T(8,128)S(1)}, bf16[8,64,128]{2,1,0:T(8,128)(2,1)}) custom-call(bf16[8,64,128]{2,1,0:T(8,128)(2,1)S(1)} %all_to_all.43.refs_0_, bf16[16,128,256]{2,1,0:T(8,128)(2,1)S(1)} %get-tuple-element.56.refs_1_, bf16[16,128,256]{2,1,0:T(8,128)(2,1)S(1)} %copy-done.16, ...), custom_call_target="tpu_custom_call" | custom-call | tf_op jit(solution)/shard_map/pallas_call | solution.py:765
  157.5 8.6 %collective-permute-start.5 = (f32[576,128]{1,0:T(8,128)S(1)}, f32[576,128]{1,0:T(8,128)S(1)}, u32[]{:S(2)}, u32[]{:S(2)}) collective-permute-start(f32[576,128]{1,0:T(8,128)S(1)} %get-tuple-element.67), channel_id=1, source_target_pairs={{0,4},{4,0},{8,12},{12,8},{1,5},{5,1},{9,13},{13,9},{2,6},{6,2},{1... | collective-permute-start | bytes 884744 | tf_op jit(solution)/shard_map/ppermute | solution.py:856
  166.1 1.2 collective-permute-done.5.theirs_ref
  167.4 5.6 %grads.1 = (f32[4,32,2,64,64]{4,3,2,1,0:T(8,128)}, f32[64,64]{1,0:T(8,128)}) custom-call(f32[576,128]{1,0:T(8,128)S(1)} %get-tuple-element.66.mine_ref, f32[576,128]{1,0:T(8,128)S(1)} %collective-permute-done.5.theirs_ref, f32[64,64]{1,0:T(8,128)S(1)} %copy-done.11, f32[64,64]{1,0:T(8,128)S(1)} %copy-done.11), custom_call_target="tpu_custom_call" | custom-call | tf_op jit(solution)/shard_map/grads/pallas_call | solution.py:858
  (133 shorter events, 18.5 us)
Async XLA Ops:
  4.0 29.1 %copy-start.1 = (bf16[4,16,128,128]{3,2,1,0:T(8,128)(2,1)}, bf16[4,16,128,128]{3,2,1,0:T(8,128)(2,1)S(1)}, u32[]{:S(2)}) copy-start(bf16[4,16,128,128]{3,2,1,0:T(8,128)(2,1)S(1)} %pack.1.refs_3_.refs_8_.refs_13_.refs_9_) | copy-start | bytes 6291460
  4.0 11.8 %copy-start.48 = (f32[64]{0:T(128)S(1)}, f32[64]{0:T(128)}, u32[]{:S(2)}) copy-start(f32[64]{0:T(128)} %param.23) | copy-start | bytes 772
  4.0 12.6 %copy-start.45 = (bf16[8,64]{1,0:T(8,128)(2,1)S(1)}, bf16[8,64]{1,0:T(8,128)(2,1)}, u32[]{:S(2)}) copy-start(bf16[8,64]{1,0:T(8,128)(2,1)} %param.22) | copy-start | bytes 3076
  4.0 19.9 %copy-start.13 = (bf16[8,16,256]{2,1,0:T(8,128)(2,1)S(1)}, bf16[8,16,256]{2,1,0:T(8,128)(2,1)}, u32[]{:S(2)}) copy-start(bf16[8,16,256]{2,1,0:T(8,128)(2,1)} %constant.56.clone.refs_3_.refs_5_) | copy-start | bytes 196612
  4.0 25.6 %copy-start.10 = (f32[64,64]{1,0:T(8,128)S(1)}, f32[64,64]{1,0:T(8,128)}, u32[]{:S(2)}) copy-start(f32[64,64]{1,0:T(8,128)} %constant.60.clone.refs_2_.refs_7_.refs_12_.refs_8_) | copy-start | bytes 49156
  4.0 25.5 %copy-start.26 = (f32[64,128]{1,0:T(8,128)S(1)}, f32[64,128]{1,0:T(8,128)}, u32[]{:S(2)}) copy-start(f32[64,128]{1,0:T(8,128)} %constant.58.clone.refs_1_.refs_6_) | copy-start | bytes 98308
  4.1 25.5 %collective-permute-start = (bf16[4,16,128,128]{3,2,1,0:T(8,128)(2,1)S(1)}, bf16[4,16,128,128]{3,2,1,0:T(8,128)(2,1)}, u32[]{:S(2)}, u32[]{:S(2)}) collective-permute-start(bf16[4,16,128,128]{3,2,1,0:T(8,128)(2,1)S(1)} %pack.1.refs_3_.refs_8_.refs_13_.refs_9_), channel_id=1, source_target_pairs={{0,4},{4,0},{8,12},{12,8},{1,5},{5,1},{9,13},{13,9},{2,6},{6,2},{1... | collective-permute-start | bytes 6291464 | tf_op jit(solution)/shard_map/ppermute | solution.py:689
  5.9 20.4 %collective-permute-start.1 = (bf16[2,16,128,128]{3,2,1,0:T(8,128)(2,1)}, bf16[2,16,128,128]{3,2,1,0:T(8,128)(2,1)S(1)}, u32[]{:S(2)}, u32[]{:S(2)}) collective-permute-start(bf16[2,16,128,128]{3,2,1,0:T(8,128)(2,1)} %constant_dynamic-slice_fusion), channel_id=1, source_target_pairs={{4,12},{12,4},{5,13},{13,5},{6,14},{14,6},{7,15},{15,7},{20,28},{2... | collective-permute-start | bytes 3145736 | tf_op jit(solution)/shard_map/ppermute | solution.py:691
  9.4 14.5 %all-to-all-start = ((bf16[16,24,256]{2,1,0:T(8,128)(2,1)}), bf16[16,24,256]{2,1,0:T(8,128)(2,1)S(1)}, u32[]{:S(2)}, u32[]{:S(2)}) async-start(bf16[16,24,256]{2,1,0:T(8,128)(2,1)} %bitcast.22), calls=%async_computation | async-start | bytes 393216 | tf_op jit(solution)/shard_map/all_to_all | solution.py:693
  26.3 15.8 %collective-permute-start.2 = (bf16[2,16,128,128]{3,2,1,0:T(8,128)(2,1)S(1)}, bf16[2,16,128,128]{3,2,1,0:T(8,128)(2,1)}, u32[]{:S(2)}, u32[]{:S(2)}) collective-permute-start(bf16[2,16,128,128]{3,2,1,0:T(8,128)(2,1)S(1)} %collective-permute-done.1.refs_10_.refs_15_.refs_11_), channel_id=1, source_target_pairs={{4,0},{12,8},{5,1},{13,9},{6,2},{14,10},{7,3},{15,11},{20,16},{28,... | collective-permute-start | bytes 3145736 | tf_op jit(solution)/shard_map/ppermute | solution.py:696
  33.8 23.2 %collective-permute-start.3 = (bf16[2,16,128,128]{3,2,1,0:T(8,128)(2,1)}, bf16[2,16,128,128]{3,2,1,0:T(8,128)(2,1)}, u32[]{:S(2)}, u32[]{:S(2)}) collective-permute-start(bf16[2,16,128,128]{3,2,1,0:T(8,128)(2,1)} %constant_dynamic-slice_fusion), channel_id=1, source_target_pairs={{8,0},{9,1},{10,2},{11,3},{24,16},{25,17},{26,18},{27,19}} | collective-permute-start | bytes 3145736 | tf_op jit(solution)/shard_map/ppermute | solution.py:806
  35.4 14.4 %copy-start.8 = (bf16[16,128,256]{2,1,0:T(8,128)(2,1)S(1)}, bf16[16,128,256]{2,1,0:T(8,128)(2,1)}, u32[]{:S(2)}) copy-start(bf16[16,128,256]{2,1,0:T(8,128)(2,1)} %copy-done.7) | copy-start | bytes 3145732
  35.6 14.2 %all-to-all-start.1 = ((bf16[8,128,128]{2,1,0:T(8,128)(2,1)}), bf16[8,128,128]{2,1,0:T(8,128)(2,1)S(1)}, u32[]{:S(2)}, u32[]{:S(2)}) async-start(bf16[8,128,128]{2,1,0:T(8,128)(2,1)} %copy-done.23), calls=%async_computation.1 | async-start | bytes 524288 | tf_op jit(solution)/shard_map/all_to_all | solution.py:749
  50.5 16.4 %copy-start.33 = (bf16[32,256]{1,0:T(8,128)(2,1)S(1)}, bf16[32,256]{1,0:T(8,128)(2,1)}, u32[]{:S(2)}) copy-start(bf16[32,256]{1,0:T(8,128)(2,1)} %constant.54.clone.refs_4_.refs_5_) | copy-start | bytes 49156
  56.9 14.7 %copy-start.3 = (bf16[16,128,256]{2,1,0:T(8,128)(2,1)}, bf16[16,128,256]{2,1,0:T(8,128)(2,1)S(1)}, u32[]{:S(2)}) copy-start(bf16[16,128,256]{2,1,0:T(8,128)(2,1)S(1)} %get-tuple-element.40.refs_1_.refs_3_) | copy-start | bytes 3145732
  56.9 10.0 %collective-permute-start.4 = (bf16[2,16,128,128]{3,2,1,0:T(8,128)(2,1)}, bf16[2,16,128,128]{3,2,1,0:T(8,128)(2,1)S(1)}, u32[]{:S(2)}, u32[]{:S(2)}) collective-permute-start(bf16[2,16,128,128]{3,2,1,0:T(8,128)(2,1)} %collective-permute-done.3.refs_10_.refs_11_), channel_id=1, source_target_pairs={{0,4},{1,5},{2,6},{3,7},{16,20},{17,21},{18,22},{19,23}} | collective-permute-start | bytes 3145736 | tf_op jit(solution)/shard_map/ppermute | solution.py:823
  67.0 15.2 %copy-start.14 = (bf16[8,16,256]{2,1,0:T(8,128)(2,1)S(1)}, bf16[8,16,256]{2,1,0:T(8,128)(2,1)}, u32[]{:S(2)}) copy-start(bf16[8,16,256]{2,1,0:T(8,128)(2,1)} %constant.56.clone.refs_3_.refs_5_) | copy-start | bytes 196612
  73.3 14.2 %copy-start.5 = (bf16[16,128,256]{2,1,0:T(8,128)(2,1)}, bf16[16,128,256]{2,1,0:T(8,128)(2,1)S(1)}, u32[]{:S(2)}) copy-start(bf16[16,128,256]{2,1,0:T(8,128)(2,1)S(1)} %get-tuple-element.45.refs_1_.refs_3_) | copy-start | bytes 3145732
  82.1 12.1 %copy-start.49 = (bf16[128]{0:T(256)(128)(2,1)S(1)}, bf16[128]{0:T(256)(128)(2,1)}, u32[]{:S(2)}) copy-start(bf16[128]{0:T(256)(128)(2,1)} %param.29) | copy-start | bytes 772
  82.1 12.2 %copy-start.46 = (f32[128]{0:T(128)S(1)}, f32[128]{0:T(128)}, u32[]{:S(2)}) copy-start(f32[128]{0:T(128)} %param.28) | copy-start | bytes 1540
  82.1 12.3 %copy-start.41 = (bf16[64,128]{1,0:T(8,128)(2,1)S(1)}, bf16[64,128]{1,0:T(8,128)(2,1)}, u32[]{:S(2)}) copy-start(bf16[64,128]{1,0:T(8,128)(2,1)} %refs_8_.4) | copy-start | bytes 49156
  82.1 17.9 %copy-start.11 = (f32[64,64]{1,0:T(8,128)S(1)}, f32[64,64]{1,0:T(8,128)}, u32[]{:S(2)}) copy-start(f32[64,64]{1,0:T(8,128)} %constant.59.clone.refs_11_.refs_7_.xz_ref.xa_ref) | copy-start | bytes 49156
  82.1 17.9 %copy-start.12 = (bf16[8,16,256]{2,1,0:T(8,128)(2,1)S(1)}, bf16[8,16,256]{2,1,0:T(8,128)(2,1)}, u32[]{:S(2)}) copy-start(bf16[8,16,256]{2,1,0:T(8,128)(2,1)} %constant.57.clone.refs_10_.refs_6_) | copy-start | bytes 196612
  89.6 10.5 %copy-start.38 = (f32[256,128]{1,0:T(8,128)}, f32[256,128]{1,0:T(8,128)S(1)}, u32[]{:S(2)}) copy-start(f32[256,128]{1,0:T(8,128)S(1)} %get-tuple-element.46.refs_3_) | copy-start | bytes 393220
  89.6 9.8 %all-to-all-start.4 = ((bf16[8,64,128]{2,1,0:T(8,128)(2,1)}), bf16[8,64,128]{2,1,0:T(8,128)(2,1)S(1)}, u32[]{:S(2)}, u32[]{:S(2)}) async-start(bf16[8,64,128]{2,1,0:T(8,128)(2,1)} %get-tuple-element.47), calls=%async_computation.4 | async-start | bytes 262144 | tf_op jit(solution)/shard_map/all_to_all | solution.py:749
  102.9 19.6 %copy-start.32 = (bf16[32,256]{1,0:T(8,128)(2,1)S(1)}, bf16[32,256]{1,0:T(8,128)(2,1)}, u32[]{:S(2)}) copy-start(bf16[32,256]{1,0:T(8,128)(2,1)} %constant.55.clone.refs_5_) | copy-start | bytes 49156
  112.7 9.8 %all-to-all-start.5 = ((bf16[8,64,128]{2,1,0:T(8,128)(2,1)}), bf16[8,64,128]{2,1,0:T(8,128)(2,1)S(1)}, u32[]{:S(2)}, u32[]{:S(2)}) async-start(bf16[8,64,128]{2,1,0:T(8,128)(2,1)} %get-tuple-element.49), calls=%async_computation.5 | async-start | bytes 262144 | tf_op jit(solution)/shard_map/all_to_all | solution.py:749
  126.1 13.5 %copy-start.4 = (bf16[16,128,256]{2,1,0:T(8,128)(2,1)S(1)}, bf16[16,128,256]{2,1,0:T(8,128)(2,1)}, u32[]{:S(2)}) copy-start(bf16[16,128,256]{2,1,0:T(8,128)(2,1)} %copy-done.3) | copy-start | bytes 3145732
  126.1 13.5 %copy-start.18 = (bf16[16,128,256]{2,1,0:T(8,128)(2,1)S(1)}, bf16[16,128,256]{2,1,0:T(8,128)(2,1)}, u32[]{:S(2)}) copy-start(bf16[16,128,256]{2,1,0:T(8,128)(2,1)} %copy-done.17) | copy-start | bytes 3145732
  139.6 13.5 %copy-start.9 = (bf16[16,128,256]{2,1,0:T(8,128)(2,1)S(1)}, bf16[16,128,256]{2,1,0:T(8,128)(2,1)}, u32[]{:S(2)}) copy-start(bf16[16,128,256]{2,1,0:T(8,128)(2,1)} %copy-done.7) | copy-start | bytes 3145732
  139.6 13.5 %copy-start.16 = (bf16[16,128,256]{2,1,0:T(8,128)(2,1)S(1)}, bf16[16,128,256]{2,1,0:T(8,128)(2,1)}, u32[]{:S(2)}) copy-start(bf16[16,128,256]{2,1,0:T(8,128)(2,1)} %copy-done.15) | copy-start | bytes 3145732
  157.5 9.8 %collective-permute-start.5 = (f32[576,128]{1,0:T(8,128)S(1)}, f32[576,128]{1,0:T(8,128)S(1)}, u32[]{:S(2)}, u32[]{:S(2)}) collective-permute-start(f32[576,128]{1,0:T(8,128)S(1)} %get-tuple-element.67), channel_id=1, source_target_pairs={{0,4},{4,0},{8,12},{12,8},{1,5},{5,1},{9,13},{13,9},{2,6},{6,2},{1... | collective-permute-start | bytes 884744 | tf_op jit(solution)/shard_map/ppermute | solution.py:856
  (28 other events, 69.0 us)

commit v4 on v3

--- a/solution.py
+++ b/solution.py
@@ -234,7 +234,7 @@
 f32, bf16 = (jnp.float32, jnp.bfloat16)
 NT = (((1,), (1,)), ((), ()))
 NN = (((1,), (0,)), ((), ()))
-VMEM_LIMIT = 48 << 20
+VMEM_LIMIT = 50 << 20
 
 
 def np_y_tables(col_count, mode_count):
@@ -693,7 +693,6 @@
     grid_in = lax.all_to_all(
         chunk.reshape((segments * space,) + chunk.shape[3:]), both, 0, 0, tiled=True
     )
-    across_odd_on = lax.ppermute(across_odd, "segment", [(1, 0), (3, 2)])
 
     def weights_of(layer):
         if layer % 2:
@@ -810,6 +809,9 @@
         recv = to_all(mine)
         table = inv_table
         if layer == 1:
+            across_odd_on = lax.ppermute(
+                lax.optimization_barrier((across_odd, recv))[0], "segment", [(1, 0), (3, 2)]
+            )
             table = jnp.asarray(y_inverse.reshape(2 * mode_count, cols), bf16)
         act, slope, y, mine = call(
             partial(forward_kernel, layer=layer),

time: 176 us -> 181 us (1.028)
  local copies, waits for them, and re-layouts: 21.5 us -> 15.5 us
  Pallas kernels: 50.5 us -> 56.2 us
  starting transfers between devices: 38.4 us -> 41.4 us
  waiting for transfers between devices: 25.3 us -> 27.4 us
    pallas_call x8, Pallas kernels: 40.6 us -> 46.3 us  [call(): pl.pallas_call(placed(kernel), in_specs=[near] * len(args) + [pl.BlockSpe...]
    unnamed x101 -> x77, local copies, waits for them, and re-layouts: 16.7 us -> 11.9 us
    ppermute x1, starting transfers between devices: 8.63 us -> 12.9 us  [replicated(): theirs = lax.ppermute(theirs, 'segment', [(0, 1), (1, 0), (2, 3), (3, 2)])]
  transfers between devices with their start and end apart: 10 -> 10, of which waited for: 5 -> 5; matrix products, arithmetic and copies ran while one was open for 3% -> 2% of each run, Pallas kernels for 5% -> 6%
where the time goes in v4:
time: 181 us; the launch traced here: 178 us
  Pallas kernels  56.2 us (31%)
  starting transfers between devices  41.4 us (23%)
  blocking collectives  35.6 us (20%)
  waiting for transfers between devices  27.4 us (15%)
  local copies, waits for them, and re-layouts  15.5 us (9%)
    pallas_call x8, Pallas kernels, call(): pl.pallas_call(placed(kernel), in_specs=[near] * len(args) + [pl.BlockSpe...  46.3 us
    all_to_all x4, blocking collectives, to_all(): lax.all_to_all(block, both, 0, 0, tiled=True, axis_index_groups=device_li...  35.6 us
    all_to_all x3, waiting for transfers between devices, to_all(): lax.all_to_all(block, both, 0, 0, tiled=True, axis_index_groups=device_li...  18.4 us
    all_to_all x3, starting transfers between devices, to_all(): lax.all_to_all(block, both, 0, 0, tiled=True, axis_index_groups=device_li...  14.8 us
    ppermute x1, starting transfers between devices, replicated(): theirs = lax.ppermute(theirs, 'segment', [(0, 1), (1, 0), (2, 3), (3, 2)])  12.9 us
    unnamed x77, local copies, waits for them, and re-layouts  11.9 us
    all_to_all x1, waiting for transfers between devices, replicated(): lax.all_to_all(chunk.reshape((segments * space,) + chunk.shape[3:]), both...  7.7 us
    all_to_all x1, starting transfers between devices, replicated(): lax.all_to_all(chunk.reshape((segments * space,) + chunk.shape[3:]), both...  6.35 us
  transfers between devices with their start and end apart: 10, of which 5 were waited for; matrix products, arithmetic and copies ran while one was open for 2% of the time, Pallas kernels for 6%

profile of v4, /device:TPU:3, one launch (start us, length us, event | category | flops | bytes accessed | tf_op | source)
XLA Modules:
  0.0 177.6 jit_solution(648625569528851485)
XLA Ops:
  0.6 3.3 %pack.1.refs_3_.refs_8_.refs_13_.refs_9_ = bf16[4,16,128,128]{3,2,1,0:T(8,128)(2,1)S(1)} custom-call(bf16[4,2,16,128,64]{4,3,2,1,0:T(8,128)(2,1)} %bitcast.21), custom_call_target="tpu_custom_call" | custom-call | tf_op jit(solution)/shard_map/pack/pallas_call | solution.py:687
  4.8 1.1 constant_dynamic-slice_fusion
  5.9 1.9 %collective-permute-start.1 = (bf16[2,16,128,128]{3,2,1,0:T(8,128)(2,1)}, bf16[2,16,128,128]{3,2,1,0:T(8,128)(2,1)}, u32[]{:S(2)}, u32[]{:S(2)}) collective-permute-start(bf16[2,16,128,128]{3,2,1,0:T(8,128)(2,1)} %constant_dynamic-slice_fusion), channel_id=1, source_target_pairs={{4,12},{12,4},{5,13},{13,5},{6,14},{14,6},{7,15},{15,7},{20,28},{2... | collective-permute-start | bytes 3145736 | tf_op jit(solution)/shard_map/ppermute | solution.py:691
  9.4 6.3 %all-to-all-start = ((bf16[16,24,256]{2,1,0:T(8,128)(2,1)}), bf16[16,24,256]{2,1,0:T(8,128)(2,1)S(1)}, u32[]{:S(2)}, u32[]{:S(2)}) async-start(bf16[16,24,256]{2,1,0:T(8,128)(2,1)} %bitcast.2), calls=%async_computation | async-start | bytes 393216 | tf_op jit(solution)/shard_map/all_to_all | solution.py:693
  16.2 7.7 %all-to-all-done.refs_0_.refs_2_ = bf16[16,24,256]{2,1,0:T(8,128)(2,1)S(1)} async-done(((bf16[16,24,256]{2,1,0:T(8,128)(2,1)}), bf16[16,24,256]{2,1,0:T(8,128)(2,1)S(1)}, u32[]{:S(2)}, u32[]{:S(2)}) %all-to-all-start) | async-done | bytes 196640 | tf_op jit(solution)/shard_map/all_to_all | solution.py:693
  25.7 4.2 %shard_map.203 = bf16[8,128,128]{2,1,0:T(8,128)(2,1)} custom-call(f32[256,128]{1,0:T(8,128)S(1)} %get-tuple-element.37.refs_0_, f32[64,128]{1,0:T(8,128)S(1)} %copy-done.19, f32[64,64]{1,0:T(8,128)S(1)} %copy-done.5, bf16[4,16,128,128]{3,2,1,0:T(8,128)(2,1)S(1)} %pack.1.refs_3_.refs_8_.refs_13_.refs_9_, ...), custom_call_target="tpu_custom_call" | custom-call | tf_op jit(solution)/shard_map/pallas_call | solution.py:764
  29.8 5.8 %all-to-all-start.1 = ((bf16[8,128,128]{2,1,0:T(8,128)(2,1)}), bf16[8,128,128]{2,1,0:T(8,128)(2,1)S(1)}, u32[]{:S(2)}, u32[]{:S(2)}) async-start(bf16[8,128,128]{2,1,0:T(8,128)(2,1)} %shard_map.203), calls=%async_computation.1 | async-start | bytes 524288 | tf_op jit(solution)/shard_map/all_to_all | solution.py:748
  35.6 8.5 %all-to-all-done.1.refs_0_ = bf16[8,128,128]{2,1,0:T(8,128)(2,1)S(1)} async-done(((bf16[8,128,128]{2,1,0:T(8,128)(2,1)}), bf16[8,128,128]{2,1,0:T(8,128)(2,1)S(1)}, u32[]{:S(2)}, u32[]{:S(2)}) %all-to-all-start.1) | async-done | bytes 262176 | tf_op jit(solution)/shard_map/all_to_all | solution.py:748
  44.2 2.3 %collective-permute-start.2 = (bf16[2,16,128,128]{3,2,1,0:T(8,128)(2,1)}, bf16[2,16,128,128]{3,2,1,0:T(8,128)(2,1)S(1)}, u32[]{:S(2)}, u32[]{:S(2)}) collective-permute-start(bf16[2,16,128,128]{3,2,1,0:T(8,128)(2,1)} %collective-permute-done.1.refs_10_.refs_15_.refs_11_), channel_id=1, source_target_pairs={{4,0},{12,8},{5,1},{13,9},{6,2},{14,10},{7,3},{15,11},{20,16},{28,... | collective-permute-start | bytes 3145736 | tf_op jit(solution)/shard_map/ppermute | solution.py:812
  46.5 1.6 collective-permute-start.3
  48.9 1.0 copy-done.28
  50.0 5.9 %shard_map.204 = (bf16[16,128,256]{2,1,0:T(8,128)(2,1)S(1)}, bf16[16,128,256]{2,1,0:T(8,128)(2,1)S(1)}, f32[256,128]{1,0:T(8,128)S(1)}, bf16[8,64,128]{2,1,0:T(8,128)(2,1)S(1)}) custom-call(bf16[8,128,128]{2,1,0:T(8,128)(2,1)S(1)} %all-to-all-done.1.refs_0_, bf16[16,128,256]{2,1,0:T(8,128)(2,1)} %copy-done.4, bf16[4,128,128]{2,1,0:T(8,128)(2,1)S(1)} %copy.46.refs_2_.refs_3_, ...), custom_call_target="tpu_custom_call" | custom-call | tf_op jit(solution)/shard_map/pallas_call | solution.py:764
  57.6 9.3 %all_to_all.40.refs_0_ = bf16[8,64,128]{2,1,0:T(8,128)(2,1)S(1)} all-to-all(bf16[8,64,128]{2,1,0:T(8,128)(2,1)S(1)} %get-tuple-element.41), channel_id=1, replica_groups={{0,1,2,3,8,9,10,11},{4,5,6,7,12,13,14,15},{16,17,18,19,24,25,26,27},{20..., dimensions={0} | all-to-all | bytes 262144 | tf_op jit(solution)/shard_map/all_to_all | solution.py:748
  67.9 4.7 %shard_map.205 = (bf16[16,128,256]{2,1,0:T(8,128)(2,1)S(1)}, bf16[16,128,256]{2,1,0:T(8,128)(2,1)S(1)}, f32[256,128]{1,0:T(8,128)S(1)}, bf16[8,64,128]{2,1,0:T(8,128)(2,1)S(1)}) custom-call(bf16[8,64,128]{2,1,0:T(8,128)(2,1)S(1)} %all_to_all.40.refs_0_, bf16[16,128,256]{2,1,0:T(8,128)(2,1)S(1)} %get-tuple-element.42.refs_1_.refs_3_, ...), custom_call_target="tpu_custom_call" | custom-call | tf_op jit(solution)/shard_map/pallas_call | solution.py:764
  73.6 8.7 %all_to_all.41.refs_0_ = bf16[8,64,128]{2,1,0:T(8,128)(2,1)S(1)} all-to-all(bf16[8,64,128]{2,1,0:T(8,128)(2,1)S(1)} %get-tuple-element.46), channel_id=1, replica_groups={{0,1,2,3,8,9,10,11},{4,5,6,7,12,13,14,15},{16,17,18,19,24,25,26,27},{20..., dimensions={0} | all-to-all | bytes 262144 | tf_op jit(solution)/shard_map/all_to_all | solution.py:748
  82.4 5.3 %shard_map.206 = (bf16[16,128,256]{2,1,0:T(8,128)(2,1)S(1)}, bf16[16,128,256]{2,1,0:T(8,128)(2,1)S(1)}, f32[256,128]{1,0:T(8,128)S(1)}, bf16[8,64,128]{2,1,0:T(8,128)(2,1)}) custom-call(bf16[8,64,128]{2,1,0:T(8,128)(2,1)S(1)} %all_to_all.41.refs_0_, bf16[16,128,256]{2,1,0:T(8,128)(2,1)S(1)} %get-tuple-element.47.refs_1_.refs_3_, ...), custom_call_target="tpu_custom_call" | custom-call | tf_op jit(solution)/shard_map/pallas_call | solution.py:764
  87.7 1.0 copy-done.13
  89.7 4.5 %all-to-all-start.4 = ((bf16[8,64,128]{2,1,0:T(8,128)(2,1)}), bf16[8,64,128]{2,1,0:T(8,128)(2,1)S(1)}, u32[]{:S(2)}, u32[]{:S(2)}) async-start(bf16[8,64,128]{2,1,0:T(8,128)(2,1)} %get-tuple-element.49), calls=%async_computation.4 | async-start | bytes 262144 | tf_op jit(solution)/shard_map/all_to_all | solution.py:748
  94.6 4.8 %all-to-all-done.4.refs_0_ = bf16[8,64,128]{2,1,0:T(8,128)(2,1)S(1)} async-done(((bf16[8,64,128]{2,1,0:T(8,128)(2,1)}), bf16[8,64,128]{2,1,0:T(8,128)(2,1)S(1)}, u32[]{:S(2)}, u32[]{:S(2)}) %all-to-all-start.4) | async-done | bytes 131104 | tf_op jit(solution)/shard_map/all_to_all | solution.py:748
  99.4 1.2 copy-done.18
  100.6 8.8 %shard_map.207 = (bf16[16,128,256]{2,1,0:T(8,128)(2,1)S(1)}, f32[256,128]{1,0:T(8,128)S(1)}, f32[128,128]{1,0:T(8,128)S(1)}, bf16[8,64,128]{2,1,0:T(8,128)(2,1)}) custom-call(bf16[8,64,128]{2,1,0:T(8,128)(2,1)S(1)} %all-to-all-done.4.refs_0_, bf16[16,128,256]{2,1,0:T(8,128)(2,1)S(1)} %copy-done.18, bf16[16,24,256]{2,1,0:T(8,128)(2,1)S(1)} %all-to-all-done.refs_0_.refs_2_, ...), custom_call_target="tpu_custom_call" | custom-call | tf_op jit(solution)/shard_map/pallas_call | solution.py:764
  111.7 4.5 %all-to-all-start.5 = ((bf16[8,64,128]{2,1,0:T(8,128)(2,1)}), bf16[8,64,128]{2,1,0:T(8,128)(2,1)S(1)}, u32[]{:S(2)}, u32[]{:S(2)}) async-start(bf16[8,64,128]{2,1,0:T(8,128)(2,1)} %get-tuple-element.51), calls=%async_computation.5 | async-start | bytes 262144 | tf_op jit(solution)/shard_map/all_to_all | solution.py:748
  116.3 5.1 %all-to-all-done.5.refs_0_ = bf16[8,64,128]{2,1,0:T(8,128)(2,1)S(1)} async-done(((bf16[8,64,128]{2,1,0:T(8,128)(2,1)}), bf16[8,64,128]{2,1,0:T(8,128)(2,1)S(1)}, u32[]{:S(2)}, u32[]{:S(2)}) %all-to-all-start.5) | async-done | bytes 131104 | tf_op jit(solution)/shard_map/all_to_all | solution.py:748
  121.4 1.2 copy-done.16
  122.6 6.0 %shard_map.208 = (bf16[16,128,256]{2,1,0:T(8,128)(2,1)S(1)}, f32[256,128]{1,0:T(8,128)S(1)}, f32[128,128]{1,0:T(8,128)S(1)}, bf16[8,64,128]{2,1,0:T(8,128)(2,1)S(1)}) custom-call(bf16[8,64,128]{2,1,0:T(8,128)(2,1)S(1)} %all-to-all-done.5.refs_0_, bf16[16,128,256]{2,1,0:T(8,128)(2,1)S(1)} %copy-done.16, bf16[16,128,256]{2,1,0:T(8,128)(2,1)S(1)} %copy-done.14, ...), custom_call_target="tpu_custom_call" | custom-call | tf_op jit(solution)/shard_map/pallas_call | solution.py:764
  128.6 8.8 %all_to_all.42.refs_0_ = bf16[8,64,128]{2,1,0:T(8,128)(2,1)S(1)} all-to-all(bf16[8,64,128]{2,1,0:T(8,128)(2,1)S(1)} %get-tuple-element.54), channel_id=1, replica_groups={{0,1,2,3,8,9,10,11},{4,5,6,7,12,13,14,15},{16,17,18,19,24,25,26,27},{20..., dimensions={0} | all-to-all | bytes 262144 | tf_op jit(solution)/shard_map/all_to_all | solution.py:748
  137.4 6.0 %shard_map.209 = (bf16[16,128,256]{2,1,0:T(8,128)(2,1)S(1)}, f32[256,128]{1,0:T(8,128)S(1)}, f32[128,128]{1,0:T(8,128)S(1)}, bf16[8,64,128]{2,1,0:T(8,128)(2,1)S(1)}) custom-call(bf16[8,64,128]{2,1,0:T(8,128)(2,1)S(1)} %all_to_all.42.refs_0_, bf16[16,128,256]{2,1,0:T(8,128)(2,1)S(1)} %get-tuple-element.55.refs_1_, bf16[16,128,256]{2,1,0:T(8,128)(2,1)S(1)} %copy-done.12, ...), custom_call_target="tpu_custom_call" | custom-call | tf_op jit(solution)/shard_map/pallas_call | solution.py:764
  143.3 8.8 %all_to_all.43.refs_0_ = bf16[8,64,128]{2,1,0:T(8,128)(2,1)S(1)} all-to-all(bf16[8,64,128]{2,1,0:T(8,128)(2,1)S(1)} %get-tuple-element.57), channel_id=1, replica_groups={{0,1,2,3,8,9,10,11},{4,5,6,7,12,13,14,15},{16,17,18,19,24,25,26,27},{20..., dimensions={0} | all-to-all | bytes 262144 | tf_op jit(solution)/shard_map/all_to_all | solution.py:748
  152.1 5.5 %shard_map.210 = (bf16[16,128,256]{2,1,0:T(8,128)(2,1)}, f32[256,128]{1,0:T(8,128)S(1)}, f32[128,128]{1,0:T(8,128)S(1)}, bf16[8,64,128]{2,1,0:T(8,128)(2,1)}) custom-call(bf16[8,64,128]{2,1,0:T(8,128)(2,1)S(1)} %all_to_all.43.refs_0_, bf16[16,128,256]{2,1,0:T(8,128)(2,1)S(1)} %get-tuple-element.58.refs_1_, bf16[16,128,256]{2,1,0:T(8,128)(2,1)S(1)} %copy-done.10, ...), custom_call_target="tpu_custom_call" | custom-call | tf_op jit(solution)/shard_map/pallas_call | solution.py:764
  157.8 12.9 %collective-permute-start.5 = (f32[576,128]{1,0:T(8,128)S(1)}, f32[576,128]{1,0:T(8,128)S(1)}, u32[]{:S(2)}, u32[]{:S(2)}) collective-permute-start(f32[576,128]{1,0:T(8,128)S(1)} %get-tuple-element.69), channel_id=1, source_target_pairs={{0,4},{4,0},{8,12},{12,8},{1,5},{5,1},{9,13},{13,9},{2,6},{6,2},{1... | collective-permute-start | bytes 884744 | tf_op jit(solution)/shard_map/ppermute | solution.py:858
  170.8 1.2 collective-permute-done.5.theirs_ref
  172.0 5.6 %grads.1 = (f32[4,32,2,64,64]{4,3,2,1,0:T(8,128)}, f32[64,64]{1,0:T(8,128)}) custom-call(f32[576,128]{1,0:T(8,128)S(1)} %get-tuple-element.68.mine_ref, f32[576,128]{1,0:T(8,128)S(1)} %collective-permute-done.5.theirs_ref, f32[64,64]{1,0:T(8,128)S(1)} %copy-done.6, f32[64,64]{1,0:T(8,128)S(1)} %copy-done.6), custom_call_target="tpu_custom_call" | custom-call | tf_op jit(solution)/shard_map/grads/pallas_call | solution.py:860
  (109 shorter events, 12.9 us)
Async XLA Ops:
  0.6 7.4 %copy-start = (bf16[2,8,8,256]{3,2,1,0:T(8,128)(2,1)S(1)}, bf16[2,8,8,256]{3,2,1,0:T(8,128)(2,1)}, u32[]{:S(2)}) copy-start(bf16[2,8,8,256]{3,2,1,0:T(8,128)(2,1)} %param.20) | copy-start | bytes 196612
  4.0 25.9 %copy-start.1 = (bf16[4,16,128,128]{3,2,1,0:T(8,128)(2,1)}, bf16[4,16,128,128]{3,2,1,0:T(8,128)(2,1)S(1)}, u32[]{:S(2)}) copy-start(bf16[4,16,128,128]{3,2,1,0:T(8,128)(2,1)S(1)} %pack.1.refs_3_.refs_8_.refs_13_.refs_9_) | copy-start | bytes 6291460
  4.0 11.8 %copy-start.36 = (f32[64]{0:T(128)S(1)}, f32[64]{0:T(128)}, u32[]{:S(2)}) copy-start(f32[64]{0:T(128)} %param.23) | copy-start | bytes 772
  4.0 12.0 %copy-start.33 = (bf16[8,64]{1,0:T(8,128)(2,1)S(1)}, bf16[8,64]{1,0:T(8,128)(2,1)}, u32[]{:S(2)}) copy-start(bf16[8,64]{1,0:T(8,128)(2,1)} %param.22) | copy-start | bytes 3076
  4.0 19.9 %copy-start.8 = (bf16[8,16,256]{2,1,0:T(8,128)(2,1)S(1)}, bf16[8,16,256]{2,1,0:T(8,128)(2,1)}, u32[]{:S(2)}) copy-start(bf16[8,16,256]{2,1,0:T(8,128)(2,1)} %constant.56.clone.refs_3_.refs_5_) | copy-start | bytes 196612
  4.0 21.6 %copy-start.5 = (f32[64,64]{1,0:T(8,128)S(1)}, f32[64,64]{1,0:T(8,128)}, u32[]{:S(2)}) copy-start(f32[64,64]{1,0:T(8,128)} %constant.60.clone.refs_2_.refs_7_.refs_12_.refs_8_) | copy-start | bytes 49156
  4.0 21.6 %copy-start.19 = (f32[64,128]{1,0:T(8,128)S(1)}, f32[64,128]{1,0:T(8,128)}, u32[]{:S(2)}) copy-start(f32[64,128]{1,0:T(8,128)} %constant.58.clone.refs_1_.refs_6_) | copy-start | bytes 98308
  4.1 21.6 %collective-permute-start = (bf16[4,16,128,128]{3,2,1,0:T(8,128)(2,1)S(1)}, bf16[4,16,128,128]{3,2,1,0:T(8,128)(2,1)}, u32[]{:S(2)}, u32[]{:S(2)}) collective-permute-start(bf16[4,16,128,128]{3,2,1,0:T(8,128)(2,1)S(1)} %pack.1.refs_3_.refs_8_.refs_13_.refs_9_), channel_id=1, source_target_pairs={{0,4},{4,0},{8,12},{12,8},{1,5},{5,1},{9,13},{13,9},{2,6},{6,2},{1... | collective-permute-start | bytes 6291464 | tf_op jit(solution)/shard_map/ppermute | solution.py:689
  5.9 29.8 %collective-permute-start.1 = (bf16[2,16,128,128]{3,2,1,0:T(8,128)(2,1)}, bf16[2,16,128,128]{3,2,1,0:T(8,128)(2,1)}, u32[]{:S(2)}, u32[]{:S(2)}) collective-permute-start(bf16[2,16,128,128]{3,2,1,0:T(8,128)(2,1)} %constant_dynamic-slice_fusion), channel_id=1, source_target_pairs={{4,12},{12,4},{5,13},{13,5},{6,14},{14,6},{7,15},{15,7},{20,28},{2... | collective-permute-start | bytes 3145736 | tf_op jit(solution)/shard_map/ppermute | solution.py:691
  9.4 14.5 %all-to-all-start = ((bf16[16,24,256]{2,1,0:T(8,128)(2,1)}), bf16[16,24,256]{2,1,0:T(8,128)(2,1)S(1)}, u32[]{:S(2)}, u32[]{:S(2)}) async-start(bf16[16,24,256]{2,1,0:T(8,128)(2,1)} %bitcast.2), calls=%async_computation | async-start | bytes 393216 | tf_op jit(solution)/shard_map/all_to_all | solution.py:693
  25.7 24.3 %copy-start.27 = (bf16[32,256]{1,0:T(8,128)(2,1)S(1)}, bf16[32,256]{1,0:T(8,128)(2,1)}, u32[]{:S(2)}) copy-start(bf16[32,256]{1,0:T(8,128)(2,1)} %constant.61.clone.refs_4_) | copy-start | bytes 49156
  29.8 14.3 %all-to-all-start.1 = ((bf16[8,128,128]{2,1,0:T(8,128)(2,1)}), bf16[8,128,128]{2,1,0:T(8,128)(2,1)S(1)}, u32[]{:S(2)}, u32[]{:S(2)}) async-start(bf16[8,128,128]{2,1,0:T(8,128)(2,1)} %shard_map.203), calls=%async_computation.1 | async-start | bytes 524288 | tf_op jit(solution)/shard_map/all_to_all | solution.py:748
  44.2 4.8 %collective-permute-start.2 = (bf16[2,16,128,128]{3,2,1,0:T(8,128)(2,1)}, bf16[2,16,128,128]{3,2,1,0:T(8,128)(2,1)S(1)}, u32[]{:S(2)}, u32[]{:S(2)}) collective-permute-start(bf16[2,16,128,128]{3,2,1,0:T(8,128)(2,1)} %collective-permute-done.1.refs_10_.refs_15_.refs_11_), channel_id=1, source_target_pairs={{4,0},{12,8},{5,1},{13,9},{6,2},{14,10},{7,3},{15,11},{20,16},{28,... | collective-permute-start | bytes 3145736 | tf_op jit(solution)/shard_map/ppermute | solution.py:812
  46.5 10.4 %collective-permute-start.3 = (bf16[2,16,128,128]{3,2,1,0:T(8,128)(2,1)}, bf16[2,16,128,128]{3,2,1,0:T(8,128)(2,1)}, u32[]{:S(2)}, u32[]{:S(2)}) collective-permute-start(bf16[2,16,128,128]{3,2,1,0:T(8,128)(2,1)} %constant_dynamic-slice_fusion), channel_id=1, source_target_pairs={{8,0},{9,1},{10,2},{11,3},{24,16},{25,17},{26,18},{27,19}} | collective-permute-start | bytes 3145736 | tf_op jit(solution)/shard_map/ppermute | solution.py:805
  50.0 18.0 %copy-start.21 = (bf16[32,256]{1,0:T(8,128)(2,1)S(1)}, bf16[32,256]{1,0:T(8,128)(2,1)}, u32[]{:S(2)}) copy-start(bf16[32,256]{1,0:T(8,128)(2,1)} %constant.54.clone.refs_4_.refs_5_) | copy-start | bytes 49156
  56.9 15.7 %copy-start.2 = (bf16[16,128,256]{2,1,0:T(8,128)(2,1)}, bf16[16,128,256]{2,1,0:T(8,128)(2,1)S(1)}, u32[]{:S(2)}) copy-start(bf16[16,128,256]{2,1,0:T(8,128)(2,1)S(1)} %get-tuple-element.42.refs_1_.refs_3_) | copy-start | bytes 3145732
  56.9 10.0 %collective-permute-start.4 = (bf16[2,16,128,128]{3,2,1,0:T(8,128)(2,1)}, bf16[2,16,128,128]{3,2,1,0:T(8,128)(2,1)S(1)}, u32[]{:S(2)}, u32[]{:S(2)}) collective-permute-start(bf16[2,16,128,128]{3,2,1,0:T(8,128)(2,1)} %collective-permute-done.3.refs_10_.refs_11_), channel_id=1, source_target_pairs={{0,4},{1,5},{2,6},{3,7},{16,20},{17,21},{18,22},{19,23}} | collective-permute-start | bytes 3145736 | tf_op jit(solution)/shard_map/ppermute | solution.py:825
  73.6 14.1 %copy-start.3 = (bf16[16,128,256]{2,1,0:T(8,128)(2,1)}, bf16[16,128,256]{2,1,0:T(8,128)(2,1)S(1)}, u32[]{:S(2)}) copy-start(bf16[16,128,256]{2,1,0:T(8,128)(2,1)S(1)} %get-tuple-element.47.refs_1_.refs_3_) | copy-start | bytes 3145732
  82.3 11.9 %copy-start.37 = (bf16[128]{0:T(256)(128)(2,1)S(1)}, bf16[128]{0:T(256)(128)(2,1)}, u32[]{:S(2)}) copy-start(bf16[128]{0:T(256)(128)(2,1)} %param.29) | copy-start | bytes 772
  82.3 12.0 %copy-start.34 = (f32[128]{0:T(128)S(1)}, f32[128]{0:T(128)}, u32[]{:S(2)}) copy-start(f32[128]{0:T(128)} %param.28) | copy-start | bytes 1540
  82.4 12.1 %copy-start.24 = (bf16[64,128]{1,0:T(8,128)(2,1)S(1)}, bf16[64,128]{1,0:T(8,128)(2,1)}, u32[]{:S(2)}) copy-start(bf16[64,128]{1,0:T(8,128)(2,1)} %refs_8_.4) | copy-start | bytes 49156
  82.4 17.0 %copy-start.6 = (f32[64,64]{1,0:T(8,128)S(1)}, f32[64,64]{1,0:T(8,128)}, u32[]{:S(2)}) copy-start(f32[64,64]{1,0:T(8,128)} %constant.59.clone.refs_11_.refs_7_.xz_ref.xa_ref) | copy-start | bytes 49156
  82.4 17.0 %copy-start.7 = (bf16[8,16,256]{2,1,0:T(8,128)(2,1)S(1)}, bf16[8,16,256]{2,1,0:T(8,128)(2,1)}, u32[]{:S(2)}) copy-start(bf16[8,16,256]{2,1,0:T(8,128)(2,1)} %constant.57.clone.refs_10_.refs_6_) | copy-start | bytes 196612
  89.7 9.7 %all-to-all-start.4 = ((bf16[8,64,128]{2,1,0:T(8,128)(2,1)}), bf16[8,64,128]{2,1,0:T(8,128)(2,1)S(1)}, u32[]{:S(2)}, u32[]{:S(2)}) async-start(bf16[8,64,128]{2,1,0:T(8,128)(2,1)} %get-tuple-element.49), calls=%async_computation.4 | async-start | bytes 262144 | tf_op jit(solution)/shard_map/all_to_all | solution.py:748
  100.6 15.6 %copy-start.31 = (bf16[4,64,64]{2,1,0:T(8,128)(2,1)S(1)}, bf16[4,64,64]{2,1,0:T(8,128)(2,1)}, u32[]{:S(2)}) copy-start(bf16[4,64,64]{2,1,0:T(8,128)(2,1)} %copy-done.30) | copy-start | bytes 98308
  100.6 20.7 %copy-start.14 = (bf16[16,128,256]{2,1,0:T(8,128)(2,1)S(1)}, bf16[16,128,256]{2,1,0:T(8,128)(2,1)}, u32[]{:S(2)}) copy-start(bf16[16,128,256]{2,1,0:T(8,128)(2,1)} %copy-done.13) | copy-start | bytes 3145732
  100.6 20.7 %copy-start.20 = (bf16[32,256]{1,0:T(8,128)(2,1)S(1)}, bf16[32,256]{1,0:T(8,128)(2,1)}, u32[]{:S(2)}) copy-start(bf16[32,256]{1,0:T(8,128)(2,1)} %constant.55.clone.refs_5_) | copy-start | bytes 49156
  111.7 9.7 %all-to-all-start.5 = ((bf16[8,64,128]{2,1,0:T(8,128)(2,1)}), bf16[8,64,128]{2,1,0:T(8,128)(2,1)S(1)}, u32[]{:S(2)}, u32[]{:S(2)}) async-start(bf16[8,64,128]{2,1,0:T(8,128)(2,1)} %get-tuple-element.51), calls=%async_computation.5 | async-start | bytes 262144 | tf_op jit(solution)/shard_map/all_to_all | solution.py:748
  122.6 14.8 %copy-start.12 = (bf16[16,128,256]{2,1,0:T(8,128)(2,1)S(1)}, bf16[16,128,256]{2,1,0:T(8,128)(2,1)}, u32[]{:S(2)}) copy-start(bf16[16,128,256]{2,1,0:T(8,128)(2,1)} %copy-done.11) | copy-start | bytes 3145732
  137.4 14.8 %copy-start.10 = (bf16[16,128,256]{2,1,0:T(8,128)(2,1)S(1)}, bf16[16,128,256]{2,1,0:T(8,128)(2,1)}, u32[]{:S(2)}) copy-start(bf16[16,128,256]{2,1,0:T(8,128)(2,1)} %copy-done.9) | copy-start | bytes 3145732
  152.1 5.5 %copy-start.26 = (f32[128,128]{1,0:T(8,128)S(1)}, f32[128,128]{1,0:T(8,128)}, u32[]{:S(2)}) copy-start(f32[128,128]{1,0:T(8,128)} %copy-done.25) | copy-start | bytes 196612
  157.8 14.1 %collective-permute-start.5 = (f32[576,128]{1,0:T(8,128)S(1)}, f32[576,128]{1,0:T(8,128)S(1)}, u32[]{:S(2)}, u32[]{:S(2)}) collective-permute-start(f32[576,128]{1,0:T(8,128)S(1)} %get-tuple-element.69), channel_id=1, source_target_pairs={{0,4},{4,0},{8,12},{12,8},{1,5},{5,1},{9,13},{13,9},{2,6},{6,2},{1... | collective-permute-start | bytes 884744 | tf_op jit(solution)/shard_map/ppermute | solution.py:858
  (16 other events, 25.6 us)

commit v5 on v4

--- a/solution.py
+++ b/solution.py
@@ -802,16 +802,13 @@
         first_modes_kernel, (y0, lx, xi), (own, neighbour), [sent_first],
         [pltpu.VMEM(own.shape, bf16)] + mode_scratch[1:],
     )
-    across_even = lax.ppermute(
-        lax.optimization_barrier((away, mine))[0], "segment", [(2, 0)]
-    )
+    across_even = lax.ppermute(away, "segment", [(2, 0)])
     for layer in range(1, segments):
         recv = to_all(mine)
         table = inv_table
         if layer == 1:
-            across_odd_on = lax.ppermute(
-                lax.optimization_barrier((across_odd, recv))[0], "segment", [(1, 0), (3, 2)]
-            )
+            ready = lax.optimization_barrier((across_odd, recv, point_fwd, bias_cols))[0]
+            across_odd_on = lax.ppermute(ready, "segment", [(1, 0), (3, 2)])
             table = jnp.asarray(y_inverse.reshape(2 * mode_count, cols), bf16)
         act, slope, y, mine = call(
             partial(forward_kernel, layer=layer),

time: 181 us -> 181 us (level)
  transfers between devices with their start and end apart: 10 -> 10, of which waited for: 5 -> 6; matrix products, arithmetic and copies ran while one was open for 2% -> 2% of each run, Pallas kernels for 6% -> 6%
where the time goes in v5:
time: 181 us; the launch traced here: 178 us
  Pallas kernels  56.2 us (31%)
  starting transfers between devices  41.4 us (23%)
  blocking collectives  35.6 us (20%)
  waiting for transfers between devices  27.4 us (15%)
  local copies, waits for them, and re-layouts  15.5 us (9%)
    pallas_call x8, Pallas kernels, call(): pl.pallas_call(placed(kernel), in_specs=[near] * len(args) + [pl.BlockSpe...  46.3 us
    all_to_all x4, blocking collectives, to_all(): lax.all_to_all(block, both, 0, 0, tiled=True, axis_index_groups=device_li...  35.6 us
    all_to_all x3, waiting for transfers between devices, to_all(): lax.all_to_all(block, both, 0, 0, tiled=True, axis_index_groups=device_li...  18 us
    all_to_all x3, starting transfers between devices, to_all(): lax.all_to_all(block, both, 0, 0, tiled=True, axis_index_groups=device_li...  14.8 us
    ppermute x1, starting transfers between devices, replicated(): theirs = lax.ppermute(theirs, 'segment', [(0, 1), (1, 0), (2, 3), (3, 2)])  12.9 us
    unnamed x77, local copies, waits for them, and re-layouts  11.9 us
    all_to_all x1, waiting for transfers between devices, replicated(): lax.all_to_all(chunk.reshape((segments * space,) + chunk.shape[3:]), both...  7.7 us
    all_to_all x1, starting transfers between devices, replicated(): lax.all_to_all(chunk.reshape((segments * space,) + chunk.shape[3:]), both...  6.35 us
  transfers between devices with their start and end apart: 10, of which 6 were waited for; matrix products, arithmetic and copies ran while one was open for 2% of the time, Pallas kernels for 6%

profile of v5, /device:TPU:3, one launch (start us, length us, event | category | flops | bytes accessed | tf_op | source)
XLA Modules:
  0.0 177.6 jit_solution(7179979845626467370)
XLA Ops:
  0.6 3.3 %pack.1.refs_3_.refs_8_.refs_13_.refs_9_ = bf16[4,16,128,128]{3,2,1,0:T(8,128)(2,1)S(1)} custom-call(bf16[4,2,16,128,64]{4,3,2,1,0:T(8,128)(2,1)} %bitcast.21), custom_call_target="tpu_custom_call" | custom-call | tf_op jit(solution)/shard_map/pack/pallas_call | solution.py:687
  4.8 1.1 constant_dynamic-slice_fusion
  5.9 1.9 %collective-permute-start.1 = (bf16[2,16,128,128]{3,2,1,0:T(8,128)(2,1)}, bf16[2,16,128,128]{3,2,1,0:T(8,128)(2,1)}, u32[]{:S(2)}, u32[]{:S(2)}) collective-permute-start(bf16[2,16,128,128]{3,2,1,0:T(8,128)(2,1)} %constant_dynamic-slice_fusion), channel_id=1, source_target_pairs={{4,12},{12,4},{5,13},{13,5},{6,14},{14,6},{7,15},{15,7},{20,28},{2... | collective-permute-start | bytes 3145736 | tf_op jit(solution)/shard_map/ppermute | solution.py:691
  9.4 6.3 %all-to-all-start = ((bf16[16,24,256]{2,1,0:T(8,128)(2,1)}), bf16[16,24,256]{2,1,0:T(8,128)(2,1)S(1)}, u32[]{:S(2)}, u32[]{:S(2)}) async-start(bf16[16,24,256]{2,1,0:T(8,128)(2,1)} %bitcast.2), calls=%async_computation | async-start | bytes 393216 | tf_op jit(solution)/shard_map/all_to_all | solution.py:693
  16.2 7.7 %all-to-all-done.refs_0_.refs_2_ = bf16[16,24,256]{2,1,0:T(8,128)(2,1)S(1)} async-done(((bf16[16,24,256]{2,1,0:T(8,128)(2,1)}), bf16[16,24,256]{2,1,0:T(8,128)(2,1)S(1)}, u32[]{:S(2)}, u32[]{:S(2)}) %all-to-all-start) | async-done | bytes 196640 | tf_op jit(solution)/shard_map/all_to_all | solution.py:693
  25.7 4.2 %shard_map.203 = bf16[8,128,128]{2,1,0:T(8,128)(2,1)} custom-call(f32[256,128]{1,0:T(8,128)S(1)} %get-tuple-element.36.refs_0_, f32[64,128]{1,0:T(8,128)S(1)} %copy-done.19, f32[64,64]{1,0:T(8,128)S(1)} %copy-done.5, bf16[4,16,128,128]{3,2,1,0:T(8,128)(2,1)S(1)} %pack.1.refs_3_.refs_8_.refs_13_.refs_9_, ...), custom_call_target="tpu_custom_call" | custom-call | tf_op jit(solution)/shard_map/pallas_call | solution.py:764
  29.8 5.8 %all-to-all-start.1 = ((bf16[8,128,128]{2,1,0:T(8,128)(2,1)}), bf16[8,128,128]{2,1,0:T(8,128)(2,1)S(1)}, u32[]{:S(2)}, u32[]{:S(2)}) async-start(bf16[8,128,128]{2,1,0:T(8,128)(2,1)} %shard_map.203), calls=%async_computation.1 | async-start | bytes 524288 | tf_op jit(solution)/shard_map/all_to_all | solution.py:748
  36.1 8.1 %all-to-all-done.1.refs_0_ = bf16[8,128,128]{2,1,0:T(8,128)(2,1)S(1)} async-done(((bf16[8,128,128]{2,1,0:T(8,128)(2,1)}), bf16[8,128,128]{2,1,0:T(8,128)(2,1)S(1)}, u32[]{:S(2)}, u32[]{:S(2)}) %all-to-all-start.1) | async-done | bytes 262176 | tf_op jit(solution)/shard_map/all_to_all | solution.py:748
  44.2 2.3 %collective-permute-start.2 = (bf16[2,16,128,128]{3,2,1,0:T(8,128)(2,1)}, bf16[2,16,128,128]{3,2,1,0:T(8,128)(2,1)S(1)}, u32[]{:S(2)}, u32[]{:S(2)}) collective-permute-start(bf16[2,16,128,128]{3,2,1,0:T(8,128)(2,1)} %collective-permute-done.1.refs_10_.refs_15_.refs_11_), channel_id=1, source_target_pairs={{4,0},{12,8},{5,1},{13,9},{6,2},{14,10},{7,3},{15,11},{20,16},{28,... | collective-permute-start | bytes 3145736 | tf_op jit(solution)/shard_map/ppermute | solution.py:811
  46.5 1.6 collective-permute-start.3
  48.9 1.0 copy-done.28
  50.0 5.9 %shard_map.204 = (bf16[16,128,256]{2,1,0:T(8,128)(2,1)S(1)}, bf16[16,128,256]{2,1,0:T(8,128)(2,1)S(1)}, f32[256,128]{1,0:T(8,128)S(1)}, bf16[8,64,128]{2,1,0:T(8,128)(2,1)S(1)}) custom-call(bf16[8,128,128]{2,1,0:T(8,128)(2,1)S(1)} %all-to-all-done.1.refs_0_, bf16[16,128,256]{2,1,0:T(8,128)(2,1)} %copy-done.4, bf16[4,128,128]{2,1,0:T(8,128)(2,1)S(1)} %copy.46.refs_2_.refs_3_, ...), custom_call_target="tpu_custom_call" | custom-call | tf_op jit(solution)/shard_map/pallas_call | solution.py:764
  57.6 9.3 %all_to_all.40.refs_0_ = bf16[8,64,128]{2,1,0:T(8,128)(2,1)S(1)} all-to-all(bf16[8,64,128]{2,1,0:T(8,128)(2,1)S(1)} %get-tuple-element.40), channel_id=1, replica_groups={{0,1,2,3,8,9,10,11},{4,5,6,7,12,13,14,15},{16,17,18,19,24,25,26,27},{20..., dimensions={0} | all-to-all | bytes 262144 | tf_op jit(solution)/shard_map/all_to_all | solution.py:748
  67.9 4.7 %shard_map.205 = (bf16[16,128,256]{2,1,0:T(8,128)(2,1)S(1)}, bf16[16,128,256]{2,1,0:T(8,128)(2,1)S(1)}, f32[256,128]{1,0:T(8,128)S(1)}, bf16[8,64,128]{2,1,0:T(8,128)(2,1)S(1)}) custom-call(bf16[8,64,128]{2,1,0:T(8,128)(2,1)S(1)} %all_to_all.40.refs_0_, bf16[16,128,256]{2,1,0:T(8,128)(2,1)S(1)} %get-tuple-element.41.refs_1_.refs_3_, ...), custom_call_target="tpu_custom_call" | custom-call | tf_op jit(solution)/shard_map/pallas_call | solution.py:764
  73.6 8.7 %all_to_all.41.refs_0_ = bf16[8,64,128]{2,1,0:T(8,128)(2,1)S(1)} all-to-all(bf16[8,64,128]{2,1,0:T(8,128)(2,1)S(1)} %get-tuple-element.44), channel_id=1, replica_groups={{0,1,2,3,8,9,10,11},{4,5,6,7,12,13,14,15},{16,17,18,19,24,25,26,27},{20..., dimensions={0} | all-to-all | bytes 262144 | tf_op jit(solution)/shard_map/all_to_all | solution.py:748
  82.4 5.3 %shard_map.206 = (bf16[16,128,256]{2,1,0:T(8,128)(2,1)S(1)}, bf16[16,128,256]{2,1,0:T(8,128)(2,1)S(1)}, f32[256,128]{1,0:T(8,128)S(1)}, bf16[8,64,128]{2,1,0:T(8,128)(2,1)}) custom-call(bf16[8,64,128]{2,1,0:T(8,128)(2,1)S(1)} %all_to_all.41.refs_0_, bf16[16,128,256]{2,1,0:T(8,128)(2,1)S(1)} %get-tuple-element.45.refs_1_.refs_3_, ...), custom_call_target="tpu_custom_call" | custom-call | tf_op jit(solution)/shard_map/pallas_call | solution.py:764
  87.7 1.0 copy-done.13
  89.7 4.5 %all-to-all-start.4 = ((bf16[8,64,128]{2,1,0:T(8,128)(2,1)}), bf16[8,64,128]{2,1,0:T(8,128)(2,1)S(1)}, u32[]{:S(2)}, u32[]{:S(2)}) async-start(bf16[8,64,128]{2,1,0:T(8,128)(2,1)} %get-tuple-element.47), calls=%async_computation.4 | async-start | bytes 262144 | tf_op jit(solution)/shard_map/all_to_all | solution.py:748
  94.6 4.8 %all-to-all-done.4.refs_0_ = bf16[8,64,128]{2,1,0:T(8,128)(2,1)S(1)} async-done(((bf16[8,64,128]{2,1,0:T(8,128)(2,1)}), bf16[8,64,128]{2,1,0:T(8,128)(2,1)S(1)}, u32[]{:S(2)}, u32[]{:S(2)}) %all-to-all-start.4) | async-done | bytes 131104 | tf_op jit(solution)/shard_map/all_to_all | solution.py:748
  99.4 1.2 copy-done.18
  100.6 8.8 %shard_map.207 = (bf16[16,128,256]{2,1,0:T(8,128)(2,1)S(1)}, f32[256,128]{1,0:T(8,128)S(1)}, f32[128,128]{1,0:T(8,128)S(1)}, bf16[8,64,128]{2,1,0:T(8,128)(2,1)}) custom-call(bf16[8,64,128]{2,1,0:T(8,128)(2,1)S(1)} %all-to-all-done.4.refs_0_, bf16[16,128,256]{2,1,0:T(8,128)(2,1)S(1)} %copy-done.18, bf16[16,24,256]{2,1,0:T(8,128)(2,1)S(1)} %all-to-all-done.refs_0_.refs_2_, ...), custom_call_target="tpu_custom_call" | custom-call | tf_op jit(solution)/shard_map/pallas_call | solution.py:764
  111.7 4.5 %all-to-all-start.5 = ((bf16[8,64,128]{2,1,0:T(8,128)(2,1)}), bf16[8,64,128]{2,1,0:T(8,128)(2,1)S(1)}, u32[]{:S(2)}, u32[]{:S(2)}) async-start(bf16[8,64,128]{2,1,0:T(8,128)(2,1)} %get-tuple-element.49), calls=%async_computation.5 | async-start | bytes 262144 | tf_op jit(solution)/shard_map/all_to_all | solution.py:748
  116.3 5.1 %all-to-all-done.5.refs_0_ = bf16[8,64,128]{2,1,0:T(8,128)(2,1)S(1)} async-done(((bf16[8,64,128]{2,1,0:T(8,128)(2,1)}), bf16[8,64,128]{2,1,0:T(8,128)(2,1)S(1)}, u32[]{:S(2)}, u32[]{:S(2)}) %all-to-all-start.5) | async-done | bytes 131104 | tf_op jit(solution)/shard_map/all_to_all | solution.py:748
  121.4 1.2 copy-done.16
  122.6 6.0 %shard_map.208 = (bf16[16,128,256]{2,1,0:T(8,128)(2,1)S(1)}, f32[256,128]{1,0:T(8,128)S(1)}, f32[128,128]{1,0:T(8,128)S(1)}, bf16[8,64,128]{2,1,0:T(8,128)(2,1)S(1)}) custom-call(bf16[8,64,128]{2,1,0:T(8,128)(2,1)S(1)} %all-to-all-done.5.refs_0_, bf16[16,128,256]{2,1,0:T(8,128)(2,1)S(1)} %copy-done.16, bf16[16,128,256]{2,1,0:T(8,128)(2,1)S(1)} %copy-done.14, ...), custom_call_target="tpu_custom_call" | custom-call | tf_op jit(solution)/shard_map/pallas_call | solution.py:764
  128.6 8.8 %all_to_all.42.refs_0_ = bf16[8,64,128]{2,1,0:T(8,128)(2,1)S(1)} all-to-all(bf16[8,64,128]{2,1,0:T(8,128)(2,1)S(1)} %get-tuple-element.52), channel_id=1, replica_groups={{0,1,2,3,8,9,10,11},{4,5,6,7,12,13,14,15},{16,17,18,19,24,25,26,27},{20..., dimensions={0} | all-to-all | bytes 262144 | tf_op jit(solution)/shard_map/all_to_all | solution.py:748
  137.4 6.0 %shard_map.209 = (bf16[16,128,256]{2,1,0:T(8,128)(2,1)S(1)}, f32[256,128]{1,0:T(8,128)S(1)}, f32[128,128]{1,0:T(8,128)S(1)}, bf16[8,64,128]{2,1,0:T(8,128)(2,1)S(1)}) custom-call(bf16[8,64,128]{2,1,0:T(8,128)(2,1)S(1)} %all_to_all.42.refs_0_, bf16[16,128,256]{2,1,0:T(8,128)(2,1)S(1)} %get-tuple-element.53.refs_1_, bf16[16,128,256]{2,1,0:T(8,128)(2,1)S(1)} %copy-done.12, ...), custom_call_target="tpu_custom_call" | custom-call | tf_op jit(solution)/shard_map/pallas_call | solution.py:764
  143.3 8.8 %all_to_all.43.refs_0_ = bf16[8,64,128]{2,1,0:T(8,128)(2,1)S(1)} all-to-all(bf16[8,64,128]{2,1,0:T(8,128)(2,1)S(1)} %get-tuple-element.55), channel_id=1, replica_groups={{0,1,2,3,8,9,10,11},{4,5,6,7,12,13,14,15},{16,17,18,19,24,25,26,27},{20..., dimensions={0} | all-to-all | bytes 262144 | tf_op jit(solution)/shard_map/all_to_all | solution.py:748
  152.1 5.5 %shard_map.210 = (bf16[16,128,256]{2,1,0:T(8,128)(2,1)}, f32[256,128]{1,0:T(8,128)S(1)}, f32[128,128]{1,0:T(8,128)S(1)}, bf16[8,64,128]{2,1,0:T(8,128)(2,1)}) custom-call(bf16[8,64,128]{2,1,0:T(8,128)(2,1)S(1)} %all_to_all.43.refs_0_, bf16[16,128,256]{2,1,0:T(8,128)(2,1)S(1)} %get-tuple-element.56.refs_1_, bf16[16,128,256]{2,1,0:T(8,128)(2,1)S(1)} %copy-done.10, ...), custom_call_target="tpu_custom_call" | custom-call | tf_op jit(solution)/shard_map/pallas_call | solution.py:764
  157.8 12.9 %collective-permute-start.5 = (f32[576,128]{1,0:T(8,128)S(1)}, f32[576,128]{1,0:T(8,128)S(1)}, u32[]{:S(2)}, u32[]{:S(2)}) collective-permute-start(f32[576,128]{1,0:T(8,128)S(1)} %get-tuple-element.67), channel_id=1, source_target_pairs={{0,4},{4,0},{8,12},{12,8},{1,5},{5,1},{9,13},{13,9},{2,6},{6,2},{1... | collective-permute-start | bytes 884744 | tf_op jit(solution)/shard_map/ppermute | solution.py:855
  170.8 1.2 collective-permute-done.5.theirs_ref
  172.0 5.6 %grads.1 = (f32[4,32,2,64,64]{4,3,2,1,0:T(8,128)}, f32[64,64]{1,0:T(8,128)}) custom-call(f32[576,128]{1,0:T(8,128)S(1)} %get-tuple-element.66.mine_ref, f32[576,128]{1,0:T(8,128)S(1)} %collective-permute-done.5.theirs_ref, f32[64,64]{1,0:T(8,128)S(1)} %copy-done.6, f32[64,64]{1,0:T(8,128)S(1)} %copy-done.6), custom_call_target="tpu_custom_call" | custom-call | tf_op jit(solution)/shard_map/grads/pallas_call | solution.py:857
  (109 shorter events, 13.3 us)
Async XLA Ops:
  0.6 7.4 %copy-start = (bf16[2,8,8,256]{3,2,1,0:T(8,128)(2,1)S(1)}, bf16[2,8,8,256]{3,2,1,0:T(8,128)(2,1)}, u32[]{:S(2)}) copy-start(bf16[2,8,8,256]{3,2,1,0:T(8,128)(2,1)} %param.20) | copy-start | bytes 196612
  4.0 25.9 %copy-start.1 = (bf16[4,16,128,128]{3,2,1,0:T(8,128)(2,1)}, bf16[4,16,128,128]{3,2,1,0:T(8,128)(2,1)S(1)}, u32[]{:S(2)}) copy-start(bf16[4,16,128,128]{3,2,1,0:T(8,128)(2,1)S(1)} %pack.1.refs_3_.refs_8_.refs_13_.refs_9_) | copy-start | bytes 6291460
  4.0 11.8 %copy-start.36 = (f32[64]{0:T(128)S(1)}, f32[64]{0:T(128)}, u32[]{:S(2)}) copy-start(f32[64]{0:T(128)} %param.23) | copy-start | bytes 772
  4.0 12.0 %copy-start.33 = (bf16[8,64]{1,0:T(8,128)(2,1)S(1)}, bf16[8,64]{1,0:T(8,128)(2,1)}, u32[]{:S(2)}) copy-start(bf16[8,64]{1,0:T(8,128)(2,1)} %param.22) | copy-start | bytes 3076
  4.0 19.9 %copy-start.8 = (bf16[8,16,256]{2,1,0:T(8,128)(2,1)S(1)}, bf16[8,16,256]{2,1,0:T(8,128)(2,1)}, u32[]{:S(2)}) copy-start(bf16[8,16,256]{2,1,0:T(8,128)(2,1)} %constant.56.clone.refs_3_.refs_5_) | copy-start | bytes 196612
  4.0 21.6 %copy-start.5 = (f32[64,64]{1,0:T(8,128)S(1)}, f32[64,64]{1,0:T(8,128)}, u32[]{:S(2)}) copy-start(f32[64,64]{1,0:T(8,128)} %constant.60.clone.refs_2_.refs_7_.refs_12_.refs_8_) | copy-start | bytes 49156
  4.0 21.6 %copy-start.19 = (f32[64,128]{1,0:T(8,128)S(1)}, f32[64,128]{1,0:T(8,128)}, u32[]{:S(2)}) copy-start(f32[64,128]{1,0:T(8,128)} %constant.58.clone.refs_1_.refs_6_) | copy-start | bytes 98308
  4.1 21.6 %collective-permute-start = (bf16[4,16,128,128]{3,2,1,0:T(8,128)(2,1)S(1)}, bf16[4,16,128,128]{3,2,1,0:T(8,128)(2,1)}, u32[]{:S(2)}, u32[]{:S(2)}) collective-permute-start(bf16[4,16,128,128]{3,2,1,0:T(8,128)(2,1)S(1)} %pack.1.refs_3_.refs_8_.refs_13_.refs_9_), channel_id=1, source_target_pairs={{0,4},{4,0},{8,12},{12,8},{1,5},{5,1},{9,13},{13,9},{2,6},{6,2},{1... | collective-permute-start | bytes 6291464 | tf_op jit(solution)/shard_map/ppermute | solution.py:689
  5.9 30.2 %collective-permute-start.1 = (bf16[2,16,128,128]{3,2,1,0:T(8,128)(2,1)}, bf16[2,16,128,128]{3,2,1,0:T(8,128)(2,1)}, u32[]{:S(2)}, u32[]{:S(2)}) collective-permute-start(bf16[2,16,128,128]{3,2,1,0:T(8,128)(2,1)} %constant_dynamic-slice_fusion), channel_id=1, source_target_pairs={{4,12},{12,4},{5,13},{13,5},{6,14},{14,6},{7,15},{15,7},{20,28},{2... | collective-permute-start | bytes 3145736 | tf_op jit(solution)/shard_map/ppermute | solution.py:691
  9.4 14.5 %all-to-all-start = ((bf16[16,24,256]{2,1,0:T(8,128)(2,1)}), bf16[16,24,256]{2,1,0:T(8,128)(2,1)S(1)}, u32[]{:S(2)}, u32[]{:S(2)}) async-start(bf16[16,24,256]{2,1,0:T(8,128)(2,1)} %bitcast.2), calls=%async_computation | async-start | bytes 393216 | tf_op jit(solution)/shard_map/all_to_all | solution.py:693
  25.7 24.3 %copy-start.27 = (bf16[32,256]{1,0:T(8,128)(2,1)S(1)}, bf16[32,256]{1,0:T(8,128)(2,1)}, u32[]{:S(2)}) copy-start(bf16[32,256]{1,0:T(8,128)(2,1)} %constant.61.clone.refs_4_) | copy-start | bytes 49156
  29.8 14.3 %all-to-all-start.1 = ((bf16[8,128,128]{2,1,0:T(8,128)(2,1)}), bf16[8,128,128]{2,1,0:T(8,128)(2,1)S(1)}, u32[]{:S(2)}, u32[]{:S(2)}) async-start(bf16[8,128,128]{2,1,0:T(8,128)(2,1)} %shard_map.203), calls=%async_computation.1 | async-start | bytes 524288 | tf_op jit(solution)/shard_map/all_to_all | solution.py:748
  35.8 13.1 %copy-start.30 = (bf16[4,64,64]{2,1,0:T(8,128)(2,1)}, bf16[4,64,64]{2,1,0:T(8,128)(2,1)S(1)}, u32[]{:S(2)}) copy-start(bf16[4,64,64]{2,1,0:T(8,128)(2,1)S(1)} %reshape.67) | copy-start | bytes 98308
  44.2 4.8 %collective-permute-start.2 = (bf16[2,16,128,128]{3,2,1,0:T(8,128)(2,1)}, bf16[2,16,128,128]{3,2,1,0:T(8,128)(2,1)S(1)}, u32[]{:S(2)}, u32[]{:S(2)}) collective-permute-start(bf16[2,16,128,128]{3,2,1,0:T(8,128)(2,1)} %collective-permute-done.1.refs_10_.refs_15_.refs_11_), channel_id=1, source_target_pairs={{4,0},{12,8},{5,1},{13,9},{6,2},{14,10},{7,3},{15,11},{20,16},{28,... | collective-permute-start | bytes 3145736 | tf_op jit(solution)/shard_map/ppermute | solution.py:811
  46.5 10.4 %collective-permute-start.3 = (bf16[2,16,128,128]{3,2,1,0:T(8,128)(2,1)}, bf16[2,16,128,128]{3,2,1,0:T(8,128)(2,1)}, u32[]{:S(2)}, u32[]{:S(2)}) collective-permute-start(bf16[2,16,128,128]{3,2,1,0:T(8,128)(2,1)} %constant_dynamic-slice_fusion), channel_id=1, source_target_pairs={{8,0},{9,1},{10,2},{11,3},{24,16},{25,17},{26,18},{27,19}} | collective-permute-start | bytes 3145736 | tf_op jit(solution)/shard_map/ppermute | solution.py:805
  50.0 18.0 %copy-start.21 = (bf16[32,256]{1,0:T(8,128)(2,1)S(1)}, bf16[32,256]{1,0:T(8,128)(2,1)}, u32[]{:S(2)}) copy-start(bf16[32,256]{1,0:T(8,128)(2,1)} %constant.54.clone.refs_4_.refs_5_) | copy-start | bytes 49156
  56.9 15.7 %copy-start.2 = (bf16[16,128,256]{2,1,0:T(8,128)(2,1)}, bf16[16,128,256]{2,1,0:T(8,128)(2,1)S(1)}, u32[]{:S(2)}) copy-start(bf16[16,128,256]{2,1,0:T(8,128)(2,1)S(1)} %get-tuple-element.41.refs_1_.refs_3_) | copy-start | bytes 3145732
  56.9 10.0 %collective-permute-start.4 = (bf16[2,16,128,128]{3,2,1,0:T(8,128)(2,1)}, bf16[2,16,128,128]{3,2,1,0:T(8,128)(2,1)S(1)}, u32[]{:S(2)}, u32[]{:S(2)}) collective-permute-start(bf16[2,16,128,128]{3,2,1,0:T(8,128)(2,1)} %collective-permute-done.3.refs_10_.refs_11_), channel_id=1, source_target_pairs={{0,4},{1,5},{2,6},{3,7},{16,20},{17,21},{18,22},{19,23}} | collective-permute-start | bytes 3145736 | tf_op jit(solution)/shard_map/ppermute | solution.py:822
  73.6 14.1 %copy-start.3 = (bf16[16,128,256]{2,1,0:T(8,128)(2,1)}, bf16[16,128,256]{2,1,0:T(8,128)(2,1)S(1)}, u32[]{:S(2)}) copy-start(bf16[16,128,256]{2,1,0:T(8,128)(2,1)S(1)} %get-tuple-element.45.refs_1_.refs_3_) | copy-start | bytes 3145732
  82.3 11.9 %copy-start.37 = (bf16[128]{0:T(256)(128)(2,1)S(1)}, bf16[128]{0:T(256)(128)(2,1)}, u32[]{:S(2)}) copy-start(bf16[128]{0:T(256)(128)(2,1)} %param.29) | copy-start | bytes 772
  82.3 12.0 %copy-start.34 = (f32[128]{0:T(128)S(1)}, f32[128]{0:T(128)}, u32[]{:S(2)}) copy-start(f32[128]{0:T(128)} %param.28) | copy-start | bytes 1540
  82.4 12.1 %copy-start.24 = (bf16[64,128]{1,0:T(8,128)(2,1)S(1)}, bf16[64,128]{1,0:T(8,128)(2,1)}, u32[]{:S(2)}) copy-start(bf16[64,128]{1,0:T(8,128)(2,1)} %refs_8_.4) | copy-start | bytes 49156
  82.4 17.0 %copy-start.6 = (f32[64,64]{1,0:T(8,128)S(1)}, f32[64,64]{1,0:T(8,128)}, u32[]{:S(2)}) copy-start(f32[64,64]{1,0:T(8,128)} %constant.59.clone.refs_11_.refs_7_.xz_ref.xa_ref) | copy-start | bytes 49156
  82.4 17.0 %copy-start.7 = (bf16[8,16,256]{2,1,0:T(8,128)(2,1)S(1)}, bf16[8,16,256]{2,1,0:T(8,128)(2,1)}, u32[]{:S(2)}) copy-start(bf16[8,16,256]{2,1,0:T(8,128)(2,1)} %constant.57.clone.refs_10_.refs_6_) | copy-start | bytes 196612
  89.7 9.7 %all-to-all-start.4 = ((bf16[8,64,128]{2,1,0:T(8,128)(2,1)}), bf16[8,64,128]{2,1,0:T(8,128)(2,1)S(1)}, u32[]{:S(2)}, u32[]{:S(2)}) async-start(bf16[8,64,128]{2,1,0:T(8,128)(2,1)} %get-tuple-element.47), calls=%async_computation.4 | async-start | bytes 262144 | tf_op jit(solution)/shard_map/all_to_all | solution.py:748
  100.6 15.6 %copy-start.31 = (bf16[4,64,64]{2,1,0:T(8,128)(2,1)S(1)}, bf16[4,64,64]{2,1,0:T(8,128)(2,1)}, u32[]{:S(2)}) copy-start(bf16[4,64,64]{2,1,0:T(8,128)(2,1)} %copy-done.30) | copy-start | bytes 98308
  100.6 20.7 %copy-start.14 = (bf16[16,128,256]{2,1,0:T(8,128)(2,1)S(1)}, bf16[16,128,256]{2,1,0:T(8,128)(2,1)}, u32[]{:S(2)}) copy-start(bf16[16,128,256]{2,1,0:T(8,128)(2,1)} %copy-done.13) | copy-start | bytes 3145732
  100.6 20.7 %copy-start.20 = (bf16[32,256]{1,0:T(8,128)(2,1)S(1)}, bf16[32,256]{1,0:T(8,128)(2,1)}, u32[]{:S(2)}) copy-start(bf16[32,256]{1,0:T(8,128)(2,1)} %constant.55.clone.refs_5_) | copy-start | bytes 49156
  111.7 9.7 %all-to-all-start.5 = ((bf16[8,64,128]{2,1,0:T(8,128)(2,1)}), bf16[8,64,128]{2,1,0:T(8,128)(2,1)S(1)}, u32[]{:S(2)}, u32[]{:S(2)}) async-start(bf16[8,64,128]{2,1,0:T(8,128)(2,1)} %get-tuple-element.49), calls=%async_computation.5 | async-start | bytes 262144 | tf_op jit(solution)/shard_map/all_to_all | solution.py:748
  122.6 14.8 %copy-start.12 = (bf16[16,128,256]{2,1,0:T(8,128)(2,1)S(1)}, bf16[16,128,256]{2,1,0:T(8,128)(2,1)}, u32[]{:S(2)}) copy-start(bf16[16,128,256]{2,1,0:T(8,128)(2,1)} %copy-done.11) | copy-start | bytes 3145732
  137.4 14.8 %copy-start.10 = (bf16[16,128,256]{2,1,0:T(8,128)(2,1)S(1)}, bf16[16,128,256]{2,1,0:T(8,128)(2,1)}, u32[]{:S(2)}) copy-start(bf16[16,128,256]{2,1,0:T(8,128)(2,1)} %copy-done.9) | copy-start | bytes 3145732
  157.8 14.1 %collective-permute-start.5 = (f32[576,128]{1,0:T(8,128)S(1)}, f32[576,128]{1,0:T(8,128)S(1)}, u32[]{:S(2)}, u32[]{:S(2)}) collective-permute-start(f32[576,128]{1,0:T(8,128)S(1)} %get-tuple-element.67), channel_id=1, source_target_pairs={{0,4},{4,0},{8,12},{12,8},{1,5},{5,1},{9,13},{13,9},{2,6},{6,2},{1... | collective-permute-start | bytes 884744 | tf_op jit(solution)/shard_map/ppermute | solution.py:855
  (16 other events, 30.5 us)
